TPU v7x, 32 devices: a whole 2x2x4 slice. The times are simulated.
32 devices in a mesh: dp: 16 (over z, y, x), tensor: 2 (over core).
Axes of the slice: x: 2, y: 2, z: 4, core: 2. Of those that a mesh axis runs over, the one named last changes fastest.
Arguments:
- media: bfloat16 [64, 576, 1024], P('dp'), may hold values from -6 to 6
- buckets: int32 [64], P('dp'), may hold values 0 or 1
- latents: bfloat16 [64, 64, 1024], P('dp'), may hold values from -6 to 6
- cotangent: bfloat16 [64, 64, 1024], P('dp'), may hold values from -6 to 6
- query_weight: bfloat16 [1024, 512], P(None, 'tensor'), may hold values from -0.375 to 0.375
- key_weight: bfloat16 [1024, 512], P(None, 'tensor'), may hold values from -0.1875 to 0.1875
- value_weight: bfloat16 [1024, 512], P(None, 'tensor'), may hold values from -0.1875 to 0.1875
- output_weight: bfloat16 [512, 1024], P('tensor'), may hold values from -2 to 2
- up_weight: bfloat16 [1024, 4096], P(None, 'tensor'), may hold values from -0.1875 to 0.1875
- down_weight: bfloat16 [4096, 1024], P('tensor'), may hold values from -0.125 to 0.125
- media_gain: float32 [1024], replicated, may hold values from 0.1 to 1.9
- media_bias: float32 [1024], replicated, may hold values from -1.5 to 1.5
- latent_gain: float32 [1024], replicated, may hold values from 0.1 to 1.9
- latent_bias: float32 [1024], replicated, may hold values from -1.5 to 1.5
- feed_gain: float32 [1024], replicated, may hold values from 0.1 to 1.9
- feed_bias: float32 [1024], replicated, may hold values from -1.5 to 1.5
Outputs:
- latents_out: bfloat16 [64, 64, 1024], P('dp')
- grad_media: bfloat16 [64, 576, 1024], P('dp')
- grad_latents: bfloat16 [64, 64, 1024], P('dp')
- grad_query_weight: float32 [1024, 512], P('dp', 'tensor')
- grad_key_weight: float32 [1024, 512], P('dp', 'tensor')
- grad_value_weight: float32 [1024, 512], P('dp', 'tensor')
- grad_output_weight: float32 [512, 1024], P('tensor', 'dp')
- grad_up_weight: float32 [1024, 4096], P('dp', 'tensor')
- grad_down_weight: float32 [4096, 1024], P('tensor', 'dp')
- grad_media_gain: float32 [1024], P('dp')
- grad_media_bias: float32 [1024], P('dp')
- grad_latent_gain: float32 [1024], P('dp')
- grad_latent_bias: float32 [1024], P('dp')
- grad_feed_gain: float32 [1024], P('dp')
- grad_feed_bias: float32 [1024], P('dp')
Inputs may be any that keep to these rules, and one draw needn't show every extreme that they name: `buckets`: bucket 1 marks an image with 576 patches, 0 one with 256; patch slots past an image's count are padding.
All inputs are finite; a program needn't handle non-finite values. No bound on the sum of `buckets` on one device may be relied on, other than what follows from the above.
Results may differ from a plain program's by a relative error of at most 0.014.
The roundings to bfloat16 on the way count: a program that leaves them out, or rounds other values in their place, can miss the bound.
Values sent between devices are 32-bit elements; how exact they have to be, the bound alone decides.
No kernel may reach another device: no remote copies, remote signals or barrier semaphores. Data moves between devices by JAX's collectives and lax.ppermute only.
A program may use at most 192 MiB of HBM per device.

v0:
```python
import jax
import jax.numpy as jnp
from jax import lax
from jax.sharding import PartitionSpec as P

HEAD = 64
PATCH = 576
SHORT = 256


EPSILON = 1e-05


def layer_norm(values, gain, offset):
    center = values - jnp.mean(values, -1, keepdims=True)
    inverse = lax.rsqrt(jnp.mean(center * center, -1, keepdims=True) + EPSILON)
    normed = center * inverse
    return (normed * gain + offset, normed, inverse)


def norm_back(upstream, normed, inverse, gain):
    scaled = upstream * gain
    result = inverse * (
        scaled
        - jnp.mean(scaled, -1, keepdims=True)
        - normed * jnp.mean(scaled * normed, -1, keepdims=True)
    )
    return (result, jnp.sum(upstream * normed, axis=(0, 1)), jnp.sum(upstream, axis=(0, 1)))


def exact_gelu(values):
    return jax.nn.gelu(values, approximate=False)


def local(
    media,
    buckets,
    latents,
    cotangent,
    query_weight,
    key_weight,
    value_weight,
    output_weight,
    up_weight,
    down_weight,
    media_gain,
    media_bias,
    latent_gain,
    latent_bias,
    feed_gain,
    feed_bias,
):
    single = jnp.float32
    half = jnp.bfloat16
    images, patches = (media.shape[0], media.shape[1])
    latent_rows = latents.shape[1]
    keys_all = patches + latent_rows
    inner_here = query_weight.shape[1]
    heads_here = inner_here // HEAD
    factor = HEAD ** (-0.5)
    media_norm, media_hat, media_inv = layer_norm(media.astype(single), media_gain, media_bias)
    latent_in = latents.astype(single)
    latent_norm, latent_hat, latent_inv = layer_norm(latent_in, latent_gain, latent_bias)
    kv_input = jnp.concatenate([media_norm.astype(half), latent_norm.astype(half)], axis=1)
    query_input = kv_input[:, patches:]
    queries = jnp.einsum(
        "ird,de->ire", query_input, query_weight, preferred_element_type=single
    ).astype(half)
    keys = jnp.einsum("ikd,de->ike", kv_input, key_weight, preferred_element_type=single).astype(
        half
    )
    values = jnp.einsum(
        "ikd,de->ike", kv_input, value_weight, preferred_element_type=single
    ).astype(half)
    query_heads = queries.reshape(images, latent_rows, heads_here, HEAD)
    key_heads = keys.reshape(images, keys_all, heads_here, HEAD)
    value_heads = values.reshape(images, keys_all, heads_here, HEAD)
    counts = SHORT + (PATCH - SHORT) * buckets
    position = lax.broadcasted_iota(jnp.int32, (images, keys_all), 1)
    usable = (position < counts[:, None]) | (position >= patches)
    scores = (
        jnp.einsum("irhc,ikhc->ihrk", query_heads, key_heads, preferred_element_type=single)
        * factor
    )
    scores = jnp.where(usable[:, None, None, :], scores, -1e30)
    shifted = jnp.exp(scores - jnp.max(scores, -1, keepdims=True))
    probs = shifted / jnp.sum(shifted, -1, keepdims=True)
    probs_low = probs.astype(half)
    attended = jnp.einsum("ihrk,ikhc->irhc", probs_low, value_heads, preferred_element_type=single)
    attended = attended.reshape(images, latent_rows, inner_here).astype(half)
    branch = lax.psum(
        jnp.einsum("ire,ed->ird", attended, output_weight, preferred_element_type=single), "tensor"
    )
    middle = latent_in + branch
    feed_norm, feed_hat, feed_inv = layer_norm(middle, feed_gain, feed_bias)
    feed_low = feed_norm.astype(half)
    hidden_pre = jnp.einsum("ird,df->irf", feed_low, up_weight, preferred_element_type=single)
    hidden_low = exact_gelu(hidden_pre).astype(half)
    feed_out = lax.psum(
        jnp.einsum("irf,fd->ird", hidden_low, down_weight, preferred_element_type=single), "tensor"
    )
    result = (middle + feed_out).astype(half)
    grad_down = jnp.einsum("irf,ird->fd", hidden_low, cotangent, preferred_element_type=single)
    grad_hidden = jnp.einsum("ird,fd->irf", cotangent, down_weight, preferred_element_type=single)
    unused_value, gelu_back = jax.vjp(exact_gelu, hidden_pre)
    grad_pre = gelu_back(grad_hidden)[0].astype(half)
    grad_up = jnp.einsum("ird,irf->df", feed_low, grad_pre, preferred_element_type=single)
    feed_part = jnp.einsum("irf,df->ird", grad_pre, up_weight, preferred_element_type=single)
    grad_feed = lax.psum(feed_part, "tensor")
    grad_middle_norm, grad_feed_gain, grad_feed_bias = norm_back(
        grad_feed, feed_hat, feed_inv, feed_gain
    )
    grad_middle = cotangent.astype(single) + grad_middle_norm
    grad_branch = grad_middle.astype(half)
    grad_output = jnp.einsum("ire,ird->ed", attended, grad_branch, preferred_element_type=single)
    grad_attended = jnp.einsum(
        "ird,ed->ire", grad_branch, output_weight, preferred_element_type=single
    ).astype(half)
    grad_attended = grad_attended.reshape(images, latent_rows, heads_here, HEAD)
    grad_probs = jnp.einsum(
        "irhc,ikhc->ihrk", grad_attended, value_heads, preferred_element_type=single
    )
    grad_scores = (probs * (grad_probs - jnp.sum(probs * grad_probs, -1, keepdims=True))).astype(
        half
    )
    grad_queries = (
        jnp.einsum("ihrk,ikhc->irhc", grad_scores, key_heads, preferred_element_type=single)
        * factor
    ).astype(half)
    grad_queries = grad_queries.reshape(images, latent_rows, inner_here)
    grad_keys = (
        jnp.einsum("ihrk,irhc->ikhc", grad_scores, query_heads, preferred_element_type=single)
        * factor
    ).astype(half)
    grad_keys = grad_keys.reshape(images, keys_all, inner_here)
    grad_values = jnp.einsum(
        "ihrk,irhc->ikhc", probs_low, grad_attended, preferred_element_type=single
    ).astype(half)
    grad_values = grad_values.reshape(images, keys_all, inner_here)
    grad_query = jnp.einsum("ird,ire->de", query_input, grad_queries, preferred_element_type=single)
    grad_key = jnp.einsum("ikd,ike->de", kv_input, grad_keys, preferred_element_type=single)
    grad_value = jnp.einsum("ikd,ike->de", kv_input, grad_values, preferred_element_type=single)
    kv_part = jnp.einsum("ike,de->ikd", grad_keys, key_weight, preferred_element_type=single)
    kv_part = kv_part + jnp.einsum(
        "ike,de->ikd", grad_values, value_weight, preferred_element_type=single
    )
    latent_part = kv_part[:, patches:] + jnp.einsum(
        "ire,de->ird", grad_queries, query_weight, preferred_element_type=single
    )
    media_part = kv_part[:, :patches]
    grad_media_norm, grad_latent_norm = lax.psum((media_part, latent_part), "tensor")
    grad_media, grad_media_gain, grad_media_bias = norm_back(
        grad_media_norm, media_hat, media_inv, media_gain
    )
    grad_latent_in, grad_latent_gain, grad_latent_bias = norm_back(
        grad_latent_norm, latent_hat, latent_inv, latent_gain
    )
    grad_latents = grad_middle + grad_latent_in
    shares = (
        lax.psum_scatter(grad_query, "dp", scatter_dimension=0, tiled=True),
        lax.psum_scatter(grad_key, "dp", scatter_dimension=0, tiled=True),
        lax.psum_scatter(grad_value, "dp", scatter_dimension=0, tiled=True),
        lax.psum_scatter(grad_output, "dp", scatter_dimension=1, tiled=True),
        lax.psum_scatter(grad_up, "dp", scatter_dimension=0, tiled=True),
        lax.psum_scatter(grad_down, "dp", scatter_dimension=1, tiled=True),
        lax.psum_scatter(grad_media_gain, "dp", scatter_dimension=0, tiled=True),
        lax.psum_scatter(grad_media_bias, "dp", scatter_dimension=0, tiled=True),
        lax.psum_scatter(grad_latent_gain, "dp", scatter_dimension=0, tiled=True),
        lax.psum_scatter(grad_latent_bias, "dp", scatter_dimension=0, tiled=True),
        lax.psum_scatter(grad_feed_gain, "dp", scatter_dimension=0, tiled=True),
        lax.psum_scatter(grad_feed_bias, "dp", scatter_dimension=0, tiled=True),
    )
    return (result, grad_media.astype(half), grad_latents.astype(half)) + tuple(shares)


def solution(mesh):
    placed = (
        P("dp", None, None),
        P("dp"),
        P("dp", None, None),
        P("dp", None, None),
        P(None, "tensor"),
        P(None, "tensor"),
        P(None, "tensor"),
        P("tensor", None),
        P(None, "tensor"),
        P("tensor", None),
        P(),
        P(),
        P(),
        P(),
        P(),
        P(),
    )
    return jax.shard_map(
        local,
        mesh=mesh,
        in_specs=placed,
        out_specs=(
            P("dp", None, None),
            P("dp", None, None),
            P("dp", None, None),
            P("dp", "tensor"),
            P("dp", "tensor"),
            P("dp", "tensor"),
            P("tensor", "dp"),
            P("dp", "tensor"),
            P("tensor", "dp"),
            P("dp"),
            P("dp"),
            P("dp"),
            P("dp"),
            P("dp"),
            P("dp"),
        ),
        check_vma=False,
    )
```

profile of v0, /device:TPU:0, one launch (start us, length us, event | category | flops | bytes accessed | tf_op | source)
XLA Modules:
  0.0 840.3 jit_solution(7820481578424748253)
XLA Ops:
  7.3 0.7 multiply_add_fusion.1
  8.0 1.2 convert_reduce_fusion.1
  9.2 1.3 fusion.50
  10.5 3.2 convert_reduce_fusion
  14.3 1.4 fusion.14
  16.6 3.7 fusion.8
  20.3 1.9 convolution_convert_fusion.1
  22.5 2.7 convolution_convert_fusion.2
  25.3 2.4 fusion.74
  27.8 2.8 convolution_convert_fusion.3
  30.6 1.3 fusion.54
  32.3 22.0 %all-reduce.12.cloned.1.call-done = f32[4,64,1024]{2,1,0:T(8,128)} async-done(((f32[4,64,1024]{2,1,0:T(8,128)}), f32[4,64,1024]{2,1,0:T(8,128)}) %all-reduce.12.cloned.1.call-update) | async-done | bytes 1048592 | tf_op jit(solution)/shard_map/psum | solution.py:91
  54.3 1.4 fusion.73
  56.0 4.1 fusion.64
  60.1 4.7 multiply_convert_fusion.2
  64.9 2.0 add_convert_fusion
  66.9 1.0 copy-done.53
  67.9 2.3 fusion.19
  70.5 4.5 fusion.17
  75.0 16.0 %all-reduce.14.cloned.1.call-done = f32[4,64,1024]{2,1,0:T(8,128)} async-done(((f32[4,64,1024]{2,1,0:T(8,128)}), f32[4,64,1024]{2,1,0:T(8,128)}) %all-reduce.14.cloned.1.call-update) | async-done | bytes 1048592 | tf_op jit(solution)/shard_map/psum | solution.py:109
  91.0 2.4 multiply_reduce_fusion.2
  95.0 2.5 convolution_convert_fusion
  97.9 0.7 multiply_reduce_fusion.1
  99.0 0.9 copy-done.21
  101.4 1.6 fusion.56
  103.0 1.6 convolution_add_fusion
  104.6 4.7 slice.8
  109.2 1.5 convolution_add_fusion.1
  110.8 2.5 convolution_bitcast_fusion.2
  113.4 5.3 convolution_bitcast_fusion.3
  119.1 5.4 convolution_bitcast_fusion.4
  124.5 1.5 convolution_bitcast_fusion.5
  126.2 6.4 convolution_bitcast_fusion.1
  132.6 1.0 copy-done.16
  133.6 5.8 convolution_bitcast_fusion
  139.5 0.6 copy-done.52
  141.3 16.2 %all-reduce.16.cloned.1.call-done = (f32[4,64,1024]{2,1,0:T(8,128)}, f32[4,576,1024]{2,1,0:T(8,128)}, f32[4,64,1024]{2,1,0:T(8,128)}) async-done(((f32[4,64,1024]{2,1,0:T(8,128)}, f32[4,576,1024]{2,1,0:T(8,128)}, f32[4,64,1024]{2,1,0:T(8,128)}), (f32[4,64,1024]{2,1,0:T(8,128)}, f32[4,576,1024]{2,1,0:T(8,128)}, f32[4,64,1024]{2,1,0:T(8,128)})) %all-reduce.16.cloned.1.call-update) | async-done | bytes 11534352 | tf_op jit(solution)/shard_map/psum | solution.py:99
  157.5 1.7 fusion.49
  159.3 7.3 fusion.13
  166.6 77.1 %all-reduce.6 = (f32[1024]{0:T(1024)S(1)}, f32[1024]{0:T(1024)S(1)}, f32[1024]{0:T(1024)S(1)}, f32[1024]{0:T(1024)S(1)}, f32[1024]{0:T(1024)S(1)}, /*index=5*/f32[1024]{0:T(1024)S(1)}) all-reduce(f32[1024]{0:T(1024)S(1)} %get-tuple-element.15, f32[1024]{0:T(1024)S(1)} %get-tuple-element.18, ...), channel_id=8, replica_groups=mesh['dp'=16,'tensor'=2] {'dp'}, use_global_device_ids=true, to_apply=%region_27.28.clone | all-reduce | flops 6144 | bytes 49152
  247.2 2.2 add_convert_fusion.1
  249.4 1.2 fusion.48
  250.6 9.1 %fusion.12 = bf16[4,576,1024]{2,1,0:T(8,128)(2,1)} fusion(bf16[4,576,1024]{2,1,0:T(8,128)(2,1)} %param.16, f32[4,576,1024]{2,1,0:T(8,128)} %get-tuple-element.36, f32[4,576]{1,0:T(4,128)S(1)} %broadcast_multiply_fusion, f32[4,576]{1,0:T(4,128)S(1)} %broadcast_multiply_fusion.1, f32[1024]{0:T(1024)S(1)} %copy-done.30, f32[4,576]{1,0:T(4,128)S(1)} %copy-done.28, ...), kind=kLoop, calls=%fused_computation.14 | loop fusion | flops 21233664 | bytes 18915328 | tf_op jit(solution)/shard_map/convert_element_type | solution.py:173
  259.7 57.9 %reduce-scatter.11.cloned.1.call-done = f32[64,256]{1,0:T(8,128)} async-done(((f32[1024,256]{1,0:T(8,128)}), f32[64,256]{1,0:T(8,128)}) %reduce-scatter.11.cloned.1.call-update) | async-done | bytes 65552 | tf_op jit(solution)/shard_map/reduce_scatter | solution.py:162
  317.6 77.8 %reduce-scatter.9.cloned.1.call-done = f32[64,256]{1,0:T(8,128)} async-done(((f32[1024,256]{1,0:T(8,128)}), f32[64,256]{1,0:T(8,128)}) %reduce-scatter.9.cloned.1.call-update) | async-done | bytes 65552 | tf_op jit(solution)/shard_map/reduce_scatter | solution.py:161
  395.4 78.0 %reduce-scatter.7.cloned.1.call-done = f32[64,256]{1,0:T(8,128)} async-done(((f32[1024,256]{1,0:T(8,128)}), f32[64,256]{1,0:T(8,128)}) %reduce-scatter.7.cloned.1.call-update) | async-done | bytes 65552 | tf_op jit(solution)/shard_map/reduce_scatter | solution.py:160
  473.4 177.1 %reduce-scatter.15.cloned.1.call-done = f32[64,2048]{1,0:T(8,128)} async-done(((f32[1024,2048]{1,0:T(8,128)}), f32[64,2048]{1,0:T(8,128)}) %reduce-scatter.15.cloned.1.call-update) | async-done | bytes 524304 | tf_op jit(solution)/shard_map/reduce_scatter | solution.py:164
  650.5 183.2 %reduce-scatter.17.cloned.1.call-done = f32[2048,64]{0,1:T(8,128)} async-done(((f32[2048,1024]{0,1:T(8,128)}), f32[2048,64]{0,1:T(8,128)}) %reduce-scatter.17.cloned.1.call-update) | async-done | bytes 524304 | tf_op jit(solution)/shard_map/reduce_scatter | solution.py:165
  (153 shorter events, 11.2 us)
Async XLA Ops:
  7.2 13.1 %copy-start = (bf16[1024,256]{1,0:T(8,128)(2,1)S(1)}, bf16[1024,256]{1,0:T(8,128)(2,1)}, u32[]{:S(2)}) copy-start(bf16[1024,256]{1,0:T(8,128)(2,1)} %param.21) | copy-start | bytes 1572868
  7.2 47.1 %all-reduce.12.cloned.1.call-start = ((), (), s32[]{:S(2)}) async-start(), calls=%async_computation.6 | async-start | bytes 2097152 | tf_op jit(solution)/shard_map/psum | solution.py:91
  10.5 5.3 copy-start.33
  10.5 3.8 copy-start.2
  14.3 1.8 copy-start.17
  15.8 4.5 copy-start.27
  16.1 6.2 copy-start.7
  16.6 8.7 %copy-start.23 = (bf16[4,64,256]{1,2,0:T(8,128)(2,1)}, bf16[4,64,256]{1,2,0:T(8,128)(2,1)S(1)}, u32[]{:S(2)}) copy-start(bf16[4,64,256]{1,2,0:T(8,128)(2,1)S(1)} %copy.77) | copy-start | bytes 393220
  20.3 2.2 copy-start.6
  20.3 2.2 copy-start.25
  22.5 2.8 copy-start.20
  27.8 2.8 copy-start.43
  27.8 2.9 copy-start.12
  32.0 24.0 %copy-start.41 = (f32[1024]{0:T(1024)S(1)}, f32[1024]{0:T(1024)}, u32[]{:S(2)}) copy-start(f32[1024]{0:T(1024)} %param.30) | copy-start | bytes 12292
  32.0 24.0 %copy-start.49 = (f32[1024]{0:T(1024)S(1)}, f32[1024]{0:T(1024)}, u32[]{:S(2)}) copy-start(f32[1024]{0:T(1024)} %param.31) | copy-start | bytes 12292
  32.0 59.0 %all-reduce.14.cloned.1.call-start = ((), (), s32[]{:S(2)}) async-start(), calls=%async_computation.7 | async-start | bytes 2097152 | tf_op jit(solution)/shard_map/psum | solution.py:109
  55.7 37.7 %copy-start.35 = (f32[4,64]{1,0:T(4,128)}, f32[4,64]{1,0:T(4,128)S(1)}, u32[]{:S(2)}) copy-start(f32[4,64]{1,0:T(4,128)S(1)} %broadcast_multiply_fusion.7) | copy-start | bytes 3076
  56.0 37.4 %copy-start.37 = (f32[4,64]{1,0:T(4,128)}, f32[4,64]{1,0:T(4,128)S(1)}, u32[]{:S(2)}) copy-start(f32[4,64]{1,0:T(4,128)S(1)} %add_rsqrt_fusion.1) | copy-start | bytes 3076
  60.1 4.8 copy-start.14
  60.1 4.8 copy-start.48
  64.9 5.6 copy-start.5
  64.9 2.9 copy-start.47
  70.2 87.3 %all-reduce.16.cloned.1.call-start = ((), (), s32[]{:S(2)}) async-start(), calls=%async_computation.14 | async-start | bytes 23068672 | tf_op jit(solution)/shard_map/psum | solution.py:99
  91.0 2.4 copy-start.10
  91.0 2.4 copy-start.15
  95.0 2.5 copy-start.11
  95.0 2.5 copy-start.44
  95.0 2.9 copy-start.51
  97.9 5.1 copy-start.19
  104.6 4.7 copy-start.18
  110.8 2.6 copy-start.8
  110.8 149.0 %reduce-scatter.13.cloned.1.call-start = ((), (), s32[]{:S(2)}) async-start(), calls=%async_computation.11 | async-start | bytes 1114112 | tf_op jit(solution)/shard_map/reduce_scatter | solution.py:163
  113.4 204.2 %reduce-scatter.11.cloned.1.call-start = ((), (), s32[]{:S(2)}) async-start(), calls=%async_computation.10 | async-start | bytes 1114112 | tf_op jit(solution)/shard_map/reduce_scatter | solution.py:162
  118.8 276.6 %reduce-scatter.9.cloned.1.call-start = ((), (), s32[]{:S(2)}) async-start(), calls=%async_computation.9 | async-start | bytes 1114112 | tf_op jit(solution)/shard_map/reduce_scatter | solution.py:161
  124.4 1.7 copy-start.38
  124.4 1.7 copy-start.42
  124.4 1.7 copy-start.50
  124.5 348.9 %reduce-scatter.7.cloned.1.call-start = ((), (), s32[]{:S(2)}) async-start(), calls=%async_computation.8 | async-start | bytes 1114112 | tf_op jit(solution)/shard_map/reduce_scatter | solution.py:160
  126.1 524.5 %reduce-scatter.15.cloned.1.call-start = ((), (), s32[]{:S(2)}) async-start(), calls=%async_computation.12 | async-start | bytes 8912896 | tf_op jit(solution)/shard_map/reduce_scatter | solution.py:164
  132.6 701.1 %reduce-scatter.17.cloned.1.call-start = ((), (), s32[]{:S(2)}) async-start(), calls=%async_computation.13 | async-start | bytes 8912896 | tf_op jit(solution)/shard_map/reduce_scatter | solution.py:165
  139.4 18.1 %copy-start.32 = (f32[1024]{0:T(1024)S(1)}, f32[1024]{0:T(1024)}, u32[]{:S(2)}) copy-start(f32[1024]{0:T(1024)} %param.28) | copy-start | bytes 12292
  139.4 18.1 %copy-start.34 = (f32[4,64]{1,0:T(4,128)S(1)}, f32[4,64]{1,0:T(4,128)}, u32[]{:S(2)}) copy-start(f32[4,64]{1,0:T(4,128)} %copy-done.33) | copy-start | bytes 3076
  139.4 19.8 %copy-start.28 = (f32[4,576]{1,0:T(4,128)S(1)}, f32[4,576]{1,0:T(4,128)}, u32[]{:S(2)}) copy-start(f32[4,576]{1,0:T(4,128)} %copy-done.27) | copy-start | bytes 27652
  139.4 19.8 %copy-start.30 = (f32[1024]{0:T(1024)S(1)}, f32[1024]{0:T(1024)}, u32[]{:S(2)}) copy-start(f32[1024]{0:T(1024)} %param.26) | copy-start | bytes 12292
  159.3 7.3 copy-start.39
  159.3 7.3 copy-start.40
  243.7 5.7 copy-start.9
  250.6 583.1 %copy-start.1 = (bf16[1024,256]{1,0:T(8,128)(2,1)S(1)}, bf16[1024,256]{1,0:T(8,128)(2,1)}, u32[]{:S(2)}) copy-start(bf16[1024,256]{1,0:T(8,128)(2,1)} %param.21) | copy-start | bytes 1572868
  (15 other events, 18.9 us)
Sparse Core Ops, SparseCore 0:
  32.1 22.1 all-reduce.11
  70.3 20.6 all-reduce.13
  110.9 46.5 all-reduce.15
  160.2 79.8 reduce-scatter.12
  242.8 74.7 reduce-scatter.10
  320.3 75.0 reduce-scatter.8
  398.2 75.1 reduce-scatter.6
  476.3 174.2 reduce-scatter.14
  653.4 180.2 reduce-scatter.16
where the time goes:
time: 843 us; the launch traced here: 840 us
  waiting for transfers between devices  628 us (74%)
  blocking collectives  77.1 us (9%)
  matrix products  60.4 us (7%)
  other arithmetic  43.1 us (5%)
  between operations  15.2 us (2%)
  local copies, waits for them, and re-layouts  14.9 us (2%)
    reduce_scatter x1, waiting for transfers between devices, local(): lax.psum_scatter(grad_down, 'dp', scatter_dimension=1, tiled=True)  183 us
    reduce_scatter x1, waiting for transfers between devices, local(): lax.psum_scatter(grad_up, 'dp', scatter_dimension=0, tiled=True)  177 us
    reduce_scatter x1, waiting for transfers between devices, local(): lax.psum_scatter(grad_query, 'dp', scatter_dimension=0, tiled=True)  78 us
    reduce_scatter x1, waiting for transfers between devices, local(): lax.psum_scatter(grad_key, 'dp', scatter_dimension=0, tiled=True)  77.8 us
    unnamed x1, blocking collectives  77.1 us
    reduce_scatter x1, waiting for transfers between devices, local(): lax.psum_scatter(grad_value, 'dp', scatter_dimension=0, tiled=True)  57.9 us
    psum x1, waiting for transfers between devices, local(): lax.psum(jnp.einsum('ire,ed->ird', attended, output_weight, preferred_ele...  22 us
  transfers between devices with their start and end apart: 9, of which 8 were waited for; matrix products, arithmetic and copies ran while one was open for 7% of the time, Pallas kernels for 0%

commit v1 on v0

v1 whole, which is shorter than its diff:
```python
import jax
import jax.numpy as jnp
from jax import lax
from jax.experimental import pallas as pl
from jax.sharding import PartitionSpec as P

HEAD = 64
PATCH = 576
SHORT = 256
GROUP = 4
EPSILON = 1e-05
SINGLE = jnp.float32
HALF = jnp.bfloat16


def layer_norm(values, gain, offset):
    center = values - jnp.mean(values, -1, keepdims=True)
    inverse = lax.rsqrt(jnp.mean(center * center, -1, keepdims=True) + EPSILON)
    normed = center * inverse
    return (normed * gain + offset, normed, inverse)


def norm_back(upstream, normed, inverse, gain):
    scaled = upstream * gain
    result = inverse * (
        scaled
        - jnp.mean(scaled, -1, keepdims=True)
        - normed * jnp.mean(scaled * normed, -1, keepdims=True)
    )
    return (result, jnp.sum(upstream * normed, axis=(0, 1)), jnp.sum(upstream, axis=(0, 1)))


def exact_gelu(values):
    return jax.nn.gelu(values, approximate=False)


def narrow_body(wide_ref, low_ref):
    low_ref[...] = wide_ref[...].astype(HALF)


def narrow(array):
    count, width = array.shape
    block = 256 if count % 256 == 0 else count
    spec = pl.BlockSpec((block, width), lambda at: (at, 0))
    return pl.pallas_call(
        narrow_body,
        grid=(count // block,),
        in_specs=[spec],
        out_specs=spec,
        out_shape=jax.ShapeDtypeStruct(array.shape, HALF),
        cost_estimate=pl.CostEstimate(
            flops=array.size, bytes_accessed=6 * array.size, transcendentals=0
        ),
        name="narrow",
    )(array)


def pick(array, index, axis):
    return lax.dynamic_index_in_dim(array, index, axis, keepdims=False)


class Links:
    def __init__(self, devices):
        self.devices = devices
        self.bits = devices.bit_length() - 1
        self.row = lax.axis_index("dp")
        self.core = lax.axis_index("tensor")

    def swap(self, array):
        return lax.ppermute(array, "tensor", [(0, 1), (1, 0)])

    def send(self, array, step_zero, step_one):
        pairs = []
        for row in range(self.devices):
            pairs.append((2 * row, 2 * (row ^ step_zero)))
            pairs.append((2 * row + 1, 2 * (row ^ step_one) + 1))
        return lax.ppermute(array, ("dp", "tensor"), pairs)

    def bit(self, which):
        return (self.row >> which) & 1

    def halve(self, blocks, low, high):
        own = self.core == 0
        at = low
        while at < high:
            count = blocks.shape[0]
            rest = blocks.shape[1:]
            if at + 1 < high:
                grid = blocks.reshape((count // 4, 2, 2) + rest)
                first, second = self.bit(at), self.bit(at + 1)
                out = jnp.where(own, pick(grid, 1 - first, 2), pick(grid, 1 - second, 1))
                keep = jnp.where(own, pick(grid, first, 2), pick(grid, second, 1))
                part = keep + self.send(out, 1 << at, 2 << at)
                other = jnp.where(own, second, first)
                blocks = pick(part, other, 1) + self.send(
                    pick(part, 1 - other, 1), 2 << at, 1 << at
                )
                at += 2
            else:
                grid = blocks.reshape((count // 2, 2) + rest)
                mine = self.bit(at)
                blocks = pick(grid, mine, 1) + self.send(pick(grid, 1 - mine, 1), 1 << at, 1 << at)
                at += 1
        return blocks[0]

    def gather(self, rows):
        half = rows.shape[0] // 2
        own = lax.dynamic_slice_in_dim(rows, self.core * half, half, 0)
        near = self.send(own, 1, 2)
        pair = jnp.concatenate([own, near], 0)
        far = self.send(pair, 2, 1)
        mine = jnp.concatenate([pair, far], 0)
        return jnp.concatenate([mine, self.swap(mine)], 0)

    def spread(self, blocks):
        member = self.row % GROUP
        got = [pick(blocks, member, 0)]
        for step in range(1, GROUP):
            got.append(self.send(pick(blocks, member ^ step, 0), step, step))
        stack = jnp.stack(got)
        return [pick(stack, member ^ place, 0) for place in range(GROUP)]


def dot(form, left, right):
    return jnp.einsum(form, left, right, preferred_element_type=SINGLE)


def local(
    media,
    buckets,
    latents,
    cotangent,
    query_weight,
    key_weight,
    value_weight,
    output_weight,
    up_weight,
    down_weight,
    media_gain,
    media_bias,
    latent_gain,
    latent_bias,
    feed_gain,
    feed_bias,
    devices,
):
    links = Links(devices)
    images, patches, width = media.shape
    latent_rows = latents.shape[1]
    rows_here = images * latent_rows
    keys_all = patches + latent_rows
    inner_here = query_weight.shape[1]
    heads_here = inner_here // HEAD
    hidden_here = up_weight.shape[1]
    factor = HEAD ** (-0.5)
    cot_rows = cotangent.reshape(rows_here, width)
    cot_all = narrow(links.gather(cot_rows.astype(SINGLE)))
    weights_other = narrow(
        links.swap(jnp.concatenate([query_weight, key_weight, value_weight], 1).astype(SINGLE))
    )
    media_norm, media_hat, media_inv = layer_norm(media.astype(SINGLE), media_gain, media_bias)
    latent_in = latents.astype(SINGLE)
    latent_norm, latent_hat, latent_inv = layer_norm(latent_in, latent_gain, latent_bias)
    kv_input = jnp.concatenate([media_norm.astype(HALF), latent_norm.astype(HALF)], axis=1)
    query_input = kv_input[:, patches:]
    queries = dot("ird,de->ire", query_input, query_weight).astype(HALF)
    keys = dot("ikd,de->ike", kv_input, key_weight).astype(HALF)
    values = dot("ikd,de->ike", kv_input, value_weight).astype(HALF)
    query_heads = queries.reshape(images, latent_rows, heads_here, HEAD)
    key_heads = keys.reshape(images, keys_all, heads_here, HEAD)
    value_heads = values.reshape(images, keys_all, heads_here, HEAD)
    counts = SHORT + (PATCH - SHORT) * buckets
    position = lax.broadcasted_iota(jnp.int32, (images, keys_all), 1)
    usable = (position < counts[:, None]) | (position >= patches)
    scores = dot("irhc,ikhc->ihrk", query_heads, key_heads) * factor
    scores = jnp.where(usable[:, None, None, :], scores, -1e30)
    shifted = jnp.exp(scores - jnp.max(scores, -1, keepdims=True))
    probs = shifted / jnp.sum(shifted, -1, keepdims=True)
    probs_low = probs.astype(HALF)
    attended = dot("ihrk,ikhc->irhc", probs_low, value_heads)
    attended = attended.reshape(images, latent_rows, inner_here).astype(HALF)
    branch = dot("ire,ed->ird", attended, output_weight)
    middle = latent_in + (branch + links.swap(branch))
    feed_norm, feed_hat, feed_inv = layer_norm(middle, feed_gain, feed_bias)
    feed_low = feed_norm.astype(HALF)
    feed_all = narrow(links.gather(feed_low.astype(SINGLE).reshape(rows_here, width)))
    hidden_pre = dot("ird,df->irf", feed_low, up_weight)
    hidden_low = exact_gelu(hidden_pre).astype(HALF)
    grad_hidden = dot("ird,fd->irf", cotangent, down_weight)
    unused_value, gelu_back = jax.vjp(exact_gelu, hidden_pre)
    grad_pre = gelu_back(grad_hidden)[0].astype(HALF)
    feed_part = dot("irf,df->ird", grad_pre, up_weight)
    grad_feed = feed_part + links.swap(feed_part)
    feed_out = dot("irf,fd->ird", hidden_low, down_weight)
    result = (middle + (feed_out + links.swap(feed_out))).astype(HALF)
    grad_middle_norm, grad_feed_gain, grad_feed_bias = norm_back(
        grad_feed, feed_hat, feed_inv, feed_gain
    )
    grad_middle = cotangent.astype(SINGLE) + grad_middle_norm
    grad_branch = grad_middle.astype(HALF)

    member = links.row % GROUP
    piece = hidden_here // GROUP
    up_piece = lax.dynamic_slice_in_dim(up_weight, member * piece, piece, 1)
    down_piece = lax.dynamic_slice_in_dim(down_weight, member * piece, piece, 0)
    pre_all = dot("rd,df->rf", feed_all, up_piece)
    hidden_all = exact_gelu(pre_all).astype(HALF)
    back_all = dot("rd,fd->rf", cot_all, down_piece)
    grad_pre_all = jax.vjp(exact_gelu, pre_all)[1](back_all)[0].astype(HALF)
    grad_up = dot("rd,rf->df", feed_all, grad_pre_all)
    grad_down = dot("rd,rf->df", cot_all, hidden_all)
    wide = jnp.concatenate([grad_up, grad_down], 1).reshape(devices // GROUP, -1, 2 * piece)
    wide = links.halve(wide, 2, links.bits)
    share = wide.shape[0] // GROUP
    wide = links.spread(wide.reshape(GROUP, share, 2 * piece))
    grad_up = jnp.concatenate([block[:, :piece] for block in wide], 1)
    grad_down = jnp.concatenate([block[:, piece:] for block in wide], 1).T

    grad_attended = dot("ird,ed->ire", grad_branch, output_weight).astype(HALF)
    grad_attended = grad_attended.reshape(images, latent_rows, heads_here, HEAD)
    grad_probs = dot("irhc,ikhc->ihrk", grad_attended, value_heads)
    grad_scores = (probs * (grad_probs - jnp.sum(probs * grad_probs, -1, keepdims=True))).astype(
        HALF
    )
    grad_queries = (dot("ihrk,ikhc->irhc", grad_scores, key_heads) * factor).astype(HALF)
    grad_queries = grad_queries.reshape(images, latent_rows, inner_here)
    grad_keys = (dot("ihrk,irhc->ikhc", grad_scores, query_heads) * factor).astype(HALF)
    grad_keys = grad_keys.reshape(images, keys_all, inner_here)
    grad_values = dot("ihrk,irhc->ikhc", probs_low, grad_attended).astype(HALF)
    grad_values = grad_values.reshape(images, keys_all, inner_here)
    small = jnp.concatenate(
        [
            dot("ikd,ike->de", kv_input, grad_keys),
            dot("ikd,ike->de", kv_input, grad_values),
            dot("ird,ire->de", query_input, grad_queries),
            dot("ird,ire->de", grad_branch, attended),
        ],
        1,
    )
    small = links.halve(small.reshape(devices, -1, 4 * inner_here), 0, links.bits)
    grad_key, grad_value, grad_query, grad_output = jnp.split(small, 4, axis=1)

    heads_out = jnp.concatenate([grad_keys, grad_values], 2)
    heads_in = links.swap(heads_out.astype(SINGLE))
    heads_in = narrow(heads_in.reshape(-1, 2 * inner_here)).reshape(heads_out.shape)
    query_in = links.swap(grad_queries.astype(SINGLE))
    query_in = narrow(query_in.reshape(-1, inner_here)).reshape(grad_queries.shape)
    all_heads = jnp.concatenate([heads_out, heads_in], 2)
    weights_kv = jnp.concatenate([key_weight, value_weight, weights_other[:, inner_here:]], 1)
    weights_q = jnp.concatenate([query_weight, weights_other[:, :inner_here]], 1)
    grad_media_norm = dot("ike,de->ikd", all_heads[:, :patches], weights_kv)
    grad_latent_norm = dot("ike,de->ikd", all_heads[:, patches:], weights_kv) + dot(
        "ire,de->ird", jnp.concatenate([grad_queries, query_in], 2), weights_q
    )
    grad_media, grad_media_gain, grad_media_bias = norm_back(
        grad_media_norm, media_hat, media_inv, media_gain
    )
    grad_latent_in, grad_latent_gain, grad_latent_bias = norm_back(
        grad_latent_norm, latent_hat, latent_inv, latent_gain
    )
    grad_latents = grad_middle + grad_latent_in
    vectors = jnp.stack(
        [
            grad_media_gain,
            grad_media_bias,
            grad_latent_gain,
            grad_latent_bias,
            grad_feed_gain,
            grad_feed_bias,
        ]
    )
    vectors = vectors.reshape(6, devices, -1).transpose(1, 0, 2)
    vectors = links.halve(vectors, 0, links.bits)
    return (
        result,
        grad_media.astype(HALF),
        grad_latents.astype(HALF),
        grad_query,
        grad_key,
        grad_value,
        grad_output.T,
        grad_up,
        grad_down,
    ) + tuple(vectors[at] for at in range(6))


def solution(mesh):
    devices = mesh.shape["dp"]
    images = P("dp", None, None)
    columns = P(None, "tensor")
    lines = P("tensor", None)

    def body(*args):
        return local(*args, devices=devices)

    return jax.shard_map(
        body,
        mesh=mesh,
        in_specs=(images, P("dp"), images, images)
        + (columns, columns, columns, lines, columns, lines)
        + (P(),) * 6,
        out_specs=(images,) * 3
        + (P("dp", "tensor"),) * 3
        + (P("tensor", "dp"), P("dp", "tensor"), P("tensor", "dp"))
        + (P("dp"),) * 6,
        check_vma=False,
    )
```

time: 843 us -> 378 us (0.45)
  waiting for transfers between devices: 628 us -> 78.4 us
  blocking collectives: 77.1 us -> 0 us
  local copies, waits for them, and re-layouts: 14.9 us -> 71.1 us
  other arithmetic: 43.1 us -> 89.2 us
  starting transfers between devices: 1.04 us -> 25.8 us
  matrix products: 60.4 us -> 83.7 us
  Pallas kernels: 0 us -> 21.3 us
  between operations: 15.2 us -> 2.08 us
    reduce_scatter x6 -> x0, waiting for transfers between devices: 574 us -> none  [the longest x1 183 us: local(): lax.psum_scatter(grad_down, 'dp', scatter_dimension=1, tiled=True)]
    ppermute x0 -> x25, waiting for transfers between devices: none -> 78.4 us  [the longest x17 78.4 us: send(): return lax.ppermute(array, ('dp', 'tensor'), pairs)]
    unnamed x1 -> x0, blocking collectives: 77.1 us -> none
    psum x3 -> x0, waiting for transfers between devices: 54.3 us -> none  [the longest x1 22 us: local(): lax.psum(jnp.einsum('ire,ed->ird', attended, output_weight, preferred_ele...]
    dynamic_slice x0 -> x11, local copies, waits for them, and re-layouts: none -> 36.2 us  [the longest x10 36.1 us: pick(): return lax.dynamic_index_in_dim(array, index, axis, keepdims=False)]
    concatenate x0 -> x10, other arithmetic: none -> 31.1 us  [the longest x2 9.03 us: gather(): return jnp.concatenate([mine, self.swap(mine)], 0)]
    ppermute x0 -> x25, starting transfers between devices: none -> 25.8 us  [the longest x17 24.2 us: send(): return lax.ppermute(array, ('dp', 'tensor'), pairs)]
    dot_general x23, matrix products: 58 us -> 81.3 us  [dot(): return jnp.einsum(form, left, right, preferred_element_type=SINGLE)]
  transfers between devices with their start and end apart: 9 -> 25, of which waited for: 8 -> 7; matrix products, arithmetic and copies ran while one was open for 7% -> 57% of each run, Pallas kernels for 0% -> 6%
where the time goes in v1:
time: 378 us; the launch traced here: 372 us
  other arithmetic  89.2 us (24%)
  matrix products  83.7 us (22%)
  waiting for transfers between devices  78.4 us (21%)
  local copies, waits for them, and re-layouts  71.1 us (19%)
  starting transfers between devices  25.8 us (7%)
  Pallas kernels  21.3 us (6%)
    dot_general x23, matrix products, dot(): return jnp.einsum(form, left, right, preferred_element_type=SINGLE)  81.3 us
    ppermute x17, waiting for transfers between devices, send(): return lax.ppermute(array, ('dp', 'tensor'), pairs)  78.4 us
    dynamic_slice x10, local copies, waits for them, and re-layouts, pick(): return lax.dynamic_index_in_dim(array, index, axis, keepdims=False)  36.1 us
    ppermute x17, starting transfers between devices, send(): return lax.ppermute(array, ('dp', 'tensor'), pairs)  24.2 us
    pallas_call x5, Pallas kernels, narrow(): pl.pallas_call(narrow_body, grid=(count // block,), in_specs=[spec], out_...  21.3 us
    convert_element_type x1, other arithmetic, local(): grad_media.astype(HALF)  9.09 us
    concatenate x2, other arithmetic, gather(): return jnp.concatenate([mine, self.swap(mine)], 0)  9.03 us
    select_n x5, other arithmetic, halve(): out = jnp.where(own, pick(grid, 1 - first, 2), pick(grid, 1 - second, 1))  8.35 us
  transfers between devices with their start and end apart: 25, of which 7 were waited for; matrix products, arithmetic and copies ran while one was open for 57% of the time, Pallas kernels for 6%

profile of v1, /device:TPU:0, one launch (start us, length us, event | category | flops | bytes accessed | tf_op | source)
XLA Modules:
  0.0 371.6 jit_solution(1529351410238651227)
XLA Ops:
  4.0 3.2 convert_reduce_fusion
  10.1 3.7 fusion.8
  16.0 2.9 convolution_convert_fusion.2
  21.4 2.8 convolution_convert_fusion.3
  25.4 3.0 collective-permute-start.13
  28.5 7.2 %collective-permute-done.13 = f32[128,1024]{1,0:T(8,128)S(1)} collective-permute-done((f32[128,1024]{1,0:T(8,128)S(1)}, f32[128,1024]{1,0:T(8,128)S(1)}, u32[]{:S(2)}, u32[]{:S(2)}) %collective-permute-start.13) | collective-permute-done | bytes 524320 | tf_op jit(solution)/shard_map/ppermute | solution.py:77
  42.9 3.9 %fusion.94 = (u8[64,2048]{1,0:T(8,128)(4,1)}, u8[64,2048]{1,0:T(8,128)(4,1)}, f32[4,64,2048]{2,1,0:T(8,128)}) fusion(bf16[4,64,1024]{2,1,0:T(8,128)(2,1)S(1)} %add_convert_fusion.3, bf16[1024,2048]{1,0:T(8,128)(2,1)S(1)} %copy-done.59), kind=kOutput, calls=%fused_computation.172 | convolution fusion | flops 1080295424 | bytes 7077888 | tf_op jit(solution)/shard_map/ird,df->irf/dot_general | solution.py:125
  46.8 12.4 %fusion.21 = f32[4,64,1024]{2,1,0:T(8,128)} fusion(bf16[1024,2048]{1,0:T(8,128)(2,1)} %param.24, bf16[4,64,1024]{2,1,0:T(8,128)(2,1)} %param.19, bf16[2048,1024]{1,0:T(8,128)(2,1)} %param.25, f32[4,64,2048]{2,1,0:T(8,128)} %get-tuple-element.72, u8[64,2048]{1,0:T(8,128)(4,1)} %get-tuple-element.22, u8[64,2048]{1,0:T(8,128)(4,1)} %get-tuple-element.21), kind=kOutput, calls=%fused_computation.30 | convolution fusion | flops 2187853824 | bytes 12320768 | tf_op jit(solution)/shard_map/irf,df->ird/dot_general | solution.py:125
  59.2 9.6 %fusion.19 = f32[4,64,1024]{2,1,0:T(8,128)} fusion(bf16[2048,1024]{1,0:T(8,128)(2,1)} %param.25, f32[4,64,2048]{2,1,0:T(8,128)} %get-tuple-element.72, u8[64,2048]{1,0:T(8,128)(4,1)} %get-tuple-element.22, u8[64,2048]{1,0:T(8,128)(4,1)} %get-tuple-element.21), kind=kOutput, calls=%fused_computation.28 | convolution fusion | flops 1110441984 | bytes 7602176 | tf_op jit(solution)/shard_map/irf,fd->ird/dot_general | solution.py:125
  69.3 2.9 pad_maximum_fusion.7
  77.3 2.7 multiply_add_fusion
  92.0 2.6 pad_maximum_fusion.2
  94.6 5.5 %copy.116 = f32[1024,1024]{1,0:T(8,128)} copy(f32[1024,1024]{0,1:T(8,128)} %pad_maximum_fusion.2) | data formatting | bytes 8388608 | tf_op jit(solution)/shard_map/concatenate | solution.py:231
  100.1 4.2 %bitcast_select_fusion.2 = f32[4,2,64,1024]{3,2,1,0:T(8,128)} fusion(f32[4,2,2,64,1024]{4,3,2,1,0:T(8,128)} %bitcast.213, s32[]{:T(128)S(6)} %select_n.231, s32[]{:T(128)S(6)} %select_n.230, pred[]{:T(512)S(6)} %eq.8), kind=kLoop, calls=%fused_computation.55 | loop fusion | flops 524288 | bytes 6291465 | tf_op jit(solution)/shard_map/jit(_where)/select_n | solution.py:91
  104.5 3.1 pad_maximum_fusion.6
  110.0 4.5 %maximum_convert_fusion = f32[4,640,512]{1,2,0:T(8,128)} fusion(bf16[4,640,256]{1,2,0:T(8,128)(2,1)} %bitcast.224, bf16[4,640,256]{1,2,0:T(8,128)(2,1)} %bitcast.217), kind=kLoop, calls=%fused_computation.36 | loop fusion | flops 5242880 | bytes 7864320 | tf_op jit(solution)/shard_map/convert_element_type | solution.py:244
  114.6 4.4 %pad_maximum_fusion.4.wide_ref = f32[1024,1024]{1,0:T(8,128)} fusion(f32[512,1024]{1,0:T(8,128)} %collective-permute-done.15, f32[256,1024]{1,0:T(8,128)} %collective-permute-done.14, f32[128,1024]{1,0:T(8,128)S(1)} %copy-done.19, f32[128,1024]{1,0:T(8,128)S(1)} %constant_dynamic-slice_fusion.11), kind=kLoop, calls=%fused_computation.24 | loop fusion | flops 3145728 | bytes 8388608 | tf_op jit(solution)/shard_map/concatenate | solution.py:113
  119.0 4.2 %narrow.9 = bf16[1024,1024]{1,0:T(8,128)(2,1)} custom-call(f32[1024,1024]{1,0:T(8,128)} %pad_maximum_fusion.4.wide_ref), custom_call_target="tpu_custom_call" | custom-call | flops 1048576 | bytes 6291456 | tf_op jit(solution)/shard_map/narrow/pallas_call | solution.py:45
  123.2 7.4 %collective-permute-done.6 = f32[4,2,64,1024]{3,2,1,0:T(8,128)} collective-permute-done((f32[4,2,64,1024]{3,2,1,0:T(8,128)}, f32[4,2,64,1024]{3,2,1,0:T(8,128)}, u32[]{:S(2)}, u32[]{:S(2)}) %collective-permute-start.6) | collective-permute-done | bytes 2097184 | tf_op jit(solution)/shard_map/ppermute | solution.py:77
  130.6 3.5 fusion.28
  137.3 4.6 %pad_maximum_fusion.3.wide_ref = f32[1024,1024]{1,0:T(8,128)} fusion(f32[512,1024]{1,0:T(8,128)} %collective-permute-done.12, f32[256,1024]{1,0:T(8,128)} %collective-permute-done.11, f32[128,1024]{1,0:T(8,128)} %collective-permute-done.10, f32[128,1024]{1,0:T(8,128)S(1)} %copy-done.11), kind=kLoop, calls=%fused_computation.23 | loop fusion | flops 3145728 | bytes 8388608 | tf_op jit(solution)/shard_map/concatenate | solution.py:113
  141.9 4.2 %narrow.8 = bf16[1024,1024]{1,0:T(8,128)(2,1)} custom-call(f32[1024,1024]{1,0:T(8,128)} %pad_maximum_fusion.3.wide_ref), custom_call_target="tpu_custom_call" | custom-call | flops 1048576 | bytes 6291456 | tf_op jit(solution)/shard_map/narrow/pallas_call | solution.py:45
  146.2 4.4 %fusion.74 = f32[1024,512]{1,0:T(8,128)} fusion(bf16[1024,1024]{1,0:T(8,128)(2,1)} %narrow.8, bf16[1024,2048]{1,0:T(8,128)(2,1)} %param.24, s32[]{:T(128)S(6)} %select_n.248), kind=kOutput, calls=%fused_computation.141 | convolution fusion | flops 1073741824 | bytes 5242884 | tf_op jit(solution)/shard_map/rd,df->rf/dot_general | solution.py:125
  150.6 11.6 %fusion.70 = f32[1024,512]{0,1:T(8,128)} fusion(bf16[1024,1024]{1,0:T(8,128)(2,1)} %narrow.8, f32[1024,512]{1,0:T(8,128)} %fusion.74, bf16[1024,1024]{1,0:T(8,128)(2,1)} %narrow.9, bf16[2048,1024]{1,0:T(8,128)(2,1)} %param.25, s32[]{:T(128)S(6)} %select_n.248), kind=kOutput, calls=%fused_computation.138 | convolution fusion | flops 2185232384 | bytes 9437188 | tf_op jit(solution)/shard_map/rd,rf->df/dot_general | solution.py:125
  162.2 7.8 %fusion.61 = f32[1024,512]{0,1:T(8,128)S(1)} fusion(bf16[1024,1024]{1,0:T(8,128)(2,1)} %narrow.9, f32[1024,512]{1,0:T(8,128)} %fusion.74), kind=kOutput, calls=%fused_computation.124 | convolution fusion | flops 1107820544 | bytes 6291456 | tf_op jit(solution)/shard_map/rd,rf->df/dot_general | solution.py:125
  172.5 6.6 %reshape_reshape.7 = f32[1,2,2,256,1024]{3,2,1,4,0:T(2,128)} reshape(f32[1024,1024]{0,1:T(8,128)} %pad_maximum_fusion.5) | data formatting | bytes 8388608 | tf_op jit(solution)/shard_map/reshape;reshape | solution.py:89
  179.1 9.9 %constant_dynamic-slice_fusion.10 = (f32[1,2,1,256,1024]{3,2,1,4,0:T(1,128)}, f32[1,2,1,256,1024]{3,2,1,4,0:T(1,128)}) fusion(f32[1,2,2,256,1024]{3,2,1,4,0:T(2,128)} %reshape_reshape.7, s32[]{:T(128)S(6)} %select_n.236, s32[]{:T(128)S(6)} %select_n.239), kind=kLoop, calls=%fused_computation.210 | loop fusion | bytes 8388616 | tf_op jit(solution)/shard_map/jit(dynamic_index_in_dim)/dynamic_slice | solution.py:59
  189.0 6.0 %copy.119 = f32[1,2,1,256,1024]{4,3,1,2,0:T(8,128)} copy(f32[1,2,1,256,1024]{3,2,1,4,0:T(1,128)} %get-tuple-element.33) | data formatting | bytes 4194304 | tf_op jit(solution)/shard_map/jit(dynamic_index_in_dim)/dynamic_slice | solution.py:59
  195.0 5.7 %constant_dynamic-slice_fusion.9 = (f32[1,1,2,256,1024]{3,2,1,4,0:T(2,128)}, f32[1,1,2,256,1024]{3,2,1,4,0:T(2,128)}) fusion(f32[1,2,2,256,1024]{3,2,1,4,0:T(2,128)} %reshape_reshape.7, s32[]{:T(128)S(6)} %select_n.237, s32[]{:T(128)S(6)} %select_n.240), kind=kLoop, calls=%fused_computation.209 | loop fusion | bytes 8388616 | tf_op jit(solution)/shard_map/jit(dynamic_index_in_dim)/dynamic_slice | solution.py:59
  200.7 4.1 %copy.120 = f32[1,1,2,256,1024]{4,3,2,1,0:T(8,128)} copy(f32[1,1,2,256,1024]{3,2,1,4,0:T(2,128)} %get-tuple-element.35) | data formatting | bytes 4194304 | tf_op jit(solution)/shard_map/jit(dynamic_index_in_dim)/dynamic_slice | solution.py:59
  204.9 4.1 %bitcast_select_fusion = f32[1,2,256,1024]{3,2,1,0:T(8,128)} fusion(f32[1,1,2,256,1024]{4,3,2,1,0:T(8,128)} %copy.120, f32[1,2,1,256,1024]{4,3,1,2,0:T(8,128)} %copy.119, pred[]{:T(512)S(6)} %eq.8), kind=kLoop, calls=%fused_computation.52 | loop fusion | flops 524288 | bytes 6291457 | tf_op jit(solution)/shard_map/jit(_where)/select_n | solution.py:91
  213.7 54.2 %collective-permute-done.8 = f32[1,2,64,1024]{3,2,1,0:T(8,128)} collective-permute-done((f32[1,2,64,1024]{3,2,1,0:T(8,128)S(1)}, f32[1,2,64,1024]{3,2,1,0:T(8,128)}, u32[]{:S(2)}, u32[]{:S(2)}) %collective-permute-start.8) | collective-permute-done | bytes 524320 | tf_op jit(solution)/shard_map/ppermute | solution.py:77
  269.0 2.7 collective-permute-start.9
  274.2 2.7 copy.111
  278.6 3.9 %narrow.6 = bf16[1024,768]{1,0:T(8,128)(2,1)} custom-call(f32[1024,768]{1,0:T(8,128)} %collective-permute-done.4.wide_ref), custom_call_target="tpu_custom_call" | custom-call | flops 786432 | bytes 4718592 | tf_op jit(solution)/shard_map/narrow/pallas_call | solution.py:45
  286.4 4.1 %copy.118 = f32[1,1,2,256,1024]{4,3,2,1,0:T(8,128)} copy(f32[1,1,2,256,1024]{3,2,1,4,0:T(2,128)} %get-tuple-element.34) | data formatting | bytes 4194304 | tf_op jit(solution)/shard_map/jit(dynamic_index_in_dim)/dynamic_slice | solution.py:59
  290.5 6.0 %copy.117 = f32[1,2,1,256,1024]{4,3,1,2,0:T(8,128)} copy(f32[1,2,1,256,1024]{3,2,1,4,0:T(1,128)} %get-tuple-element.32) | data formatting | bytes 4194304 | tf_op jit(solution)/shard_map/jit(dynamic_index_in_dim)/dynamic_slice | solution.py:59
  297.3 3.5 fusion.27
  302.6 6.0 %copy.109 = f32[4,640,512]{2,1,0:T(8,128)} copy(f32[4,640,512]{1,2,0:T(8,128)} %collective-permute-done.3) | data formatting | bytes 10485760 | tf_op jit(solution)/shard_map/ppermute | solution.py:70
  308.6 7.3 %narrow.5 = bf16[2560,512]{1,0:T(8,128)(2,1)} custom-call(f32[2560,512]{1,0:T(8,128)} %bitcast.215), custom_call_target="tpu_custom_call" | custom-call | flops 1310720 | bytes 7864320 | tf_op jit(solution)/shard_map/narrow/pallas_call | solution.py:45
  316.0 6.8 %pad_maximum_fusion.1 = bf16[4,640,1024]{2,1,0:T(8,128)(2,1)} fusion(bf16[4,640,512]{2,1,0:T(8,128)(2,1)} %bitcast.219, bf16[4,640,256]{2,1,0:T(8,128)(2,1)} %copy.111, bf16[4,640,256]{2,1,0:T(8,128)(2,1)} %copy.110), kind=kLoop, calls=%fused_computation.19 | loop fusion | flops 15728640 | bytes 10485760 | tf_op jit(solution)/shard_map/concatenate | solution.py:248
  324.9 11.8 %fusion.13 = (f32[1024]{0:T(1024)S(1)}, f32[4,576]{1,0:T(4,128)S(1)}, f32[4,576]{1,0:T(4,128)S(1)}, f32[1024]{0:T(1024)S(1)}, f32[4,576,1024]{2,1,0:T(8,128)}) fusion(bf16[4,576,1024]{2,1,0:T(8,128)(2,1)} %param.16, f32[4,576]{1,0:T(4,128)S(1)} %copy-done.45, f32[4,576]{1,0:T(4,128)S(1)} %copy-done.42, f32[1024]{0:T(1024)S(1)} %copy-done.52, ...), kind=kOutput, calls=%fused_computation.15 | convolution fusion | flops 4861716480 | bytes 21020672 | tf_op jit(solution)/shard_map/ike,de->ikd/dot_general | solution.py:125
  337.3 9.1 %fusion.12 = bf16[4,576,1024]{2,1,0:T(8,128)(2,1)} fusion(bf16[4,576,1024]{2,1,0:T(8,128)(2,1)} %param.16, f32[4,576,1024]{2,1,0:T(8,128)} %get-tuple-element.75, f32[4,576]{1,0:T(4,128)S(1)} %broadcast_multiply_fusion, f32[4,576]{1,0:T(4,128)S(1)} %broadcast_multiply_fusion.1, f32[1024]{0:T(1024)S(1)} %copy-done.52, f32[4,576]{1,0:T(4,128)S(1)} %copy-done.45, ...), kind=kLoop, calls=%fused_computation.14 | loop fusion | flops 21233664 | bytes 18915328 | tf_op jit(solution)/shard_map/convert_element_type | solution.py:276
  347.0 3.2 collective-permute-done.22
  350.3 2.6 collective-permute-start.23
  354.5 2.9 collective-permute-start.24
  363.1 3.3 collective-permute-done.20
  366.4 2.7 collective-permute-done.19
  (263 shorter events, 73.8 us)
Async XLA Ops:
  0.6 23.6 %copy-start = (bf16[256,1024]{1,0:T(8,128)(2,1)S(1)}, bf16[256,1024]{1,0:T(8,128)(2,1)}, u32[]{:S(2)}) copy-start(bf16[256,1024]{1,0:T(8,128)(2,1)} %param.23) | copy-start | bytes 1572868
  2.6 6.6 %copy-start.47 = (f32[4,64]{1,0:T(4,128)}, f32[4,64]{1,0:T(4,128)S(1)}, u32[]{:S(2)}) copy-start(f32[4,64]{1,0:T(4,128)S(1)} %broadcast_multiply_fusion.8) | copy-start | bytes 3076
  3.9 5.3 %copy-start.49 = (f32[4,64]{1,0:T(4,128)}, f32[4,64]{1,0:T(4,128)S(1)}, u32[]{:S(2)}) copy-start(f32[4,64]{1,0:T(4,128)S(1)} %add_rsqrt_fusion.2) | copy-start | bytes 3076
  9.6 6.2 %copy-start.16 = (bf16[4,64,1024]{2,1,0:T(8,128)(2,1)}, bf16[4,64,1024]{2,1,0:T(8,128)(2,1)S(1)}, u32[]{:S(2)}) copy-start(bf16[4,64,1024]{2,1,0:T(8,128)(2,1)S(1)} %fusion.53) | copy-start | bytes 1572868
  10.1 8.9 %copy-start.33 = (bf16[4,64,256]{1,2,0:T(8,128)(2,1)}, bf16[4,64,256]{1,2,0:T(8,128)(2,1)S(1)}, u32[]{:S(2)}) copy-start(bf16[4,64,256]{1,2,0:T(8,128)(2,1)S(1)} %copy.128) | copy-start | bytes 393220
  24.5 12.2 %copy-start.20 = (f32[4,64,1024]{2,1,0:T(8,128)}, f32[4,64,1024]{2,1,0:T(8,128)S(1)}, u32[]{:S(2)}) copy-start(f32[4,64,1024]{2,1,0:T(8,128)S(1)} %fusion.88) | copy-start | bytes 3145732
  24.6 14.3 %collective-permute-start = (f32[4,64,1024]{2,1,0:T(8,128)S(1)}, f32[4,64,1024]{2,1,0:T(8,128)}, u32[]{:S(2)}, u32[]{:S(2)}) collective-permute-start(f32[4,64,1024]{2,1,0:T(8,128)S(1)} %fusion.88), channel_id=1, source_target_pairs={{0,1},{1,0},{2,3},{3,2},{4,5},{5,4},{6,7},{7,6},{8,9},{9,8},{10,11... | collective-permute-start | bytes 3145736 | tf_op jit(solution)/shard_map/ppermute | solution.py:70
  25.4 10.2 %collective-permute-start.13 = (f32[128,1024]{1,0:T(8,128)S(1)}, f32[128,1024]{1,0:T(8,128)S(1)}, u32[]{:S(2)}, u32[]{:S(2)}) collective-permute-start(f32[128,1024]{1,0:T(8,128)S(1)} %constant_dynamic-slice_fusion.11), channel_id=1, source_target_pairs={{0,2},{1,5},{2,0},{3,7},{4,6},{5,1},{6,4},{7,3},{8,10},{9,13},{10,... | collective-permute-start | bytes 1572872 | tf_op jit(solution)/shard_map/ppermute | solution.py:77
  35.6 33.7 %copy-start.18 = (f32[128,1024]{1,0:T(8,128)}, f32[128,1024]{1,0:T(8,128)S(1)}, u32[]{:S(2)}) copy-start(f32[128,1024]{1,0:T(8,128)S(1)} %collective-permute-done.13) | copy-start | bytes 1572868
  36.8 32.5 %collective-permute-start.14 = (f32[256,1024]{1,0:T(8,128)}, f32[256,1024]{1,0:T(8,128)}, u32[]{:S(2)}, u32[]{:S(2)}) collective-permute-start(f32[256,1024]{1,0:T(8,128)} %pad_maximum_fusion.9), channel_id=1, source_target_pairs={{0,4},{1,3},{2,6},{3,1},{4,0},{5,7},{6,2},{7,5},{8,12},{9,11},{10,... | collective-permute-start | bytes 3145736 | tf_op jit(solution)/shard_map/ppermute | solution.py:77
  41.4 30.9 %copy-start.10 = (f32[128,1024]{1,0:T(8,128)}, f32[128,1024]{1,0:T(8,128)S(1)}, u32[]{:S(2)}) copy-start(f32[128,1024]{1,0:T(8,128)S(1)} %dynamic-slice_convert_fusion) | copy-start | bytes 1572868
  41.4 30.9 %collective-permute-start.10 = (f32[128,1024]{1,0:T(8,128)S(1)}, f32[128,1024]{1,0:T(8,128)}, u32[]{:S(2)}, u32[]{:S(2)}) collective-permute-start(f32[128,1024]{1,0:T(8,128)S(1)} %dynamic-slice_convert_fusion), channel_id=1, source_target_pairs={{0,2},{1,5},{2,0},{3,7},{4,6},{5,1},{6,4},{7,3},{8,10},{9,13},{10,... | collective-permute-start | bytes 1572872 | tf_op jit(solution)/shard_map/ppermute | solution.py:77
  59.2 15.7 %collective-permute-start.2 = (f32[4,64,1024]{2,1,0:T(8,128)}, f32[4,64,1024]{2,1,0:T(8,128)}, u32[]{:S(2)}, u32[]{:S(2)}) collective-permute-start(f32[4,64,1024]{2,1,0:T(8,128)} %fusion.21), channel_id=1, source_target_pairs={{0,1},{1,0},{2,3},{3,2},{4,5},{5,4},{6,7},{7,6},{8,9},{9,8},{10,11... | collective-permute-start | bytes 3145736 | tf_op jit(solution)/shard_map/ppermute | solution.py:70
  68.8 8.5 %collective-permute-start.1 = (f32[4,64,1024]{2,1,0:T(8,128)}, f32[4,64,1024]{2,1,0:T(8,128)}, u32[]{:S(2)}, u32[]{:S(2)}) collective-permute-start(f32[4,64,1024]{2,1,0:T(8,128)} %fusion.19), channel_id=1, source_target_pairs={{0,1},{1,0},{2,3},{3,2},{4,5},{5,4},{6,7},{7,6},{8,9},{9,8},{10,11... | collective-permute-start | bytes 3145736 | tf_op jit(solution)/shard_map/ppermute | solution.py:70
  69.3 5.6 %copy-start.30 = (f32[4,64,1024]{2,1,0:T(8,128)S(1)}, f32[4,64,1024]{2,1,0:T(8,128)}, u32[]{:S(2)}) copy-start(f32[4,64,1024]{2,1,0:T(8,128)} %fusion.21) | copy-start | bytes 3145732
  72.2 42.3 %collective-permute-start.15 = (f32[512,1024]{1,0:T(8,128)}, f32[512,1024]{1,0:T(8,128)}, u32[]{:S(2)}, u32[]{:S(2)}) collective-permute-start(f32[512,1024]{1,0:T(8,128)} %pad_maximum_fusion.7), channel_id=1, source_target_pairs={{0,1},{1,0},{2,3},{3,2},{4,5},{5,4},{6,7},{7,6},{8,9},{9,8},{10,11... | collective-permute-start | bytes 6291464 | tf_op jit(solution)/shard_map/ppermute | solution.py:70
  74.4 30.1 %collective-permute-start.11 = (f32[256,1024]{1,0:T(8,128)}, f32[256,1024]{1,0:T(8,128)}, u32[]{:S(2)}, u32[]{:S(2)}) collective-permute-start(f32[256,1024]{1,0:T(8,128)} %pad_maximum_fusion.8), channel_id=1, source_target_pairs={{0,4},{1,3},{2,6},{3,1},{4,0},{5,7},{6,2},{7,5},{8,12},{9,11},{10,... | collective-permute-start | bytes 3145736 | tf_op jit(solution)/shard_map/ppermute | solution.py:77
  104.3 26.4 %collective-permute-start.6 = (f32[4,2,64,1024]{3,2,1,0:T(8,128)}, f32[4,2,64,1024]{3,2,1,0:T(8,128)}, u32[]{:S(2)}, u32[]{:S(2)}) collective-permute-start(f32[4,2,64,1024]{3,2,1,0:T(8,128)} %bitcast_select_fusion.2), channel_id=1, source_target_pairs={{0,2},{1,5},{2,0},{3,7},{4,6},{5,1},{6,4},{7,3},{8,10},{9,13},{10,... | collective-permute-start | bytes 6291464 | tf_op jit(solution)/shard_map/ppermute | solution.py:77
  107.6 29.7 %collective-permute-start.12 = (f32[512,1024]{1,0:T(8,128)}, f32[512,1024]{1,0:T(8,128)}, u32[]{:S(2)}, u32[]{:S(2)}) collective-permute-start(f32[512,1024]{1,0:T(8,128)} %pad_maximum_fusion.6), channel_id=1, source_target_pairs={{0,1},{1,0},{2,3},{3,2},{4,5},{5,4},{6,7},{7,6},{8,9},{9,8},{10,11... | collective-permute-start | bytes 6291464 | tf_op jit(solution)/shard_map/ppermute | solution.py:70
  109.6 169.1 %collective-permute-start.4 = (f32[1024,768]{1,0:T(8,128)}, f32[1024,768]{1,0:T(8,128)}, u32[]{:S(2)}, u32[]{:S(2)}) collective-permute-start(f32[1024,768]{1,0:T(8,128)} %maximum_convert_fusion.1), channel_id=1, source_target_pairs={{0,1},{1,0},{2,3},{3,2},{4,5},{5,4},{6,7},{7,6},{8,9},{9,8},{10,11... | collective-permute-start | bytes 9437192 | tf_op jit(solution)/shard_map/ppermute | solution.py:70
  114.5 188.1 %collective-permute-start.3 = (f32[4,640,512]{1,2,0:T(8,128)}, f32[4,640,512]{1,2,0:T(8,128)}, u32[]{:S(2)}, u32[]{:S(2)}) collective-permute-start(f32[4,640,512]{1,2,0:T(8,128)} %maximum_convert_fusion), channel_id=1, source_target_pairs={{0,1},{1,0},{2,3},{3,2},{4,5},{5,4},{6,7},{7,6},{8,9},{9,8},{10,11... | collective-permute-start | bytes 15728648 | tf_op jit(solution)/shard_map/ppermute | solution.py:70
  135.7 74.8 %collective-permute-start.7 = (f32[4,64,1024]{2,1,0:T(8,128)S(1)}, f32[4,64,1024]{2,1,0:T(8,128)}, u32[]{:S(2)}, u32[]{:S(2)}) collective-permute-start(f32[4,64,1024]{2,1,0:T(8,128)S(1)} %dynamic-slice_bitcast_fusion.1), channel_id=1, source_target_pairs={{0,4},{1,3},{2,6},{3,1},{4,0},{5,7},{6,2},{7,5},{8,12},{9,11},{10,... | collective-permute-start | bytes 3145736 | tf_op jit(solution)/shard_map/ppermute | solution.py:77
  162.2 7.8 %copy-start.25 = (f32[1024,512]{0,1:T(8,128)S(1)}, f32[1024,512]{0,1:T(8,128)}, u32[]{:S(2)}) copy-start(f32[1024,512]{0,1:T(8,128)} %fusion.70) | copy-start | bytes 6291460
  209.0 88.3 %collective-permute-start.16 = (f32[1,2,256,1024]{3,2,1,0:T(8,128)}, f32[1,2,256,1024]{3,2,1,0:T(8,128)}, u32[]{:S(2)}, u32[]{:S(2)}) collective-permute-start(f32[1,2,256,1024]{3,2,1,0:T(8,128)} %bitcast_select_fusion), channel_id=1, source_target_pairs={{0,8},{1,17},{2,10},{3,19},{4,12},{5,21},{6,14},{7,23},{8,0},{9,25... | collective-permute-start | bytes 6291464 | tf_op jit(solution)/shard_map/ppermute | solution.py:77
  212.3 55.6 %collective-permute-start.8 = (f32[1,2,64,1024]{3,2,1,0:T(8,128)S(1)}, f32[1,2,64,1024]{3,2,1,0:T(8,128)}, u32[]{:S(2)}, u32[]{:S(2)}) collective-permute-start(f32[1,2,64,1024]{3,2,1,0:T(8,128)S(1)} %bitcast_select_fusion.4), channel_id=1, source_target_pairs={{0,8},{1,17},{2,10},{3,19},{4,12},{5,21},{6,14},{7,23},{8,0},{9,25... | collective-permute-start | bytes 1572872 | tf_op jit(solution)/shard_map/ppermute | solution.py:77
  213.7 63.3 %collective-permute-start.5 = (f32[4,64,256]{2,1,0:T(8,128)}, f32[4,64,256]{2,1,0:T(8,128)}, u32[]{:S(2)}, u32[]{:S(2)}) collective-permute-start(f32[4,64,256]{2,1,0:T(8,128)} %convert_element_type.131), channel_id=1, source_target_pairs={{0,1},{1,0},{2,3},{3,2},{4,5},{5,4},{6,7},{7,6},{8,9},{9,8},{10,11... | collective-permute-start | bytes 786440 | tf_op jit(solution)/shard_map/ppermute | solution.py:70
  269.0 27.5 %collective-permute-start.9 = (f32[1,64,1024]{2,1,0:T(8,128)S(1)}, f32[1,64,1024]{2,1,0:T(8,128)S(1)}, u32[]{:S(2)}, u32[]{:S(2)}) collective-permute-start(f32[1,64,1024]{2,1,0:T(8,128)S(1)} %dynamic-slice_bitcast_fusion.9), channel_id=1, source_target_pairs={{0,16},{1,9},{2,18},{3,11},{4,20},{5,13},{6,22},{7,15},{8,24},{9,1... | collective-permute-start | bytes 786440 | tf_op jit(solution)/shard_map/ppermute | solution.py:77
  302.2 55.2 %collective-permute-start.17 = (f32[1,256,1024]{2,1,0:T(8,128)S(1)}, f32[1,256,1024]{2,1,0:T(8,128)}, u32[]{:S(2)}, u32[]{:S(2)}) collective-permute-start(f32[1,256,1024]{2,1,0:T(8,128)S(1)} %dynamic-slice_bitcast_fusion), channel_id=1, source_target_pairs={{0,16},{1,9},{2,18},{3,11},{4,20},{5,13},{6,22},{7,15},{8,24},{9,1... | collective-permute-start | bytes 3145736 | tf_op jit(solution)/shard_map/ppermute | solution.py:77
  315.9 6.9 %copy-start.4 = (bf16[4,64,1024]{2,1,0:T(8,128)(2,1)S(1)}, bf16[4,64,1024]{2,1,0:T(8,128)(2,1)}, u32[]{:S(2)}) copy-start(bf16[4,64,1024]{2,1,0:T(8,128)(2,1)} %param.18) | copy-start | bytes 1572868
  315.9 6.9 %copy-start.6 = (bf16[2560,512]{1,0:T(8,128)(2,1)S(1)}, bf16[2560,512]{1,0:T(8,128)(2,1)}, u32[]{:S(2)}) copy-start(bf16[2560,512]{1,0:T(8,128)(2,1)} %narrow.5) | copy-start | bytes 7864324
  315.9 6.9 %copy-start.12 = (bf16[4,640,256]{2,1,0:T(8,128)(2,1)S(1)}, bf16[4,640,256]{2,1,0:T(8,128)(2,1)}, u32[]{:S(2)}) copy-start(bf16[4,640,256]{2,1,0:T(8,128)(2,1)} %copy.110) | copy-start | bytes 3932164
  315.9 6.9 %copy-start.13 = (bf16[4,640,256]{2,1,0:T(8,128)(2,1)S(1)}, bf16[4,640,256]{2,1,0:T(8,128)(2,1)}, u32[]{:S(2)}) copy-start(bf16[4,640,256]{2,1,0:T(8,128)(2,1)} %copy.111) | copy-start | bytes 3932164
  315.9 6.9 %copy-start.32 = (bf16[1024,512]{1,0:T(8,128)(2,1)S(1)}, bf16[1024,512]{1,0:T(8,128)(2,1)}, u32[]{:S(2)}) copy-start(bf16[1024,512]{1,0:T(8,128)(2,1)} %slice.79) | copy-start | bytes 3145732
  315.9 6.9 %copy-start.37 = (bf16[1024,256]{1,0:T(8,128)(2,1)S(1)}, bf16[1024,256]{1,0:T(8,128)(2,1)}, u32[]{:S(2)}) copy-start(bf16[1024,256]{1,0:T(8,128)(2,1)} %param.22) | copy-start | bytes 1572868
  315.9 6.9 %copy-start.40 = (bf16[1024,256]{1,0:T(8,128)(2,1)S(1)}, bf16[1024,256]{1,0:T(8,128)(2,1)}, u32[]{:S(2)}) copy-start(bf16[1024,256]{1,0:T(8,128)(2,1)} %param.21) | copy-start | bytes 1572868
  315.9 6.9 %copy-start.48 = (f32[4,64]{1,0:T(4,128)S(1)}, f32[4,64]{1,0:T(4,128)}, u32[]{:S(2)}) copy-start(f32[4,64]{1,0:T(4,128)} %copy-done.47) | copy-start | bytes 3076
  315.9 6.9 %copy-start.50 = (f32[4,64]{1,0:T(4,128)S(1)}, f32[4,64]{1,0:T(4,128)}, u32[]{:S(2)}) copy-start(f32[4,64]{1,0:T(4,128)} %copy-done.49) | copy-start | bytes 3076
  315.9 6.9 %copy-start.54 = (f32[1024]{0:T(1024)S(1)}, f32[1024]{0:T(1024)}, u32[]{:S(2)}) copy-start(f32[1024]{0:T(1024)} %param.28) | copy-start | bytes 12292
  315.9 6.9 %copy-start.61 = (f32[4,64,1024]{2,1,0:T(8,128)S(1)}, f32[4,64,1024]{2,1,0:T(8,128)}, u32[]{:S(2)}) copy-start(f32[4,64,1024]{2,1,0:T(8,128)} %fusion.62) | copy-start | bytes 3145732
  337.0 9.4 %collective-permute-start.21 = (f32[4,2,6,64]{3,1,0,2:T(2,128)S(1)}, f32[4,2,6,64]{3,1,0,2:T(2,128)S(1)}, u32[]{:S(2)}, u32[]{:S(2)}) collective-permute-start(f32[4,2,6,64]{3,1,0,2:T(2,128)S(1)} %bitcast_select_fusion.6), channel_id=1, source_target_pairs={{0,2},{1,5},{2,0},{3,7},{4,6},{5,1},{6,4},{7,3},{8,10},{9,13},{10,... | collective-permute-start | bytes 36872 | tf_op jit(solution)/shard_map/ppermute | solution.py:77
  337.3 15.6 %copy-start.31 = (f32[4,64,1024]{2,1,0:T(8,128)S(1)}, f32[4,64,1024]{2,1,0:T(8,128)}, u32[]{:S(2)}) copy-start(f32[4,64,1024]{2,1,0:T(8,128)} %get-tuple-element.76) | copy-start | bytes 3145732
  346.4 11.1 %copy-start.9 = (f32[1,2,256,1024]{3,2,1,0:T(8,128)S(1)}, f32[1,2,256,1024]{3,2,1,0:T(8,128)}, u32[]{:S(2)}) copy-start(f32[1,2,256,1024]{3,2,1,0:T(8,128)} %copy-done.8) | copy-start | bytes 6291460
  346.4 3.8 %collective-permute-start.22 = (f32[4,6,64]{2,0,1:T(4,128)S(1)}, f32[4,6,64]{2,0,1:T(4,128)S(1)}, u32[]{:S(2)}, u32[]{:S(2)}) collective-permute-start(f32[4,6,64]{2,0,1:T(4,128)S(1)} %bitcast.255), channel_id=1, source_target_pairs={{0,4},{1,3},{2,6},{3,1},{4,0},{5,7},{6,2},{7,5},{8,12},{9,11},{10,... | collective-permute-start | bytes 18440 | tf_op jit(solution)/shard_map/ppermute | solution.py:77
  350.3 4.3 %collective-permute-start.23 = (f32[1,2,6,64]{3,1,2,0:T(2,128)S(1)}, f32[1,2,6,64]{3,1,2,0:T(2,128)S(1)}, u32[]{:S(2)}, u32[]{:S(2)}) collective-permute-start(f32[1,2,6,64]{3,1,2,0:T(2,128)S(1)} %fusion.109), channel_id=1, source_target_pairs={{0,8},{1,17},{2,10},{3,19},{4,12},{5,21},{6,14},{7,23},{8,0},{9,25... | collective-permute-start | bytes 9224 | tf_op jit(solution)/shard_map/ppermute | solution.py:77
  354.5 8.0 %collective-permute-start.24 = (f32[1,6,64]{2,0,1:T(1,128)S(1)}, f32[1,6,64]{2,0,1:T(1,128)S(1)}, u32[]{:S(2)}, u32[]{:S(2)}) collective-permute-start(f32[1,6,64]{2,0,1:T(1,128)S(1)} %fusion.115), channel_id=1, source_target_pairs={{0,16},{1,9},{2,18},{3,11},{4,20},{5,13},{6,22},{7,15},{8,24},{9,1... | collective-permute-start | bytes 4616 | tf_op jit(solution)/shard_map/ppermute | solution.py:77
  359.0 7.4 %collective-permute-start.20 = (f32[64,1024]{1,0:T(8,128)S(1)}, f32[64,1024]{1,0:T(8,128)S(1)}, u32[]{:S(2)}, u32[]{:S(2)}) collective-permute-start(f32[64,1024]{1,0:T(8,128)S(1)} %get-tuple-element.41), channel_id=1, source_target_pairs={{0,6},{1,7},{2,4},{3,5},{4,2},{5,3},{6,0},{7,1},{8,14},{9,15},{10,... | collective-permute-start | bytes 786440 | tf_op jit(solution)/shard_map/ppermute | solution.py:77
  360.5 8.6 %collective-permute-start.19 = (f32[64,1024]{1,0:T(8,128)S(1)}, f32[64,1024]{1,0:T(8,128)S(1)}, u32[]{:S(2)}, u32[]{:S(2)}) collective-permute-start(f32[64,1024]{1,0:T(8,128)S(1)} %get-tuple-element.42), channel_id=1, source_target_pairs={{0,4},{1,5},{2,6},{3,7},{4,0},{5,1},{6,2},{7,3},{8,12},{9,13},{10,... | collective-permute-start | bytes 786440 | tf_op jit(solution)/shard_map/ppermute | solution.py:77
  362.1 7.1 %collective-permute-start.18 = (f32[64,1024]{1,0:T(8,128)S(1)}, f32[64,1024]{1,0:T(8,128)S(1)}, u32[]{:S(2)}, u32[]{:S(2)}) collective-permute-start(f32[64,1024]{1,0:T(8,128)S(1)} %get-tuple-element.43), channel_id=1, source_target_pairs={{0,2},{1,3},{2,0},{3,1},{4,6},{5,7},{6,4},{7,5},{8,10},{9,11},{10,... | collective-permute-start | bytes 786440 | tf_op jit(solution)/shard_map/ppermute | solution.py:77
  (42 other events, 109.1 us)

commit v2 on v1

v2 whole, which is shorter than its diff:
```python
import functools

import jax
import jax.numpy as jnp
from jax import lax
from jax.experimental import pallas as pl
from jax.experimental.pallas import tpu as pltpu
from jax.sharding import PartitionSpec as P

HEAD = 64
PATCH = 576
SHORT = 256
GROUP = 4
LANES = 128
EPSILON = 1e-05
SINGLE = jnp.float32
HALF = jnp.bfloat16


def dot(left, right, left_axis=1, right_axis=0):
    return lax.dot_general(
        left, right, (((left_axis,), (right_axis,)), ((), ())), preferred_element_type=SINGLE
    )


def moments(values):
    mean = jnp.mean(values, -1, keepdims=True)
    center = values - mean
    inverse = lax.rsqrt(jnp.mean(center * center, -1, keepdims=True) + EPSILON)
    return mean, center, inverse


def norm_back(upstream, normed, inverse, gain):
    product = upstream * normed
    scaled = upstream * gain
    shift = jnp.mean(scaled, -1, keepdims=True)
    slope = jnp.mean(product * gain, -1, keepdims=True)
    return inverse * (scaled - shift - normed * slope), product


def row_sums(values):
    count, width = values.shape
    return jnp.sum(values.reshape(count // 8, 8, width), axis=0)


def head_rows(array, heads):
    column = lax.broadcasted_iota(jnp.int32, array.shape, 1) // HEAD
    return jnp.concatenate([jnp.where(column == h, array, 0) for h in range(heads)], 0)


def head_merge(blocks, heads):
    rows = blocks.shape[0] // heads
    total = None
    for h in range(heads):
        part = blocks[h * rows : (h + 1) * rows]
        column = lax.broadcasted_iota(jnp.int32, part.shape, 1) // HEAD
        part = jnp.where(column == h, part, 0)
        total = part if total is None else total + part
    return total


def exact_gelu(values):
    below = 0.5 * (1.0 + lax.erf(values * (0.5**0.5)))
    density = jnp.exp(values * values * -0.5) * 0.3989422804014327
    return values * below, below + values * density


def call(body, name, grid, ins, outs, scratch=(), prefetch=(), flops=0, cost=None):
    moved = sum(a.size * a.dtype.itemsize for a, _ in ins)
    shapes = [jax.ShapeDtypeStruct(s, d) for s, d, _ in outs]
    moved += sum(s.size * s.dtype.itemsize for s in shapes)
    return pl.pallas_call(
        body,
        out_shape=shapes,
        grid_spec=pltpu.PrefetchScalarGridSpec(
            num_scalar_prefetch=len(prefetch),
            grid=grid,
            in_specs=[s for _, s in ins],
            out_specs=[s for _, _, s in outs],
            scratch_shapes=list(scratch),
        ),
        cost_estimate=pl.CostEstimate(flops=flops, bytes_accessed=moved, transcendentals=0),
        name=name,
    )(*prefetch, *[a for a, _ in ins])


def whole(array):
    zeros = (0,) * array.ndim
    return array, pl.BlockSpec(array.shape, lambda *at: zeros)


def by_image(shape):
    rest = (0,) * (len(shape) - 1)
    return pl.BlockSpec((1,) + tuple(shape[1:]), lambda at, *_: (at,) + rest)


def by_rows(rows, width):
    return pl.BlockSpec((rows, width), lambda at, *_: (at, 0))


def attend_body(
    buckets_ref, media_ref, latent_ref, wq_ref, wk_ref, wv_ref, wo_ref,
    mg_ref, mb_ref, lg_ref, lb_ref,
    kv_ref, q_ref, k_ref, v_ref, p_ref, att_ref, branch_ref, mean_ref, inv_ref,
):
    patches = media_ref.shape[1]
    latent_rows = latent_ref.shape[1]
    inner = wq_ref.shape[1]
    heads = inner // HEAD
    chunk = patches // 3
    for at in range(3):
        rows = slice(at * chunk, (at + 1) * chunk)
        mean, center, inverse = moments(media_ref[0, rows].astype(SINGLE))
        mean_ref[0, rows] = mean
        inv_ref[0, rows] = inverse
        low = (center * inverse * mg_ref[...] + mb_ref[...]).astype(HALF)
        kv_ref[0, rows] = low
        k_ref[0, rows] = dot(low, wk_ref[...]).astype(HALF)
        v_ref[0, rows] = dot(low, wv_ref[...]).astype(HALF)
    rows = slice(patches, patches + latent_rows)
    _, center, inverse = moments(latent_ref[0].astype(SINGLE))
    low = (center * inverse * lg_ref[...] + lb_ref[...]).astype(HALF)
    kv_ref[0, rows] = low
    k_ref[0, rows] = dot(low, wk_ref[...]).astype(HALF)
    v_ref[0, rows] = dot(low, wv_ref[...]).astype(HALF)
    query = dot(low, wq_ref[...]).astype(HALF)
    q_ref[0] = query
    spread = head_rows(query * HALF(HEAD**-0.5), heads)
    scores = dot(spread, k_ref[0], 1, 1)
    count = SHORT + (PATCH - SHORT) * buckets_ref[pl.program_id(0)]
    column = lax.broadcasted_iota(jnp.int32, scores.shape, 1)
    scores = jnp.where((column < count) | (column >= patches), scores, -1e30)
    shifted = jnp.exp(scores - jnp.max(scores, -1, keepdims=True))
    probs = shifted / jnp.sum(shifted, -1, keepdims=True)
    p_ref[0] = probs
    attended = head_merge(dot(probs.astype(HALF), v_ref[0]), heads).astype(HALF)
    att_ref[0] = attended
    branch_ref[0] = dot(attended, wo_ref[...])


def attend(buckets, media, latents, wq, wk, wv, wo, vectors):
    images, patches, width = media.shape
    latent_rows = latents.shape[1]
    inner = wq.shape[1]
    keys_all = patches + latent_rows
    heads = inner // HEAD
    outs = [
        ((images, keys_all, width), HALF),
        ((images, latent_rows, inner), HALF),
        ((images, keys_all, inner), HALF),
        ((images, keys_all, inner), HALF),
        ((images, heads * latent_rows, keys_all), SINGLE),
        ((images, latent_rows, inner), HALF),
        ((images, latent_rows, width), SINGLE),
        ((images, patches, 1), SINGLE),
        ((images, patches, 1), SINGLE),
    ]
    return call(
        attend_body,
        "attend",
        (images,),
        [(media, by_image(media.shape)), (latents, by_image(latents.shape))]
        + [whole(a) for a in (wq, wk, wv, wo) + tuple(vectors)],
        [(s, d, by_image(s)) for s, d in outs],
        prefetch=(buckets,),
        flops=images * keys_all * width * inner * 5,
    )


def middle_body(core_ref, latent_ref, own_ref, far_ref, gain_ref, bias_ref, mid_ref, low_ref, send_ref):
    middle = latent_ref[...].astype(SINGLE) + (own_ref[...] + far_ref[...])
    mid_ref[...] = middle
    _, center, inverse = moments(middle)
    low = (center * inverse * gain_ref[...] + bias_ref[...]).astype(HALF)
    low_ref[...] = low
    half = low.shape[0] // 2

    @pl.when(core_ref[0] == 0)
    def _():
        send_ref[...] = low[:half].astype(SINGLE)

    @pl.when(core_ref[0] == 1)
    def _():
        send_ref[...] = low[half:].astype(SINGLE)


def feed_body(low_ref, cot_ref, up_ref, down_ref, hidden_ref, part_ref):
    half = up_ref.shape[1] // 2
    total = None
    for at in range(2):
        cols = slice(at * half, (at + 1) * half)
        value, slope = exact_gelu(dot(low_ref[...], up_ref[:, cols]))
        hidden_ref[:, cols] = value.astype(HALF)
        grad = (slope * dot(cot_ref[...], down_ref[cols], 1, 1)).astype(HALF)
        piece = dot(grad, up_ref[:, cols], 1, 1)
        total = piece if total is None else total + piece

    @pl.when(pl.program_id(0) == 0)
    def _():
        part_ref[...] = total

    @pl.when(pl.program_id(0) > 0)
    def _():
        part_ref[...] += total


def feed(low, cot, up, down):
    rows, width = low.shape
    hidden = up.shape[1]
    block = 512
    return call(
        feed_body,
        "feed",
        (hidden // block,),
        [
            whole(low),
            whole(cot),
            (up, pl.BlockSpec((width, block), lambda at: (0, at))),
            (down, pl.BlockSpec((block, width), lambda at: (at, 0))),
        ],
        [
            ((rows, hidden), HALF, pl.BlockSpec((rows, block), lambda at: (0, at))),
            ((rows, width), SINGLE, pl.BlockSpec((rows, width), lambda at: (0, 0))),
        ],
        flops=6 * rows * width * hidden,
    )


def wide_body(member_ref, *refs):
    feeds, cots = refs[0:4], refs[4:8]
    up_ref, down_ref = refs[8:10]
    fl_ref, cl_ref, hid_ref, gp_ref = refs[10:14]
    fbuf, cbuf, sems = refs[14:]
    rows = fbuf.shape[1]
    copies = []
    for at in range(4):
        first = pltpu.make_async_copy(feeds[at], fbuf.at[at], sems.at[0, at])
        second = pltpu.make_async_copy(cots[at], cbuf.at[at], sems.at[1, at])
        first.start()
        second.start()
        copies.append((first, second))
    for at in range(4):
        here = slice(at * rows, (at + 1) * rows)
        copies[at][0].wait()
        low = fbuf[at].astype(HALF)
        fl_ref[here] = low
        value, slope = exact_gelu(dot(low, up_ref[...]))
        hid_ref[here] = value.astype(HALF)
        copies[at][1].wait()
        low = cbuf[at].astype(HALF)
        cl_ref[here] = low
        gp_ref[here] = (slope * dot(low, down_ref[...], 1, 1)).astype(HALF)


def wide(member, feeds, cots, up, down):
    rows, width = feeds[0].shape
    piece = up.shape[1] // GROUP
    every = pl.BlockSpec(memory_space=pl.ANY)
    outs = [((4 * rows, width), HALF)] * 2 + [((4 * rows, piece), HALF)] * 2
    return call(
        wide_body,
        "wide",
        (1,),
        [(a, every) for a in feeds + cots]
        + [
            (up, pl.BlockSpec((width, piece), lambda at, m: (0, m[0]))),
            (down, pl.BlockSpec((piece, width), lambda at, m: (m[0], 0))),
        ],
        [(s, d, pl.BlockSpec(s, lambda at, m: (0, 0))) for s, d in outs],
        scratch=[
            pltpu.VMEM((4, rows, width), SINGLE),
            pltpu.VMEM((4, rows, width), SINGLE),
            pltpu.SemaphoreType.DMA((2, 4)),
        ],
        prefetch=(member,),
        flops=4 * 4 * rows * width * piece,
    )


def wide_grad_body(order_ref, place_ref, fl_ref, cl_ref, hid_ref, gp_ref, out_ref):
    share = out_ref.shape[1]
    piece = gp_ref.shape[1]
    block = order_ref[pl.program_id(0)]
    up = dot(fl_ref[...], gp_ref[...], 0, 0)
    down = dot(cl_ref[...], hid_ref[...], 0, 0)
    per = LANES // share
    for at in range(per):
        rows = slice(at * share, (at + 1) * share)
        spot = place_ref[block * per + at]
        out_ref[spot, :, :piece] = up[rows]
        out_ref[spot, :, piece:] = down[rows]


def wide_grad(order, place, fl, cl, hid, gp, devices):
    rows, width = fl.shape
    piece = gp.shape[1]
    blocks = order.shape[0]
    share = width // devices
    count = blocks * LANES // share
    column = pl.BlockSpec((rows, LANES), lambda at, o, p: (0, o[at]))
    shape = (count, share, 2 * piece)
    return call(
        wide_grad_body,
        "wide_grad",
        (blocks,),
        [(fl, column), (cl, column), whole(hid), whole(gp)],
        [(shape, SINGLE, pl.BlockSpec(shape, lambda at, o, p: (0, 0, 0)))],
        prefetch=(order, place),
        flops=4 * rows * blocks * LANES * piece,
    )[0]


def back_body(
    mid_ref, own_ref, far_ref, cot_ref, gain_ref, wo_ref, q_ref, k_ref, v_ref, p_ref,
    gm_ref, gb_ref, gkv_ref, gkv_send_ref, gq_ref, gq_send_ref, vec_ref,
):
    inner = wo_ref.shape[0]
    heads = inner // HEAD
    upstream = own_ref[...] + far_ref[...]
    _, center, inverse = moments(mid_ref[...])
    moved, product = norm_back(upstream, center * inverse, inverse, gain_ref[...])
    grad_middle = cot_ref[...].astype(SINGLE) + moved
    gm_ref[...] = grad_middle
    branch = grad_middle.astype(HALF)
    gb_ref[...] = branch
    sums = (row_sums(product), row_sums(upstream))

    @pl.when(pl.program_id(0) == 0)
    def _():
        vec_ref[0], vec_ref[1] = sums

    @pl.when(pl.program_id(0) > 0)
    def _():
        vec_ref[0] += sums[0]
        vec_ref[1] += sums[1]

    attended = head_rows(dot(branch, wo_ref[...], 1, 1).astype(HALF), heads)
    query = head_rows(q_ref[0] * HALF(HEAD**-0.5), heads)
    probs = p_ref[0]
    grad_probs = dot(attended, v_ref[0], 1, 1)
    inside = jnp.sum(probs * grad_probs, -1, keepdims=True)
    scores = (probs * (grad_probs - inside)).astype(HALF)
    grad_query = (head_merge(dot(scores, k_ref[0]), heads) * HEAD**-0.5).astype(HALF)
    gq_ref[0] = grad_query
    gq_send_ref[0] = grad_query.astype(SINGLE)
    grad_key = dot(scores, query, 0, 0).astype(HALF)
    gkv_ref[0, :, :inner] = grad_key
    gkv_send_ref[0, :, :inner] = grad_key.astype(SINGLE)
    grad_value = dot(probs.astype(HALF), attended, 0, 0).astype(HALF)
    gkv_ref[0, :, inner:] = grad_value
    gkv_send_ref[0, :, inner:] = grad_value.astype(SINGLE)


def back(middle, own, far, cot, gain, wo, q, k, v, p):
    images, latent_rows, inner = q.shape
    keys_all = k.shape[1]
    rows, width = middle.shape
    line = by_rows(latent_rows, width)
    outs = [
        ((rows, width), SINGLE, line),
        ((rows, width), HALF, line),
        ((images, keys_all, 2 * inner), HALF, by_image((images, keys_all, 2 * inner))),
        ((images, keys_all, 2 * inner), SINGLE, by_image((images, keys_all, 2 * inner))),
        ((images, latent_rows, inner), HALF, by_image(q.shape)),
        ((images, latent_rows, inner), SINGLE, by_image(q.shape)),
        ((2, 8, width), SINGLE, pl.BlockSpec((2, 8, width), lambda at: (0, 0, 0))),
    ]
    return call(
        back_body,
        "back",
        (images,),
        [(a, line) for a in (middle, own, far, cot)]
        + [whole(gain), whole(wo)]
        + [(a, by_image(a.shape)) for a in (q, k, v, p)],
        outs,
        flops=images * 10 * q.shape[1] * 4 * keys_all * inner,
    )


def small_grad_body(place_ref, kv_ref, gb_ref, gkv_ref, gq_ref, att_ref, send_ref, keep_ref, *, images, patches):
    share = send_ref.shape[1]
    inner = att_ref.shape[1]
    held = send_ref.shape[0]
    per = LANES // share
    keys_all = kv_ref.shape[0] // images
    latent = jnp.concatenate(
        [kv_ref[i * keys_all + patches : (i + 1) * keys_all] for i in range(images)], 0
    )
    pair = dot(kv_ref[...], gkv_ref[...], 0, 0)
    query = dot(latent, gq_ref[...], 0, 0)
    output = dot(gb_ref[...], att_ref[...], 0, 0)
    for at in range(per):
        rows = slice(at * share, (at + 1) * share)
        spot = place_ref[pl.program_id(0) * per + at]

        @pl.when(spot < held)
        def _():
            send_ref[spot, :, : 2 * inner] = pair[rows]
            send_ref[spot, :, 2 * inner : 3 * inner] = query[rows]
            send_ref[spot, :, 3 * inner :] = output[rows]

        @pl.when(spot >= held)
        def _():
            keep_ref[spot - held, :, : 2 * inner] = pair[rows]
            keep_ref[spot - held, :, 2 * inner : 3 * inner] = query[rows]
            keep_ref[spot - held, :, 3 * inner :] = output[rows]


def small_grad(place, kv, gb, gkv, gq, att, devices, images, patches):
    rows, width = kv.shape
    inner = att.shape[1]
    shape = (devices // 2, width // devices, 4 * inner)
    spec = pl.BlockSpec(shape, lambda at, p: (0, 0, 0))
    return call(
        functools.partial(small_grad_body, images=images, patches=patches),
        "small_grad",
        (width // LANES,),
        [
            (kv, pl.BlockSpec((rows, LANES), lambda at, p: (0, at))),
            (gb, pl.BlockSpec((gb.shape[0], LANES), lambda at, p: (0, at))),
        ]
        + [whole(a) for a in (gkv, gq, att)],
        [(shape, SINGLE, spec), (shape, SINGLE, spec)],
        prefetch=(place,),
        flops=4 * rows * width * inner,
    )


def inputs_body(
    gkv_ref, gkv_far_ref, gq_ref, gq_far_ref, media_ref, mean_ref, inv_ref, latent_ref, gm_ref,
    wq_ref, wk_ref, wv_ref, far_ref, mg_ref, lg_ref,
    out_ref, late_ref, vec_ref, heads_ref, query_ref,
):
    inner = wq_ref.shape[1]
    patches = media_ref.shape[1]

    @pl.when(pl.program_id(0) == 0)
    def _():
        heads_ref[:, :inner] = wk_ref[...]
        heads_ref[:, inner : 2 * inner] = wv_ref[...]
        heads_ref[:, 2 * inner :] = far_ref[:, inner:].astype(HALF)
        query_ref[:, :inner] = wq_ref[...]
        query_ref[:, inner:] = far_ref[:, :inner].astype(HALF)
        vec_ref[...] = jnp.zeros_like(vec_ref)

    chunk = patches // 3
    for at in range(3):
        rows = slice(at * chunk, (at + 1) * chunk)
        left = jnp.concatenate([gkv_ref[0, rows], gkv_far_ref[0, rows].astype(HALF)], 1)
        upstream = dot(left, heads_ref[...], 1, 1)
        inverse = inv_ref[0, rows]
        normed = (media_ref[0, rows].astype(SINGLE) - mean_ref[0, rows]) * inverse
        moved, product = norm_back(upstream, normed, inverse, mg_ref[...])
        out_ref[0, rows] = moved.astype(HALF)
        vec_ref[0] += row_sums(product)
        vec_ref[1] += row_sums(upstream)
    left = jnp.concatenate([gkv_ref[0, patches:], gkv_far_ref[0, patches:].astype(HALF)], 1)
    upstream = dot(left, heads_ref[...], 1, 1)
    left = jnp.concatenate([gq_ref[0], gq_far_ref[0].astype(HALF)], 1)
    upstream += dot(left, query_ref[...], 1, 1)
    _, center, inverse = moments(latent_ref[0].astype(SINGLE))
    moved, product = norm_back(upstream, center * inverse, inverse, lg_ref[...])
    late_ref[0] = (gm_ref[0] + moved).astype(HALF)
    vec_ref[2] += row_sums(product)
    vec_ref[3] += row_sums(upstream)


def inputs_back(gkv, gkv_far, gq, gq_far, media, mean, inv, latents, gm, wq, wk, wv, far, mg, lg):
    images, patches, width = media.shape
    inner = wq.shape[1]
    vec = (4, 8, width)
    return call(
        inputs_body,
        "inputs_back",
        (images,),
        [(a, by_image(a.shape)) for a in (gkv, gkv_far, gq, gq_far, media, mean, inv, latents, gm)]
        + [whole(a) for a in (wq, wk, wv, far, mg, lg)],
        [
            (media.shape, HALF, by_image(media.shape)),
            (latents.shape, HALF, by_image(latents.shape)),
            (vec, SINGLE, pl.BlockSpec(vec, lambda at: (0, 0, 0))),
        ],
        scratch=[pltpu.VMEM((width, 4 * inner), HALF), pltpu.VMEM((width, 2 * inner), HALF)],
        flops=8 * images * patches * width * inner,
    )


def place_body(member_ref, *refs):
    blocks, (up_ref, down_ref) = refs[:GROUP], refs[GROUP:]
    piece = blocks[0].shape[1] // 2
    for step in range(GROUP):
        spot = member_ref[0] ^ step
        up_ref[:, pl.ds(pl.multiple_of(spot * piece, piece), piece)] = blocks[step][:, :piece]
        down_ref[pl.ds(pl.multiple_of(spot * piece, piece), piece), :] = blocks[step][:, piece:].T


def place_pieces(member, blocks):
    share, both = blocks[0].shape
    wide_ = both // 2 * GROUP
    return call(
        place_body,
        "place_pieces",
        (1,),
        [whole(b) for b in blocks],
        [
            ((share, wide_), SINGLE, pl.BlockSpec((share, wide_), lambda at, m: (0, 0))),
            ((wide_, share), SINGLE, pl.BlockSpec((wide_, share), lambda at, m: (0, 0))),
        ],
        prefetch=(member,),
    )


class Links:
    def __init__(self, devices):
        self.devices = devices
        self.bits = devices.bit_length() - 1
        self.row = lax.axis_index("dp")
        self.core = lax.axis_index("tensor")

    def swap(self, array):
        return lax.ppermute(array, "tensor", [(0, 1), (1, 0)])

    def send(self, array, step_zero, step_one):
        pairs = []
        for row in range(self.devices):
            pairs.append((2 * row, 2 * (row ^ step_zero)))
            pairs.append((2 * row + 1, 2 * (row ^ step_one) + 1))
        return lax.ppermute(array, ("dp", "tensor"), pairs)

    def places(self, orders, tail):
        apart = jnp.arange(self.devices, dtype=jnp.int32) ^ self.row
        found = []
        for order in orders:
            spot = jnp.zeros_like(apart)
            for which in order:
                spot = 2 * spot + 1 - ((apart >> which) & 1)
            found.append(spot * (1 << tail) + apart % (1 << tail))
        return jnp.where(self.core == 0, found[0], found[1])

    def reduce(self, leave, keep, orders):
        for step, (zero, one) in enumerate(zip(*orders)):
            come = self.send(leave, 1 << zero, 1 << one)
            if step == len(orders[0]) - 1:
                return keep + come
            half = keep.shape[0] // 2
            leave, keep = keep[:half] + come[:half], keep[half:] + come[half:]

    def gather(self, own):
        near = self.send(own, 1, 2)
        pair = jnp.concatenate([own, near], 0)
        far = self.send(pair, 2, 1)
        return [pair, far, self.swap(pair), self.swap(far)]

    def total(self, array):
        for at in range(self.bits):
            array = array + self.send(array, 1 << at, 1 << at)
        return array


def local(
    media, buckets, latents, cotangent, query_weight, key_weight, value_weight, output_weight,
    up_weight, down_weight, media_gain, media_bias, latent_gain, latent_bias, feed_gain, feed_bias,
    devices,
):
    links = Links(devices)
    images, patches, width = media.shape
    latent_rows = latents.shape[1]
    rows = images * latent_rows
    inner = query_weight.shape[1]
    keys_all = patches + latent_rows
    share = width // devices
    vectors = [v.reshape(1, width) for v in (media_gain, media_bias, latent_gain, latent_bias)]
    gain, bias = feed_gain.reshape(1, width), feed_bias.reshape(1, width)
    core = links.core.reshape(1)
    member = (links.row % GROUP).reshape(1)

    cot = cotangent.reshape(rows, width)
    half = rows // 2
    cots = links.gather(
        lax.dynamic_slice_in_dim(cot, links.core * half, half, 0).astype(SINGLE)
    )
    weights_far = links.swap(
        jnp.concatenate([query_weight, key_weight, value_weight], 1).astype(SINGLE)
    )
    kv, q, k, v, probs, attended, branch, mean, inv = attend(
        buckets, media, latents, query_weight, key_weight, value_weight, output_weight, vectors
    )
    branch = branch.reshape(rows, width)
    middle, low, low_send = call(
        middle_body,
        "middle",
        (1,),
        [whole(a) for a in (latents.reshape(rows, width), branch, links.swap(branch), gain, bias)],
        [
            ((rows, width), SINGLE, pl.BlockSpec((rows, width), lambda at, c: (0, 0))),
            ((rows, width), HALF, pl.BlockSpec((rows, width), lambda at, c: (0, 0))),
            ((half, width), SINGLE, pl.BlockSpec((half, width), lambda at, c: (0, 0))),
        ],
        prefetch=(core,),
    )
    feeds = links.gather(low_send)
    hidden, part = feed(low, cot, up_weight, down_weight)
    grad_middle, grad_branch, gkv, gkv_send, gq, gq_send, feed_vec = back(
        middle, part, links.swap(part), cot, gain, output_weight, q, k, v, probs
    )
    gkv_far, gq_far = links.swap(gkv_send), links.swap(gq_send)

    bits = links.bits
    orders = [list(range(bits)), [1, 0] + list(range(2, bits))]
    if bits >= 4:
        orders[1][2:4] = [3, 2]
    leave, keep = small_grad(
        links.places(orders, 0),
        kv.reshape(images * keys_all, width),
        grad_branch,
        gkv.reshape(images * keys_all, 2 * inner),
        gq.reshape(rows, inner),
        attended.reshape(rows, inner),
        devices,
        images,
        patches,
    )
    small = links.reduce(leave, keep, orders)[0]

    fl, cl, hid, gp = wide(member, feeds, cots, up_weight, down_weight)
    top = bits - 1
    rest = list(range(2, top - 1))
    orders = [[top, top - 1] + rest, [top - 1, top] + rest]
    place = links.places(orders, 2)
    which = jnp.where(links.core == 0, top, top - 1)
    mine = (links.row >> which) & 1
    held = width // LANES // 2
    at = which - (bits - held.bit_length())
    rank = jnp.arange(held, dtype=jnp.int32)
    order = ((rank >> at) << (at + 1)) + (rank & ((1 << at) - 1))
    count = devices // 2
    leave = wide_grad(order + ((1 - mine) << at), place % count, fl, cl, hid, gp, devices)
    keep = wide_grad(order + (mine << at), place % count, fl, cl, hid, gp, devices)
    mixed = links.reduce(leave, keep, orders)
    pieces = [mixed[0]] + [links.send(mixed[s], s, s) for s in range(1, GROUP)]
    grad_up, grad_down = place_pieces(member, pieces)

    grad_media, grad_latents, vec = inputs_back(
        gkv, gkv_far, gq, gq_far, media, mean, inv, latents,
        grad_middle.reshape(images, latent_rows, width),
        query_weight, key_weight, value_weight, weights_far, vectors[0], vectors[2],
    )
    vec = jnp.sum(jnp.concatenate([vec, feed_vec], 0), 1)
    vec = links.total(jnp.concatenate([vec, jnp.zeros((2, width), SINGLE)], 0))
    vec = lax.dynamic_slice_in_dim(vec, links.row * share, share, 1)

    feed_out = dot(hidden, down_weight)
    result = (middle + (feed_out + links.swap(feed_out))).astype(HALF)
    return (
        result.reshape(latents.shape),
        grad_media,
        grad_latents,
        small[:, 2 * inner : 3 * inner],
        small[:, :inner],
        small[:, inner : 2 * inner],
        small[:, 3 * inner :].T,
        grad_up,
        grad_down,
    ) + tuple(vec[at] for at in range(6))


def solution(mesh):
    devices = mesh.shape["dp"]
    images = P("dp", None, None)
    columns = P(None, "tensor")
    lines = P("tensor", None)

    def body(*args):
        return local(*args, devices=devices)

    return jax.shard_map(
        body,
        mesh=mesh,
        in_specs=(images, P("dp"), images, images)
        + (columns, columns, columns, lines, columns, lines)
        + (P(),) * 6,
        out_specs=(images,) * 3
        + (P("dp", "tensor"),) * 3
        + (P("tensor", "dp"), P("dp", "tensor"), P("tensor", "dp"))
        + (P("dp"),) * 6,
        check_vma=False,
    )
```

time: 378 us -> 227 us (0.60); the launches traced: 372 us -> 226 us
  matrix products: 83.7 us -> 2.25 us
  Pallas kernels: 21.3 us -> 93.7 us
  other arithmetic: 89.2 us -> 20.3 us
  local copies, waits for them, and re-layouts: 71.1 us -> 7.23 us
  waiting for transfers between devices: 78.4 us -> 66 us
  starting transfers between devices: 25.8 us -> 36 us
    dot_general x23 -> x1, matrix products: 81.3 us -> 2.25 us  [dot(): lax.dot_general(left, right, (((left_axis,), (right_axis,)), ((), ())), p...]
    pallas_call x5 -> x10, Pallas kernels: 21.3 us -> 93.7 us  [call(): pl.pallas_call(body, out_shape=shapes, grid_spec=pltpu.PrefetchScalarGrid...]
    dynamic_slice x11 -> x0, local copies, waits for them, and re-layouts: 36.2 us -> none  [the longest x10 36.1 us: pick(): return lax.dynamic_index_in_dim(array, index, axis, keepdims=False)]
    concatenate x8 -> x0, other arithmetic: 27.8 us -> none  [the longest x2 9.03 us: gather(): return jnp.concatenate([mine, self.swap(mine)], 0)]
    convert_element_type x9 -> x2, other arithmetic: 20.3 us -> 2.65 us  [the longest x1 2.6 us: local(): result = (middle + (feed_out + links.swap(feed_out))).astype(HALF)]
    ppermute x17, waiting for transfers between devices: 78.4 us -> 62.7 us  [send(): return lax.ppermute(array, ('dp', 'tensor'), pairs)]
    reduce_sum x7 -> x1, other arithmetic: 11.7 us -> 0.96 us  [local(): vec = jnp.sum(jnp.concatenate([vec, feed_vec], 0), 1)]
    ppermute x17, starting transfers between devices: 24.2 us -> 33.4 us  [send(): return lax.ppermute(array, ('dp', 'tensor'), pairs)]
  transfers between devices with their start and end apart: 25 -> 27, of which waited for: 7 -> 11; matrix products, arithmetic and copies ran while one was open for 57% -> 12% of each run, Pallas kernels for 6% -> 30%
where the time goes in v2:
time: 227 us; the launch traced here: 226 us
  Pallas kernels  93.7 us (41%)
  waiting for transfers between devices  66 us (29%)
  starting transfers between devices  36 us (16%)
  other arithmetic  20.3 us (9%)
  local copies, waits for them, and re-layouts  7.23 us (3%)
    pallas_call x10, Pallas kernels, call(): pl.pallas_call(body, out_shape=shapes, grid_spec=pltpu.PrefetchScalarGrid...  93.7 us
    ppermute x17, waiting for transfers between devices, send(): return lax.ppermute(array, ('dp', 'tensor'), pairs)  62.7 us
    ppermute x17, starting transfers between devices, send(): return lax.ppermute(array, ('dp', 'tensor'), pairs)  33.4 us
    add x4, other arithmetic, reduce(): leave, keep = (keep[:half] + come[:half], keep[half:] + come[half:])  8.72 us
    unnamed x42, local copies, waits for them, and re-layouts  5.13 us
  transfers between devices with their start and end apart: 27, of which 11 were waited for; matrix products, arithmetic and copies ran while one was open for 12% of the time, Pallas kernels for 30%

profile of v2, /device:TPU:0, one launch (start us, length us, event | category | flops | bytes accessed | tf_op | source)
XLA Modules:
  0.0 226.4 jit_solution(10513696052241641753)
XLA Ops:
  0.6 14.1 %attend.1 = (bf16[4,640,1024]{2,1,0:T(8,128)(2,1)}, bf16[4,64,256]{2,1,0:T(8,128)(2,1)}, bf16[4,640,256]{2,1,0:T(8,128)(2,1)}, bf16[4,640,256]{2,1,0:T(8,128)(2,...) custom-call(s32[4]{0:T(128)} %buckets_ref.1, ...), custom_call_target="tpu_custom_call" | custom-call | flops 3355443200 | bytes 19171328 | tf_op jit(solution)/shard_map/attend/pallas_call | solution.py:72
  14.7 0.6 collective-permute-start
  15.3 2.5 %collective-permute-done.far_ref = f32[256,1024]{1,0:T(8,128)S(1)} collective-permute-done((f32[256,1024]{1,0:T(8,128)}, f32[256,1024]{1,0:T(8,128)S(1)}, u32[]{:S(2)}, u32[]{:S(2)}) %collective-permute-start) | collective-permute-done | bytes 1048608 | tf_op jit(solution)/shard_map/ppermute | solution.py:521
  17.8 1.0 copy-done.12
  18.8 3.7 %middle.1 = (f32[256,1024]{1,0:T(8,128)}, bf16[256,1024]{1,0:T(8,128)(2,1)}, f32[128,1024]{1,0:T(8,128)}) custom-call(s32[1]{0:T(128)} %bitcast.core_ref, bf16[256,1024]{1,0:T(8,128)(2,1)} %bitcast.44, f32[256,1024]{1,0:T(8,128)} %bitcast.50, f32[256,1024]{1,0:T(8,128)} %copy-done.12, f32[1,1024]{1,0:T(1,128)} %bitcast.53, f32[1,1024]{1,0:T(1,128)} %bitcast.55), custom_call_target="tpu_custom_call" | custom-call | bytes 4726784 | tf_op jit(solution)/shard_map/middle/pallas_call | solution.py:72
  22.5 8.6 %feed.1 = (bf16[256,2048]{1,0:T(8,128)(2,1)}, f32[256,1024]{1,0:T(8,128)}) custom-call(bf16[256,1024]{1,0:T(8,128)(2,1)} %get-tuple-element.49.low_ref, bf16[256,1024]{1,0:T(8,128)(2,1)} %bitcast.45, bf16[1024,2048]{1,0:T(8,128)(2,1)} %refs_8_.1, bf16[2048,1024]{1,0:T(8,128)(2,1)} %refs_9_.1), custom_call_target="tpu_custom_call" | custom-call | flops 3221225472 | bytes 11534336 | tf_op jit(solution)/shard_map/feed/pallas_call | solution.py:72
  31.5 2.7 %collective-permute-start.14 = (f32[128,1024]{1,0:T(8,128)S(1)}, f32[128,1024]{1,0:T(8,128)S(1)}, u32[]{:S(2)}, u32[]{:S(2)}) collective-permute-start(f32[128,1024]{1,0:T(8,128)S(1)} %dynamic-slice_convert_fusion), channel_id=1, source_target_pairs={{0,2},{1,5},{2,0},{3,7},{4,6},{5,1},{6,4},{7,3},{8,10},{9,13},{10,... | collective-permute-start | bytes 1572872 | tf_op jit(solution)/shard_map/ppermute | solution.py:528
  34.3 7.1 %collective-permute-done.14 = f32[128,1024]{1,0:T(8,128)S(1)} collective-permute-done((f32[128,1024]{1,0:T(8,128)S(1)}, f32[128,1024]{1,0:T(8,128)S(1)}, u32[]{:S(2)}, u32[]{:S(2)}) %collective-permute-start.14) | collective-permute-done | bytes 524320 | tf_op jit(solution)/shard_map/ppermute | solution.py:528
  41.5 2.1 collective-permute-start.15
  43.6 6.3 %collective-permute-done.10 = f32[128,1024]{1,0:T(8,128)S(1)} collective-permute-done((f32[128,1024]{1,0:T(8,128)S(1)}, f32[128,1024]{1,0:T(8,128)S(1)}, u32[]{:S(2)}, u32[]{:S(2)}) %collective-permute-start.10) | collective-permute-done | bytes 524320 | tf_op jit(solution)/shard_map/ppermute | solution.py:528
  50.0 2.4 %collective-permute-start.11 = (f32[256,1024]{1,0:T(8,128)S(1)}, f32[256,1024]{1,0:T(8,128)}, u32[]{:S(2)}, u32[]{:S(2)}) collective-permute-start(f32[256,1024]{1,0:T(8,128)S(1)} %constant_dynamic-update-slice_fusion.refs_0_), channel_id=1, source_target_pairs={{0,4},{1,3},{2,6},{3,1},{4,0},{5,7},{6,2},{7,5},{8,12},{9,11},{10,... | collective-permute-start | bytes 3145736 | tf_op jit(solution)/shard_map/ppermute | solution.py:528
  52.5 10.5 %back.1 = (f32[256,1024]{1,0:T(8,128)}, bf16[256,1024]{1,0:T(8,128)(2,1)}, bf16[4,640,512]{2,1,0:T(8,128)(2,1)}, f32[4,640,512]{2,1,0:T(8,128)}, bf16[4,64,256]{...) custom-call(f32[256,1024]{1,0:T(8,128)} %get-tuple-element.48.mid_ref, ...), custom_call_target="tpu_custom_call" | custom-call | flops 1677721600 | bytes 19468288 | tf_op jit(solution)/shard_map/back/pallas_call | solution.py:72
  63.6 11.5 %small_grad.1 = (f32[8,64,1024]{2,1,0:T(8,128)}, f32[8,64,1024]{2,1,0:T(8,128)}) custom-call(s32[16]{0:T(128)} %broadcast_select_fusion.1.place_ref, bf16[2560,1024]{1,0:T(8,128)(2,1)} %bitcast.62, bf16[256,1024]{1,0:T(8,128)(2,1)} %get-tuple-element.66.gb_ref, bf16[2560,512]{1,0:T(8,128)(2,1)} %bitcast.43, bf16[256,256]{1,0:T(8,128)(2,1)} %bitcast.52, ...), custom_call_target="tpu_custom_call" | custom-call | flops 2684354560 | bytes 12845056 | tf_op jit(solution)/shard_map/small_grad/pallas_call | solution.py:72
  75.1 1.4 collective-permute-start.6
  78.2 2.9 %maximum_convert_fusion = f32[1024,768]{1,0:T(8,128)} fusion(bf16[1024,256]{1,0:T(8,128)(2,1)} %wv_ref.3, bf16[1024,256]{1,0:T(8,128)(2,1)S(1)} %copy-done.7, bf16[1024,256]{1,0:T(8,128)(2,1)S(1)} %copy-done.6), kind=kLoop, calls=%fused_computation | loop fusion | flops 4718592 | bytes 4718592 | tf_op jit(solution)/shard_map/convert_element_type | solution.py:583
  81.5 0.8 collective-permute-done.13.refs_3_
  82.5 9.3 %wide.1 = (bf16[1024,1024]{1,0:T(8,128)(2,1)}, bf16[1024,1024]{1,0:T(8,128)(2,1)}, bf16[1024,512]{1,0:T(8,128)(2,1)}, bf16[1024,512]{1,0:T(8,128)(2,1)}) custom-call(s32[1]{0:T(128)} %bitcast.18.member_ref, f32[256,1024]{1,0:T(8,128)} %copy-done.4, f32[256,1024]{1,0:T(8,128)} %collective-permute-done.11.refs_1_, ...), custom_call_target="tpu_custom_call" | custom-call | flops 2147483648 | bytes 23068672 | tf_op jit(solution)/shard_map/wide/pallas_call | solution.py:72
  91.8 6.4 %wide_grad.3 = f32[8,64,1024]{2,1,0:T(8,128)} custom-call(s32[4]{0:T(128)} %broadcast_add_fusion.order_ref, s32[16]{0:T(128)} %and_select_fusion.place_ref, bf16[1024,1024]{1,0:T(8,128)(2,1)} %get-tuple-element.71.fl_ref, bf16[1024,1024]{1,0:T(8,128)(2,1)} %get-tuple-element.72.cl_ref, bf16[1024,512]{1,0:T(8,128)(2,1)} %get-tuple-element.73.hid_ref, ...), custom_call_target="tpu_custom_call" | custom-call | flops 1073741824 | bytes 8388608 | tf_op jit(solution)/shard_map/wide_grad/pallas_call | solution.py:72
  98.2 2.6 %collective-permute-start.18 = (f32[8,64,1024]{2,1,0:T(8,128)}, f32[8,64,1024]{2,1,0:T(8,128)}, u32[]{:S(2)}, u32[]{:S(2)}) collective-permute-start(f32[8,64,1024]{2,1,0:T(8,128)} %wide_grad.3), channel_id=1, source_target_pairs={{0,16},{1,9},{2,18},{3,11},{4,20},{5,13},{6,22},{7,15},{8,24},{9,1... | collective-permute-start | bytes 6291464 | tf_op jit(solution)/shard_map/ppermute | solution.py:528
  100.8 0.6 collective-permute-done.6
  101.4 3.1 %slice_add_fusion.3 = (f32[4,64,1024]{2,1,0:T(8,128)S(1)}, f32[4,64,1024]{2,1,0:T(8,128)}) fusion(f32[8,64,1024]{2,1,0:T(8,128)} %collective-permute-done.6, f32[8,64,1024]{2,1,0:T(8,128)S(1)} %copy-done.5), kind=kLoop, calls=%fused_computation.5 | loop fusion | flops 524288 | bytes 6291456 | tf_op jit(solution)/shard_map/add | solution.py:546
  104.8 2.2 fusion.5
  108.1 6.3 %wide_grad.2 = f32[8,64,1024]{2,1,0:T(8,128)} custom-call(s32[4]{0:T(128)} %broadcast_add_fusion.1.order_ref, s32[16]{0:T(128)} %and_select_fusion.place_ref, bf16[1024,1024]{1,0:T(8,128)(2,1)} %get-tuple-element.71.fl_ref, bf16[1024,1024]{1,0:T(8,128)(2,1)} %get-tuple-element.72.cl_ref, bf16[1024,512]{1,0:T(8,128)(2,1)} %get-tuple-element.73.hid_ref, ...), custom_call_target="tpu_custom_call" | custom-call | flops 1073741824 | bytes 8388608 | tf_op jit(solution)/shard_map/wide_grad/pallas_call | solution.py:72
  114.4 5.3 %collective-permute-done.7 = f32[4,64,1024]{2,1,0:T(8,128)} collective-permute-done((f32[4,64,1024]{2,1,0:T(8,128)}, f32[4,64,1024]{2,1,0:T(8,128)}, u32[]{:S(2)}, u32[]{:S(2)}) %collective-permute-start.7) | collective-permute-done | bytes 1048608 | tf_op jit(solution)/shard_map/ppermute | solution.py:528
  119.6 2.3 %slice_add_fusion.5 = (f32[2,64,1024]{2,1,0:T(8,128)}, f32[2,64,1024]{2,1,0:T(8,128)}) fusion(f32[4,64,1024]{2,1,0:T(8,128)} %collective-permute-done.7, f32[4,64,1024]{2,1,0:T(8,128)S(1)} %get-tuple-element.94), kind=kLoop, calls=%fused_computation.9 | loop fusion | flops 262144 | bytes 3145728 | tf_op jit(solution)/shard_map/add | solution.py:546
  121.9 1.6 collective-permute-start.8
  123.5 35.7 %collective-permute-done.18 = f32[8,64,1024]{2,1,0:T(8,128)} collective-permute-done((f32[8,64,1024]{2,1,0:T(8,128)}, f32[8,64,1024]{2,1,0:T(8,128)}, u32[]{:S(2)}, u32[]{:S(2)}) %collective-permute-start.18) | collective-permute-done | bytes 2097184 | tf_op jit(solution)/shard_map/ppermute | solution.py:528
  159.2 2.3 %slice_add_fusion = f32[4,64,1024]{2,1,0:T(8,128)} fusion(f32[8,64,1024]{2,1,0:T(8,128)} %collective-permute-done.18, f32[8,64,1024]{2,1,0:T(8,128)S(1)} %copy-done), kind=kLoop, calls=%fused_computation.1 | loop fusion | flops 262144 | bytes 3145728 | tf_op jit(solution)/shard_map/add | solution.py:546
  161.6 12.9 %collective-permute-start.19 = (f32[4,64,1024]{2,1,0:T(8,128)}, f32[4,64,1024]{2,1,0:T(8,128)}, u32[]{:S(2)}, u32[]{:S(2)}) collective-permute-start(f32[4,64,1024]{2,1,0:T(8,128)} %slice_add_fusion), channel_id=1, source_target_pairs={{0,8},{1,17},{2,10},{3,19},{4,12},{5,21},{6,14},{7,23},{8,0},{9,25... | collective-permute-start | bytes 3145736 | tf_op jit(solution)/shard_map/ppermute | solution.py:528
  174.5 2.6 %add_convert_fusion = bf16[256,1024]{1,0:T(8,128)(2,1)} fusion(f32[256,1024]{1,0:T(8,128)S(1)} %copy-done.2, f32[256,1024]{1,0:T(8,128)} %fusion.5, f32[256,1024]{1,0:T(8,128)} %collective-permute-done.1), kind=kLoop, calls=%fused_computation.7 | loop fusion | flops 786432 | bytes 3670016 | tf_op jit(solution)/shard_map/convert_element_type | solution.py:653
  177.1 1.0 slice_add_fusion.6
  178.1 3.4 %collective-permute-start.9 = (f32[1,64,1024]{2,1,0:T(8,128)S(1)}, f32[1,64,1024]{2,1,0:T(8,128)S(1)}, u32[]{:S(2)}, u32[]{:S(2)}) collective-permute-start(f32[1,64,1024]{2,1,0:T(8,128)S(1)} %slice_add_fusion.6), channel_id=1, source_target_pairs={{0,16},{1,9},{2,18},{3,11},{4,20},{5,13},{6,22},{7,15},{8,24},{9,1... | collective-permute-start | bytes 786440 | tf_op jit(solution)/shard_map/ppermute | solution.py:528
  181.5 0.7 copy-done.14
  182.2 20.7 %inputs_back.1 = (bf16[4,576,1024]{2,1,0:T(8,128)(2,1)}, bf16[4,64,1024]{2,1,0:T(8,128)(2,1)}, f32[4,8,1024]{2,1,0:T(8,128)}) custom-call(bf16[4,640,512]{2,1,0:T(8,128)(2,1)} %get-tuple-element.56.gkv_ref, f32[4,640,512]{2,1,0:T(8,128)} %collective-permute-done.3.gkv_far_ref, bf16[4,64,256]{2,1,0:T(8,128)(2,1)} %get-tuple-element.58.gq_ref, ...), custom_call_target="tpu_custom_call" | custom-call | flops 4831838208 | bytes 24668160 | tf_op jit(solution)/shard_map/inputs_back/pallas_call | solution.py:72
  202.9 1.0 maximum_reduce_fusion
  204.3 1.8 fusion
  206.2 2.0 collective-permute-done.23
  208.2 0.8 slice_bitcast_fusion
  209.2 2.0 collective-permute-start.21
  211.2 1.3 collective-permute-start.22
  212.5 1.8 collective-permute-done.24
  214.4 1.0 fusion.2
  215.4 2.9 %collective-permute-done.25 = f32[8,1024]{1,0:T(8,128)S(1)} collective-permute-done((f32[8,1024]{1,0:T(8,128)S(1)}, f32[8,1024]{1,0:T(8,128)S(1)}, u32[]{:S(2)}, u32[]{:S(2)}) %collective-permute-start.25) | collective-permute-done | bytes 32800 | tf_op jit(solution)/shard_map/ppermute | solution.py:528
  218.3 0.7 slice_bitcast_fusion.4
  219.0 1.0 collective-permute-done.21.refs_2_
  220.0 0.7 copy-done.16
  220.8 2.7 %place_pieces.1 = (f32[64,2048]{1,0:T(8,128)}, f32[2048,64]{1,0:T(8,128)}) custom-call(s32[1]{0:T(128)} %bitcast.18.member_ref, f32[64,1024]{1,0:T(8,128)} %get-tuple-element.101.refs_0_, f32[64,1024]{1,0:T(8,128)} %copy-done.15, f32[64,1024]{1,0:T(8,128)} %copy-done.16, f32[64,1024]{1,0:T(8,128)} %copy-done.17), custom_call_target="tpu_custom_call" | custom-call | bytes 2097152 | tf_op jit(solution)/shard_map/place_pieces/pallas_call | solution.py:72
  223.4 2.3 %copy.31 = f32[2048,64]{0,1:T(8,128)} copy(f32[2048,64]{1,0:T(8,128)} %get-tuple-element.87) | data formatting | bytes 1048576
  (83 shorter events, 6.4 us)
Async XLA Ops:
  14.7 3.1 %collective-permute-start = (f32[256,1024]{1,0:T(8,128)}, f32[256,1024]{1,0:T(8,128)S(1)}, u32[]{:S(2)}, u32[]{:S(2)}) collective-permute-start(f32[256,1024]{1,0:T(8,128)} %bitcast.49), channel_id=1, source_target_pairs={{0,1},{1,0},{2,3},{3,2},{4,5},{5,4},{6,7},{7,6},{8,9},{9,8},{10,11... | collective-permute-start | bytes 3145736 | tf_op jit(solution)/shard_map/ppermute | solution.py:521
  17.8 1.0 copy-start.12
  22.5 9.0 %copy-start.10 = (bf16[4,64,1024]{2,1,0:T(8,128)(2,1)S(1)}, bf16[4,64,1024]{2,1,0:T(8,128)(2,1)}, u32[]{:S(2)}) copy-start(bf16[4,64,1024]{2,1,0:T(8,128)(2,1)} %param.19) | copy-start | bytes 1572868
  22.5 11.7 %copy-start.13 = (f32[128,1024]{1,0:T(8,128)S(1)}, f32[128,1024]{1,0:T(8,128)}, u32[]{:S(2)}) copy-start(f32[128,1024]{1,0:T(8,128)} %get-tuple-element.70) | copy-start | bytes 1572868
  31.1 21.4 %collective-permute-start.2 = (f32[256,1024]{1,0:T(8,128)}, f32[256,1024]{1,0:T(8,128)}, u32[]{:S(2)}, u32[]{:S(2)}) collective-permute-start(f32[256,1024]{1,0:T(8,128)} %get-tuple-element.51.own_ref), channel_id=1, source_target_pairs={{0,1},{1,0},{2,3},{3,2},{4,5},{5,4},{6,7},{7,6},{8,9},{9,8},{10,11... | collective-permute-start | bytes 3145736 | tf_op jit(solution)/shard_map/ppermute | solution.py:521
  31.5 9.8 %collective-permute-start.14 = (f32[128,1024]{1,0:T(8,128)S(1)}, f32[128,1024]{1,0:T(8,128)S(1)}, u32[]{:S(2)}, u32[]{:S(2)}) collective-permute-start(f32[128,1024]{1,0:T(8,128)S(1)} %dynamic-slice_convert_fusion), channel_id=1, source_target_pairs={{0,2},{1,5},{2,0},{3,7},{4,6},{5,1},{6,4},{7,3},{8,10},{9,13},{10,... | collective-permute-start | bytes 1572872 | tf_op jit(solution)/shard_map/ppermute | solution.py:528
  34.2 15.8 %collective-permute-start.10 = (f32[128,1024]{1,0:T(8,128)S(1)}, f32[128,1024]{1,0:T(8,128)S(1)}, u32[]{:S(2)}, u32[]{:S(2)}) collective-permute-start(f32[128,1024]{1,0:T(8,128)S(1)} %copy-done.13), channel_id=1, source_target_pairs={{0,2},{1,5},{2,0},{3,7},{4,6},{5,1},{6,4},{7,3},{8,10},{9,13},{10,... | collective-permute-start | bytes 1572872 | tf_op jit(solution)/shard_map/ppermute | solution.py:528
  41.5 21.5 %copy-start.3 = (f32[256,1024]{1,0:T(8,128)}, f32[256,1024]{1,0:T(8,128)S(1)}, u32[]{:S(2)}) copy-start(f32[256,1024]{1,0:T(8,128)S(1)} %pad_maximum_fusion.refs_4_) | copy-start | bytes 3145732
  41.5 35.0 %collective-permute-start.15 = (f32[256,1024]{1,0:T(8,128)S(1)}, f32[256,1024]{1,0:T(8,128)}, u32[]{:S(2)}, u32[]{:S(2)}) collective-permute-start(f32[256,1024]{1,0:T(8,128)S(1)} %pad_maximum_fusion.refs_4_), channel_id=1, source_target_pairs={{0,4},{1,3},{2,6},{3,1},{4,0},{5,7},{6,2},{7,5},{8,12},{9,11},{10,... | collective-permute-start | bytes 3145736 | tf_op jit(solution)/shard_map/ppermute | solution.py:528
  43.6 32.9 %collective-permute-start.16 = (f32[256,1024]{1,0:T(8,128)S(1)}, f32[256,1024]{1,0:T(8,128)}, u32[]{:S(2)}, u32[]{:S(2)}) collective-permute-start(f32[256,1024]{1,0:T(8,128)S(1)} %pad_maximum_fusion.refs_4_), channel_id=1, source_target_pairs={{0,1},{1,0},{2,3},{3,2},{4,5},{5,4},{6,7},{7,6},{8,9},{9,8},{10,11... | collective-permute-start | bytes 3145736 | tf_op jit(solution)/shard_map/ppermute | solution.py:521
  50.0 26.5 %copy-start.4 = (f32[256,1024]{1,0:T(8,128)}, f32[256,1024]{1,0:T(8,128)S(1)}, u32[]{:S(2)}) copy-start(f32[256,1024]{1,0:T(8,128)S(1)} %constant_dynamic-update-slice_fusion.refs_0_) | copy-start | bytes 3145732
  50.0 27.0 %collective-permute-start.11 = (f32[256,1024]{1,0:T(8,128)S(1)}, f32[256,1024]{1,0:T(8,128)}, u32[]{:S(2)}, u32[]{:S(2)}) collective-permute-start(f32[256,1024]{1,0:T(8,128)S(1)} %constant_dynamic-update-slice_fusion.refs_0_), channel_id=1, source_target_pairs={{0,4},{1,3},{2,6},{3,1},{4,0},{5,7},{6,2},{7,5},{8,12},{9,11},{10,... | collective-permute-start | bytes 3145736 | tf_op jit(solution)/shard_map/ppermute | solution.py:528
  63.0 118.5 %collective-permute-start.3 = (f32[4,640,512]{2,1,0:T(8,128)}, f32[4,640,512]{2,1,0:T(8,128)}, u32[]{:S(2)}, u32[]{:S(2)}) collective-permute-start(f32[4,640,512]{2,1,0:T(8,128)} %get-tuple-element.57), channel_id=1, source_target_pairs={{0,1},{1,0},{2,3},{3,2},{4,5},{5,4},{6,7},{7,6},{8,9},{9,8},{10,11... | collective-permute-start | bytes 15728648 | tf_op jit(solution)/shard_map/ppermute | solution.py:521
  63.6 14.5 %copy-start.6 = (bf16[1024,256]{1,0:T(8,128)(2,1)S(1)}, bf16[1024,256]{1,0:T(8,128)(2,1)}, u32[]{:S(2)}) copy-start(bf16[1024,256]{1,0:T(8,128)(2,1)} %wq_ref.3) | copy-start | bytes 1572868
  63.6 14.5 %copy-start.7 = (bf16[1024,256]{1,0:T(8,128)(2,1)S(1)}, bf16[1024,256]{1,0:T(8,128)(2,1)}, u32[]{:S(2)}) copy-start(bf16[1024,256]{1,0:T(8,128)(2,1)} %wk_ref.3) | copy-start | bytes 1572868
  75.1 26.4 %collective-permute-start.6 = (f32[8,64,1024]{2,1,0:T(8,128)}, f32[8,64,1024]{2,1,0:T(8,128)}, u32[]{:S(2)}, u32[]{:S(2)}) collective-permute-start(f32[8,64,1024]{2,1,0:T(8,128)} %get-tuple-element.69), channel_id=1, source_target_pairs={{0,2},{1,5},{2,0},{3,7},{4,6},{5,1},{6,4},{7,3},{8,10},{9,13},{10,... | collective-permute-start | bytes 6291464 | tf_op jit(solution)/shard_map/ppermute | solution.py:528
  76.5 4.6 %collective-permute-start.12 = (f32[256,1024]{1,0:T(8,128)S(1)}, f32[256,1024]{1,0:T(8,128)}, u32[]{:S(2)}, u32[]{:S(2)}) collective-permute-start(f32[256,1024]{1,0:T(8,128)S(1)} %constant_dynamic-update-slice_fusion.refs_0_), channel_id=1, source_target_pairs={{0,1},{1,0},{2,3},{3,2},{4,5},{5,4},{6,7},{7,6},{8,9},{9,8},{10,11... | collective-permute-start | bytes 3145736 | tf_op jit(solution)/shard_map/ppermute | solution.py:521
  76.5 5.0 %collective-permute-start.17 = (f32[256,1024]{1,0:T(8,128)}, f32[256,1024]{1,0:T(8,128)S(1)}, u32[]{:S(2)}, u32[]{:S(2)}) collective-permute-start(f32[256,1024]{1,0:T(8,128)} %collective-permute-done.15.refs_5_), channel_id=1, source_target_pairs={{0,1},{1,0},{2,3},{3,2},{4,5},{5,4},{6,7},{7,6},{8,9},{9,8},{10,11... | collective-permute-start | bytes 3145736 | tf_op jit(solution)/shard_map/ppermute | solution.py:521
  77.0 5.3 %collective-permute-start.13 = (f32[256,1024]{1,0:T(8,128)}, f32[256,1024]{1,0:T(8,128)}, u32[]{:S(2)}, u32[]{:S(2)}) collective-permute-start(f32[256,1024]{1,0:T(8,128)} %collective-permute-done.11.refs_1_), channel_id=1, source_target_pairs={{0,1},{1,0},{2,3},{3,2},{4,5},{5,4},{6,7},{7,6},{8,9},{9,8},{10,11... | collective-permute-start | bytes 3145736 | tf_op jit(solution)/shard_map/ppermute | solution.py:521
  81.1 100.4 %collective-permute-start.5 = (f32[1024,768]{1,0:T(8,128)}, f32[1024,768]{1,0:T(8,128)}, u32[]{:S(2)}, u32[]{:S(2)}) collective-permute-start(f32[1024,768]{1,0:T(8,128)} %maximum_convert_fusion), channel_id=1, source_target_pairs={{0,1},{1,0},{2,3},{3,2},{4,5},{5,4},{6,7},{7,6},{8,9},{9,8},{10,11... | collective-permute-start | bytes 9437192 | tf_op jit(solution)/shard_map/ppermute | solution.py:521
  81.5 1.0 copy-start.11
  91.8 9.6 %copy-start.5 = (f32[8,64,1024]{2,1,0:T(8,128)S(1)}, f32[8,64,1024]{2,1,0:T(8,128)}, u32[]{:S(2)}) copy-start(f32[8,64,1024]{2,1,0:T(8,128)} %get-tuple-element.68) | copy-start | bytes 6291460
  98.2 61.0 %collective-permute-start.18 = (f32[8,64,1024]{2,1,0:T(8,128)}, f32[8,64,1024]{2,1,0:T(8,128)}, u32[]{:S(2)}, u32[]{:S(2)}) collective-permute-start(f32[8,64,1024]{2,1,0:T(8,128)} %wide_grad.3), channel_id=1, source_target_pairs={{0,16},{1,9},{2,18},{3,11},{4,20},{5,13},{6,22},{7,15},{8,24},{9,1... | collective-permute-start | bytes 6291464 | tf_op jit(solution)/shard_map/ppermute | solution.py:528
  101.4 3.4 %copy-start.1 = (bf16[2048,1024]{1,0:T(8,128)(2,1)S(1)}, bf16[2048,1024]{1,0:T(8,128)(2,1)}, u32[]{:S(2)}) copy-start(bf16[2048,1024]{1,0:T(8,128)(2,1)} %refs_9_.1) | copy-start | bytes 12582916
  101.4 3.4 %copy-start.19 = (bf16[256,2048]{1,0:T(8,128)(2,1)S(1)}, bf16[256,2048]{1,0:T(8,128)(2,1)}, u32[]{:S(2)}) copy-start(bf16[256,2048]{1,0:T(8,128)(2,1)} %get-tuple-element.50) | copy-start | bytes 3145732
  104.5 15.1 %collective-permute-start.7 = (f32[4,64,1024]{2,1,0:T(8,128)}, f32[4,64,1024]{2,1,0:T(8,128)}, u32[]{:S(2)}, u32[]{:S(2)}) collective-permute-start(f32[4,64,1024]{2,1,0:T(8,128)} %get-tuple-element.95), channel_id=1, source_target_pairs={{0,4},{1,3},{2,6},{3,1},{4,0},{5,7},{6,2},{7,5},{8,12},{9,11},{10,... | collective-permute-start | bytes 3145736 | tf_op jit(solution)/shard_map/ppermute | solution.py:528
  107.1 67.4 %collective-permute-start.1 = (f32[256,1024]{1,0:T(8,128)}, f32[256,1024]{1,0:T(8,128)}, u32[]{:S(2)}, u32[]{:S(2)}) collective-permute-start(f32[256,1024]{1,0:T(8,128)} %fusion.5), channel_id=1, source_target_pairs={{0,1},{1,0},{2,3},{3,2},{4,5},{5,4},{6,7},{7,6},{8,9},{9,8},{10,11... | collective-permute-start | bytes 3145736 | tf_op jit(solution)/shard_map/ppermute | solution.py:521
  114.4 44.9 %copy-start = (f32[8,64,1024]{2,1,0:T(8,128)S(1)}, f32[8,64,1024]{2,1,0:T(8,128)}, u32[]{:S(2)}) copy-start(f32[8,64,1024]{2,1,0:T(8,128)} %wide_grad.2) | copy-start | bytes 6291460
  121.9 52.5 %copy-start.2 = (f32[256,1024]{1,0:T(8,128)S(1)}, f32[256,1024]{1,0:T(8,128)}, u32[]{:S(2)}) copy-start(f32[256,1024]{1,0:T(8,128)} %get-tuple-element.48.mid_ref) | copy-start | bytes 3145732
  121.9 55.1 %collective-permute-start.8 = (f32[2,64,1024]{2,1,0:T(8,128)}, f32[2,64,1024]{2,1,0:T(8,128)}, u32[]{:S(2)}, u32[]{:S(2)}) collective-permute-start(f32[2,64,1024]{2,1,0:T(8,128)} %get-tuple-element.97), channel_id=1, source_target_pairs={{0,8},{1,17},{2,10},{3,19},{4,12},{5,21},{6,14},{7,23},{8,0},{9,25... | collective-permute-start | bytes 1572872 | tf_op jit(solution)/shard_map/ppermute | solution.py:528
  161.6 42.8 %collective-permute-start.19 = (f32[4,64,1024]{2,1,0:T(8,128)}, f32[4,64,1024]{2,1,0:T(8,128)}, u32[]{:S(2)}, u32[]{:S(2)}) collective-permute-start(f32[4,64,1024]{2,1,0:T(8,128)} %slice_add_fusion), channel_id=1, source_target_pairs={{0,8},{1,17},{2,10},{3,19},{4,12},{5,21},{6,14},{7,23},{8,0},{9,25... | collective-permute-start | bytes 3145736 | tf_op jit(solution)/shard_map/ppermute | solution.py:528
  174.4 2.6 %copy-start.8 = (f32[2,64,1024]{2,1,0:T(8,128)S(1)}, f32[2,64,1024]{2,1,0:T(8,128)}, u32[]{:S(2)}) copy-start(f32[2,64,1024]{2,1,0:T(8,128)} %get-tuple-element.96) | copy-start | bytes 1572868
  174.4 7.1 %collective-permute-start.4 = (f32[4,64,256]{2,1,0:T(8,128)}, f32[4,64,256]{2,1,0:T(8,128)S(1)}, u32[]{:S(2)}, u32[]{:S(2)}) collective-permute-start(f32[4,64,256]{2,1,0:T(8,128)} %get-tuple-element.59), channel_id=1, source_target_pairs={{0,1},{1,0},{2,3},{3,2},{4,5},{5,4},{6,7},{7,6},{8,9},{9,8},{10,11... | collective-permute-start | bytes 786440 | tf_op jit(solution)/shard_map/ppermute | solution.py:521
  178.1 36.3 %collective-permute-start.9 = (f32[1,64,1024]{2,1,0:T(8,128)S(1)}, f32[1,64,1024]{2,1,0:T(8,128)S(1)}, u32[]{:S(2)}, u32[]{:S(2)}) collective-permute-start(f32[1,64,1024]{2,1,0:T(8,128)S(1)} %slice_add_fusion.6), channel_id=1, source_target_pairs={{0,16},{1,9},{2,18},{3,11},{4,20},{5,13},{6,22},{7,15},{8,24},{9,1... | collective-permute-start | bytes 786440 | tf_op jit(solution)/shard_map/ppermute | solution.py:528
  181.5 0.7 copy-start.14
  182.2 20.7 %copy-start.18 = (f32[2,8,1024]{2,1,0:T(8,128)S(1)}, f32[2,8,1024]{2,1,0:T(8,128)}, u32[]{:S(2)}) copy-start(f32[2,8,1024]{2,1,0:T(8,128)} %get-tuple-element.78) | copy-start | bytes 196612
  203.9 4.3 %collective-permute-start.23 = (f32[8,1024]{1,0:T(8,128)S(1)}, f32[8,1024]{1,0:T(8,128)S(1)}, u32[]{:S(2)}, u32[]{:S(2)}) collective-permute-start(f32[8,1024]{1,0:T(8,128)S(1)} %concatenate.19), channel_id=1, source_target_pairs={{0,2},{1,3},{2,0},{3,1},{4,6},{5,7},{6,4},{7,5},{8,10},{9,11},{10,... | collective-permute-start | bytes 98312 | tf_op jit(solution)/shard_map/ppermute | solution.py:528
  206.1 8.2 %copy-start.9 = (f32[2,64,1024]{2,1,0:T(8,128)S(1)}, f32[2,64,1024]{2,1,0:T(8,128)}, u32[]{:S(2)}) copy-start(f32[2,64,1024]{2,1,0:T(8,128)} %get-tuple-element.96) | copy-start | bytes 1572868
  208.2 6.1 %collective-permute-start.24 = (f32[8,1024]{1,0:T(8,128)S(1)}, f32[8,1024]{1,0:T(8,128)S(1)}, u32[]{:S(2)}, u32[]{:S(2)}) collective-permute-start(f32[8,1024]{1,0:T(8,128)S(1)} %pad_add_fusion), channel_id=1, source_target_pairs={{0,4},{1,5},{2,6},{3,7},{4,0},{5,1},{6,2},{7,3},{8,12},{9,13},{10,... | collective-permute-start | bytes 98312 | tf_op jit(solution)/shard_map/ppermute | solution.py:528
  209.0 10.0 %collective-permute-start.20 = (f32[64,1024]{1,0:T(8,128)S(1)}, f32[64,1024]{1,0:T(8,128)S(1)}, u32[]{:S(2)}, u32[]{:S(2)}) collective-permute-start(f32[64,1024]{1,0:T(8,128)S(1)} %get-tuple-element.100), channel_id=1, source_target_pairs={{0,2},{1,3},{2,0},{3,1},{4,6},{5,7},{6,4},{7,5},{8,10},{9,11},{10,... | collective-permute-start | bytes 786440 | tf_op jit(solution)/shard_map/ppermute | solution.py:528
  209.2 10.7 %collective-permute-start.21 = (f32[64,1024]{1,0:T(8,128)S(1)}, f32[64,1024]{1,0:T(8,128)S(1)}, u32[]{:S(2)}, u32[]{:S(2)}) collective-permute-start(f32[64,1024]{1,0:T(8,128)S(1)} %get-tuple-element.99), channel_id=1, source_target_pairs={{0,4},{1,5},{2,6},{3,7},{4,0},{5,1},{6,2},{7,3},{8,12},{9,13},{10,... | collective-permute-start | bytes 786440 | tf_op jit(solution)/shard_map/ppermute | solution.py:528
  211.2 8.7 %collective-permute-start.22 = (f32[64,1024]{1,0:T(8,128)S(1)}, f32[64,1024]{1,0:T(8,128)S(1)}, u32[]{:S(2)}, u32[]{:S(2)}) collective-permute-start(f32[64,1024]{1,0:T(8,128)S(1)} %get-tuple-element.98), channel_id=1, source_target_pairs={{0,6},{1,7},{2,4},{3,5},{4,2},{5,3},{6,0},{7,1},{8,14},{9,15},{10,... | collective-permute-start | bytes 786440 | tf_op jit(solution)/shard_map/ppermute | solution.py:528
  214.3 3.9 %collective-permute-start.25 = (f32[8,1024]{1,0:T(8,128)S(1)}, f32[8,1024]{1,0:T(8,128)S(1)}, u32[]{:S(2)}, u32[]{:S(2)}) collective-permute-start(f32[8,1024]{1,0:T(8,128)S(1)} %add.165), channel_id=1, source_target_pairs={{0,8},{1,9},{2,10},{3,11},{4,12},{5,13},{6,14},{7,15},{8,0},{9,1},... | collective-permute-start | bytes 98312 | tf_op jit(solution)/shard_map/ppermute | solution.py:528
  218.3 7.5 %collective-permute-start.26 = (f32[8,1024]{1,0:T(8,128)S(1)}, f32[8,1024]{1,0:T(8,128)S(1)}, u32[]{:S(2)}, u32[]{:S(2)}) collective-permute-start(f32[8,1024]{1,0:T(8,128)S(1)} %add.166), channel_id=1, source_target_pairs={{0,16},{1,17},{2,18},{3,19},{4,20},{5,21},{6,22},{7,23},{8,24},{9,... | collective-permute-start | bytes 98312 | tf_op jit(solution)/shard_map/ppermute | solution.py:528
  219.0 1.0 copy-start.15
  220.0 0.7 copy-start.16
  220.0 0.8 copy-start.17

commit v3 on v2

--- a/solution.py
+++ b/solution.py
@@ -12,6 +12,7 @@
 SHORT = 256
 GROUP = 4
 LANES = 128
+WIDE = 256
 EPSILON = 1e-05
 SINGLE = jnp.float32
 HALF = jnp.bfloat16
@@ -65,7 +66,7 @@
     return values * below, below + values * density
 
 
-def call(body, name, grid, ins, outs, scratch=(), prefetch=(), flops=0, cost=None):
+def call(body, name, grid, ins, outs, scratch=(), prefetch=(), flops=0, aliases=None):
     moved = sum(a.size * a.dtype.itemsize for a, _ in ins)
     shapes = [jax.ShapeDtypeStruct(s, d) for s, d, _ in outs]
     moved += sum(s.size * s.dtype.itemsize for s in shapes)
@@ -80,6 +81,7 @@
             scratch_shapes=list(scratch),
         ),
         cost_estimate=pl.CostEstimate(flops=flops, bytes_accessed=moved, transcendentals=0),
+        input_output_aliases=aliases or {},
         name=name,
     )(*prefetch, *[a for a, _ in ins])
 
@@ -167,41 +169,50 @@
     )
 
 
-def middle_body(core_ref, latent_ref, own_ref, far_ref, gain_ref, bias_ref, mid_ref, low_ref, send_ref):
+def middle_body(
+    core_ref, latent_ref, own_ref, far_ref, gain_ref, bias_ref,
+    mid_ref, low_ref, send_ref, first_ref, second_ref,
+):
     middle = latent_ref[...].astype(SINGLE) + (own_ref[...] + far_ref[...])
     mid_ref[...] = middle
     _, center, inverse = moments(middle)
     low = (center * inverse * gain_ref[...] + bias_ref[...]).astype(HALF)
     low_ref[...] = low
     half = low.shape[0] // 2
-
-    @pl.when(core_ref[0] == 0)
-    def _():
-        send_ref[...] = low[:half].astype(SINGLE)
-
-    @pl.when(core_ref[0] == 1)
-    def _():
-        send_ref[...] = low[half:].astype(SINGLE)
-
-
-def feed_body(low_ref, cot_ref, up_ref, down_ref, hidden_ref, part_ref):
+    for which in range(2):
+
+        @pl.when(core_ref[0] == which)
+        def _():
+            send = low[which * half : (which + 1) * half].astype(SINGLE)
+            send_ref[...] = send
+            first_ref[...] = send[: half // 2]
+            second_ref[...] = send[half // 2 :]
+
+
+def feed_body(low_ref, cot_ref, up_ref, down_ref, hidden_ref, grad_ref, part_ref, out_ref):
     half = up_ref.shape[1] // 2
-    total = None
+    total, result = None, None
     for at in range(2):
         cols = slice(at * half, (at + 1) * half)
         value, slope = exact_gelu(dot(low_ref[...], up_ref[:, cols]))
-        hidden_ref[:, cols] = value.astype(HALF)
+        value = value.astype(HALF)
+        hidden_ref[:, cols] = value
         grad = (slope * dot(cot_ref[...], down_ref[cols], 1, 1)).astype(HALF)
+        grad_ref[:, cols] = grad
         piece = dot(grad, up_ref[:, cols], 1, 1)
         total = piece if total is None else total + piece
+        piece = dot(value, down_ref[cols])
+        result = piece if result is None else result + piece
 
     @pl.when(pl.program_id(0) == 0)
     def _():
         part_ref[...] = total
+        out_ref[...] = result
 
     @pl.when(pl.program_id(0) > 0)
     def _():
         part_ref[...] += total
+        out_ref[...] += result
 
 
 def feed(low, cot, up, down):
@@ -220,94 +231,144 @@
         ],
         [
             ((rows, hidden), HALF, pl.BlockSpec((rows, block), lambda at: (0, at))),
+            ((rows, hidden), HALF, pl.BlockSpec((rows, block), lambda at: (0, at))),
+            ((rows, width), SINGLE, pl.BlockSpec((rows, width), lambda at: (0, 0))),
             ((rows, width), SINGLE, pl.BlockSpec((rows, width), lambda at: (0, 0))),
         ],
-        flops=6 * rows * width * hidden,
-    )
-
-
-def wide_body(member_ref, *refs):
-    feeds, cots = refs[0:4], refs[4:8]
-    up_ref, down_ref = refs[8:10]
-    fl_ref, cl_ref, hid_ref, gp_ref = refs[10:14]
-    fbuf, cbuf, sems = refs[14:]
-    rows = fbuf.shape[1]
-    copies = []
-    for at in range(4):
-        first = pltpu.make_async_copy(feeds[at], fbuf.at[at], sems.at[0, at])
-        second = pltpu.make_async_copy(cots[at], cbuf.at[at], sems.at[1, at])
-        first.start()
-        second.start()
-        copies.append((first, second))
-    for at in range(4):
-        here = slice(at * rows, (at + 1) * rows)
-        copies[at][0].wait()
-        low = fbuf[at].astype(HALF)
-        fl_ref[here] = low
-        value, slope = exact_gelu(dot(low, up_ref[...]))
-        hid_ref[here] = value.astype(HALF)
-        copies[at][1].wait()
-        low = cbuf[at].astype(HALF)
-        cl_ref[here] = low
-        gp_ref[here] = (slope * dot(low, down_ref[...], 1, 1)).astype(HALF)
-
-
-def wide(member, feeds, cots, up, down):
-    rows, width = feeds[0].shape
+        flops=8 * rows * width * hidden,
+    )
+
+
+def put_shares(value, place_ref, leave_ref, keep_ref):
+    held, share = leave_ref.shape[:2]
+    per = value.shape[0] // share
+    for at in range(per):
+        rows = value[at * share : (at + 1) * share]
+        spot = place_ref[pl.program_id(0) * per + at]
+
+        @pl.when(spot < held)
+        def _():
+            leave_ref[spot] = rows
+
+        @pl.when(spot >= held)
+        def _():
+            keep_ref[spot - held] = rows
+
+
+def down_side_body(member_ref, place_ref, *refs, counts):
+    feeds, cots = refs[: counts[0]], refs[counts[0] : sum(counts)]
+    up_ref, low_ref, cot_ref, own_ref = refs[sum(counts) :][:4]
+    leave_ref, keep_ref, fl_ref, cl_ref, slope_ref = refs[sum(counts) + 4 :][:5]
+    hid_ref, fbuf, cbuf, sems = refs[sum(counts) + 9 :]
+    far = fbuf.shape[0]
+    third = far // 3
+
+    @pl.when(pl.program_id(0) == 0)
+    def _():
+        started = []
+        for side, (arrays, buffer) in enumerate(((feeds, fbuf), (cots, cbuf))):
+            first = 0
+            for at, array in enumerate(arrays):
+                count = array.shape[0]
+                rows = pl.ds(first, count)
+                copy = pltpu.make_async_copy(array, buffer.at[rows], sems.at[side, at])
+                copy.start()
+                started.append((copy, side, first))
+                first += count
+        for at in range(3):
+            here = slice(at * third, (at + 1) * third)
+            for copy, side, first in started:
+                if side == 0 and here.start <= first < here.stop:
+                    copy.wait()
+            low = fbuf[here].astype(HALF)
+            fl_ref[here] = low
+            value, slope = exact_gelu(dot(low, up_ref[...]))
+            hid_ref[here] = value.astype(HALF)
+            slope_ref[here] = slope
+        fl_ref[far:] = low_ref[...]
+        hid_ref[far:] = own_ref[...]
+        for copy, side, first in started:
+            if side == 1:
+                copy.wait()
+        cl_ref[:far] = cbuf[...].astype(HALF)
+        cl_ref[far:] = cot_ref[...]
+
+    cols = pl.ds(pl.multiple_of(pl.program_id(0) * WIDE, WIDE), WIDE)
+    put_shares(dot(cl_ref[:, cols], hid_ref[...], 0, 0), place_ref, leave_ref, keep_ref)
+
+
+def down_side(member, place, feeds, cots, up, low, cot, hidden, devices):
+    rows, width = low.shape
+    far = 3 * rows
+    total = far + rows
+    counts = (len(feeds), len(cots))
     piece = up.shape[1] // GROUP
     every = pl.BlockSpec(memory_space=pl.ANY)
-    outs = [((4 * rows, width), HALF)] * 2 + [((4 * rows, piece), HALF)] * 2
+    shape = (devices // 2, width // devices, piece)
+    fixed = [
+        (shape, SINGLE), (shape, SINGLE), ((total, width), HALF), ((total, width), HALF),
+        ((far, piece), SINGLE),
+    ]
     return call(
-        wide_body,
-        "wide",
-        (1,),
+        functools.partial(down_side_body, counts=counts),
+        "down_side",
+        (width // WIDE,),
         [(a, every) for a in feeds + cots]
         + [
-            (up, pl.BlockSpec((width, piece), lambda at, m: (0, m[0]))),
-            (down, pl.BlockSpec((piece, width), lambda at, m: (m[0], 0))),
+            (up, pl.BlockSpec((width, piece), lambda at, m, p: (0, m[0]))),
+            whole(low),
+            whole(cot),
+            (hidden, pl.BlockSpec((rows, piece), lambda at, m, p: (0, m[0]))),
         ],
-        [(s, d, pl.BlockSpec(s, lambda at, m: (0, 0))) for s, d in outs],
+        [(s, d, whole(jax.ShapeDtypeStruct(s, d))[1]) for s, d in fixed],
         scratch=[
-            pltpu.VMEM((4, rows, width), SINGLE),
-            pltpu.VMEM((4, rows, width), SINGLE),
-            pltpu.SemaphoreType.DMA((2, 4)),
+            pltpu.VMEM((total, piece), HALF),
+            pltpu.VMEM((far, width), SINGLE),
+            pltpu.VMEM((far, width), SINGLE),
+            pltpu.SemaphoreType.DMA((2, max(counts))),
         ],
-        prefetch=(member,),
-        flops=4 * 4 * rows * width * piece,
-    )
-
-
-def wide_grad_body(order_ref, place_ref, fl_ref, cl_ref, hid_ref, gp_ref, out_ref):
-    share = out_ref.shape[1]
-    piece = gp_ref.shape[1]
-    block = order_ref[pl.program_id(0)]
-    up = dot(fl_ref[...], gp_ref[...], 0, 0)
-    down = dot(cl_ref[...], hid_ref[...], 0, 0)
-    per = LANES // share
-    for at in range(per):
-        rows = slice(at * share, (at + 1) * share)
-        spot = place_ref[block * per + at]
-        out_ref[spot, :, :piece] = up[rows]
-        out_ref[spot, :, piece:] = down[rows]
-
-
-def wide_grad(order, place, fl, cl, hid, gp, devices):
-    rows, width = fl.shape
-    piece = gp.shape[1]
-    blocks = order.shape[0]
-    share = width // devices
-    count = blocks * LANES // share
-    column = pl.BlockSpec((rows, LANES), lambda at, o, p: (0, o[at]))
-    shape = (count, share, 2 * piece)
+        prefetch=(member, place),
+    )
+
+
+def up_side_body(
+    member_ref, place_ref, fl_ref, cl_ref, slope_ref, down_ref, own_ref, leave_ref, keep_ref, gp_ref
+):
+    far = slope_ref.shape[0]
+    third = far // 3
+
+    @pl.when(pl.program_id(0) == 0)
+    def _():
+        for at in range(3):
+            here = slice(at * third, (at + 1) * third)
+            grad = slope_ref[here] * dot(cl_ref[here], down_ref[...], 1, 1)
+            gp_ref[here] = grad.astype(HALF)
+        gp_ref[far:] = own_ref[...]
+
+    put_shares(dot(fl_ref[...], gp_ref[...], 0, 0), place_ref, leave_ref, keep_ref)
+
+
+def up_side(member, place, fl, cl, slope, down, grad, devices):
+    total, width = fl.shape
+    far, piece = slope.shape
+    rows = total - far
+    shape = (devices // 2, width // devices, piece)
+    spec = pl.BlockSpec(shape, lambda at, m, p: (0, 0, 0))
     return call(
-        wide_grad_body,
-        "wide_grad",
-        (blocks,),
-        [(fl, column), (cl, column), whole(hid), whole(gp)],
-        [(shape, SINGLE, pl.BlockSpec(shape, lambda at, o, p: (0, 0, 0)))],
-        prefetch=(order, place),
-        flops=4 * rows * blocks * LANES * piece,
-    )[0]
+        up_side_body,
+        "up_side",
+        (width // WIDE,),
+        [
+            (fl, pl.BlockSpec((total, WIDE), lambda at, m, p: (0, at))),
+            (cl, pl.BlockSpec((far, width), lambda at, m, p: (0, 0))),
+            whole(slope),
+            (down, pl.BlockSpec((piece, width), lambda at, m, p: (m[0], 0))),
+            (grad, pl.BlockSpec((rows, piece), lambda at, m, p: (0, m[0]))),
+        ],
+        [(shape, SINGLE, spec), (shape, SINGLE, spec)],
+        scratch=[pltpu.VMEM((total, piece), HALF)],
+        prefetch=(member, place),
+    )
 
 
 def back_body(
@@ -465,49 +526,71 @@
     vec_ref[3] += row_sums(upstream)
 
 
-def inputs_back(gkv, gkv_far, gq, gq_far, media, mean, inv, latents, gm, wq, wk, wv, far, mg, lg):
+def inputs_back(first, count, held, gkv, gkv_far, gq, gq_far, media, mean, inv, latents, gm, weights):
     images, patches, width = media.shape
-    inner = wq.shape[1]
+    inner = weights[0].shape[1]
     vec = (4, 8, width)
+
+    def image(array):
+        rest = (0,) * (array.ndim - 1)
+        return pl.BlockSpec((1,) + array.shape[1:], lambda at: (at + first,) + rest)
+
+    arrays = (gkv, gkv_far, gq, gq_far, media, mean, inv, latents, gm)
+    ins = [(a, image(a)) for a in arrays] + [whole(a) for a in weights]
+    ins += [(a, pl.BlockSpec(memory_space=pl.ANY)) for a in held]
+    body = inputs_body
+    if held:
+        def body(*refs):
+            inputs_body(*refs[: len(arrays) + len(weights)], *refs[len(ins) :])
+
     return call(
-        inputs_body,
+        body,
         "inputs_back",
-        (images,),
-        [(a, by_image(a.shape)) for a in (gkv, gkv_far, gq, gq_far, media, mean, inv, latents, gm)]
-        + [whole(a) for a in (wq, wk, wv, far, mg, lg)],
+        (count,),
+        ins,
         [
-            (media.shape, HALF, by_image(media.shape)),
-            (latents.shape, HALF, by_image(latents.shape)),
+            (media.shape, HALF, image(media)),
+            (latents.shape, HALF, image(latents)),
             (vec, SINGLE, pl.BlockSpec(vec, lambda at: (0, 0, 0))),
         ],
         scratch=[pltpu.VMEM((width, 4 * inner), HALF), pltpu.VMEM((width, 2 * inner), HALF)],
-        flops=8 * images * patches * width * inner,
+        flops=8 * count * patches * width * inner,
+        aliases={len(ins) - len(held) + i: i for i in range(len(held))},
     )
 
 
 def place_body(member_ref, *refs):
-    blocks, (up_ref, down_ref) = refs[:GROUP], refs[GROUP:]
-    piece = blocks[0].shape[1] // 2
+    blocks, out_ref = refs[:GROUP], refs[GROUP]
+    piece = blocks[0].shape[1]
     for step in range(GROUP):
         spot = member_ref[0] ^ step
-        up_ref[:, pl.ds(pl.multiple_of(spot * piece, piece), piece)] = blocks[step][:, :piece]
-        down_ref[pl.ds(pl.multiple_of(spot * piece, piece), piece), :] = blocks[step][:, piece:].T
+        out_ref[:, pl.ds(pl.multiple_of(spot * piece, piece), piece)] = blocks[step][...]
 
 
 def place_pieces(member, blocks):
-    share, both = blocks[0].shape
-    wide_ = both // 2 * GROUP
+    share, piece = blocks[0].shape
+    shape = (share, piece * GROUP)
     return call(
         place_body,
         "place_pieces",
         (1,),
         [whole(b) for b in blocks],
-        [
-            ((share, wide_), SINGLE, pl.BlockSpec((share, wide_), lambda at, m: (0, 0))),
-            ((wide_, share), SINGLE, pl.BlockSpec((wide_, share), lambda at, m: (0, 0))),
-        ],
+        [(shape, SINGLE, pl.BlockSpec(shape, lambda at, m: (0, 0)))],
         prefetch=(member,),
-    )
+    )[0]
+
+
+def after(array, *others):
+    return lax.optimization_barrier((array,) + others)[0]
+
+
+def plan(bits):
+    if bits == 4:
+        return (0, 3), ([1, 2], [2, 1]), ([0, 3, 2, 1], [2, 0, 1, 3])
+    top = bits - 1
+    rest = list(range(2, top - 1))
+    wide_ = ([top, top - 1] + rest, [top - 1, top] + rest)
+    return (0, 1), wide_, (list(range(bits)), [1, 0] + list(range(2, bits)))
 
 
 class Links:
@@ -527,34 +610,27 @@
             pairs.append((2 * row + 1, 2 * (row ^ step_one) + 1))
         return lax.ppermute(array, ("dp", "tensor"), pairs)
 
-    def places(self, orders, tail):
+    def bit(self, which):
+        return (self.row >> which) & 1
+
+    def places(self, orders, group):
         apart = jnp.arange(self.devices, dtype=jnp.int32) ^ self.row
         found = []
         for order in orders:
             spot = jnp.zeros_like(apart)
             for which in order:
                 spot = 2 * spot + 1 - ((apart >> which) & 1)
-            found.append(spot * (1 << tail) + apart % (1 << tail))
+            for which in reversed(group):
+                spot = 2 * spot + ((apart >> which) & 1)
+            found.append(spot)
         return jnp.where(self.core == 0, found[0], found[1])
 
-    def reduce(self, leave, keep, orders):
-        for step, (zero, one) in enumerate(zip(*orders)):
-            come = self.send(leave, 1 << zero, 1 << one)
-            if step == len(orders[0]) - 1:
-                return keep + come
-            half = keep.shape[0] // 2
-            leave, keep = keep[:half] + come[:half], keep[half:] + come[half:]
-
-    def gather(self, own):
-        near = self.send(own, 1, 2)
-        pair = jnp.concatenate([own, near], 0)
-        far = self.send(pair, 2, 1)
-        return [pair, far, self.swap(pair), self.swap(far)]
-
-    def total(self, array):
-        for at in range(self.bits):
-            array = array + self.send(array, 1 << at, 1 << at)
-        return array
+    def stage(self, leave, orders, step):
+        return self.send(leave, 1 << orders[0][step], 1 << orders[1][step])
+
+    def halve(self, come, keep):
+        half = keep.shape[0] // 2
+        return keep[:half] + come[:half], keep[half:] + come[half:]
 
 
 def local(
@@ -572,45 +648,75 @@
     vectors = [v.reshape(1, width) for v in (media_gain, media_bias, latent_gain, latent_bias)]
     gain, bias = feed_gain.reshape(1, width), feed_bias.reshape(1, width)
     core = links.core.reshape(1)
-    member = (links.row % GROUP).reshape(1)
+    bits = links.bits
+    group, wide_orders, small_orders = plan(bits)
+    near_bit, far_bit = 1 << group[0], 1 << group[1]
+    member = (links.bit(group[0]) + 2 * links.bit(group[1])).reshape(1)
 
     cot = cotangent.reshape(rows, width)
     half = rows // 2
-    cots = links.gather(
-        lax.dynamic_slice_in_dim(cot, links.core * half, half, 0).astype(SINGLE)
-    )
-    weights_far = links.swap(
-        jnp.concatenate([query_weight, key_weight, value_weight], 1).astype(SINGLE)
-    )
+    cot_own = lax.dynamic_slice_in_dim(cot, links.core * half, half, 0).astype(SINGLE)
+    cot_far = links.send(cot_own, far_bit, far_bit)
     kv, q, k, v, probs, attended, branch, mean, inv = attend(
         buckets, media, latents, query_weight, key_weight, value_weight, output_weight, vectors
     )
+    branch, cot_own, cot_far = lax.optimization_barrier((branch, cot_own, cot_far))
     branch = branch.reshape(rows, width)
-    middle, low, low_send = call(
+    cot_near = links.send(cot_own, near_bit, near_bit)
+    cot_far_other = links.swap(cot_far)
+    branch_far = links.swap(branch)
+    weights_send = jnp.concatenate(
+        [after(query_weight, branch), key_weight, value_weight], 1
+    ).astype(SINGLE)
+    middle, low, low_send, low_first, low_second = call(
         middle_body,
         "middle",
         (1,),
-        [whole(a) for a in (latents.reshape(rows, width), branch, links.swap(branch), gain, bias)],
+        [
+            whole(a)
+            for a in (
+                latents.reshape(rows, width),
+                after(branch, weights_send),
+                branch_far,
+                gain,
+                bias,
+            )
+        ],
         [
             ((rows, width), SINGLE, pl.BlockSpec((rows, width), lambda at, c: (0, 0))),
             ((rows, width), HALF, pl.BlockSpec((rows, width), lambda at, c: (0, 0))),
             ((half, width), SINGLE, pl.BlockSpec((half, width), lambda at, c: (0, 0))),
-        ],
+        ]
+        + [((half // 2, width), SINGLE, pl.BlockSpec((half // 2, width), lambda at, c: (0, 0)))] * 2,
         prefetch=(core,),
     )
-    feeds = links.gather(low_send)
-    hidden, part = feed(low, cot, up_weight, down_weight)
+    low, low_send, low_first, cot_near, weights_send = lax.optimization_barrier(
+        (low, low_send, low_first, cot_near, weights_send, cot_far_other)
+    )[:5]
+    low_far_a = links.send(low_first, far_bit, far_bit)
+    low_near = links.send(low_send, near_bit, near_bit)
+    cot_near_other = links.swap(cot_near)
+    weights_far = links.swap(weights_send)
+    hidden, grad_pre, part, feed_out = feed(low, cot, up_weight, down_weight)
+    part, low_far_a, low_near, cot_far, low_second = lax.optimization_barrier(
+        (part, low_far_a, low_near, cot_far, low_second, weights_far, cot_near_other)
+    )[:5]
+    part_far = links.swap(part)
+    low_far_b = links.send(low_second, far_bit, far_bit)
+    low_both_a = links.send(low_far_a, near_bit, near_bit)
+    low_far_a_other = links.swap(low_far_a)
+    cot_both = links.send(cot_far, near_bit, near_bit)
     grad_middle, grad_branch, gkv, gkv_send, gq, gq_send, feed_vec = back(
-        middle, part, links.swap(part), cot, gain, output_weight, q, k, v, probs
-    )
-    gkv_far, gq_far = links.swap(gkv_send), links.swap(gq_send)
-
-    bits = links.bits
-    orders = [list(range(bits)), [1, 0] + list(range(2, bits))]
-    if bits >= 4:
-        orders[1][2:4] = [3, 2]
-    leave, keep = small_grad(
-        links.places(orders, 0),
+        middle, part, part_far, cot, gain, output_weight, q, k, v, probs
+    )
+    grad_branch, gkv_send, low_far_b, low_both_a, low_near, cot_both = lax.optimization_barrier(
+        (grad_branch, gkv_send, low_far_b, low_both_a, low_near, cot_both, low_far_a_other)
+    )[:6]
+    low_both_b = links.send(low_far_b, near_bit, near_bit)
+    low_far_b_other, low_both_a_other = links.swap(low_far_b), links.swap(low_both_a)
+    gkv_far, low_near_other = links.swap(gkv_send), links.swap(low_near)
+    small_leave, small_keep = small_grad(
+        links.places(small_orders, ()),
         kv.reshape(images * keys_all, width),
         grad_branch,
         gkv.reshape(images * keys_all, 2 * inner),
@@ -620,37 +726,90 @@
         images,
         patches,
     )
-    small = links.reduce(leave, keep, orders)[0]
-
-    fl, cl, hid, gp = wide(member, feeds, cots, up_weight, down_weight)
-    top = bits - 1
-    rest = list(range(2, top - 1))
-    orders = [[top, top - 1] + rest, [top - 1, top] + rest]
-    place = links.places(orders, 2)
-    which = jnp.where(links.core == 0, top, top - 1)
-    mine = (links.row >> which) & 1
-    held = width // LANES // 2
-    at = which - (bits - held.bit_length())
-    rank = jnp.arange(held, dtype=jnp.int32)
-    order = ((rank >> at) << (at + 1)) + (rank & ((1 << at) - 1))
-    count = devices // 2
-    leave = wide_grad(order + ((1 - mine) << at), place % count, fl, cl, hid, gp, devices)
-    keep = wide_grad(order + (mine << at), place % count, fl, cl, hid, gp, devices)
-    mixed = links.reduce(leave, keep, orders)
-    pieces = [mixed[0]] + [links.send(mixed[s], s, s) for s in range(1, GROUP)]
-    grad_up, grad_down = place_pieces(member, pieces)
-
+    small_leave, feed_out, gq_send, low_both_b, cot_both = lax.optimization_barrier(
+        (
+            small_leave, feed_out, gq_send, low_both_b, cot_both,
+            low_far_b_other, low_both_a_other, gkv_far, low_near_other,
+        )
+    )[:5]
+    low_both_b_other, cot_both_other = links.swap(low_both_b), links.swap(cot_both)
+    small_come = links.stage(small_leave, small_orders, 0)
+    gq_far, feed_far = links.swap(gq_send), links.swap(feed_out)
+    place = links.places(wide_orders, group)
+    down_leave, down_keep, fl, cl, slope = down_side(
+        member,
+        place,
+        [
+            low_near, low_near_other, low_far_a, low_far_b, low_far_a_other, low_far_b_other,
+            low_both_a, low_both_b, low_both_a_other, low_both_b_other,
+        ],
+        [cot_near, cot_near_other, cot_far, cot_far_other, cot_both, cot_both_other],
+        up_weight,
+        low,
+        cot,
+        hidden,
+        devices,
+    )
+    down_come = links.stage(down_leave, wide_orders, 0)
+    up_leave, up_keep = up_side(
+        member, place, fl, cl, slope, down_weight, after(grad_pre, down_leave), devices
+    )
+    up_come = links.stage(up_leave, wide_orders, 0)
+    small_leave, small_keep = links.halve(
+        small_come, after(small_keep, up_leave, gq_far, feed_far)
+    )
+    small_come = links.stage(small_leave, small_orders, 1)
     grad_media, grad_latents, vec = inputs_back(
-        gkv, gkv_far, gq, gq_far, media, mean, inv, latents,
+        0,
+        images,
+        (),
+        after(gkv, small_leave),
+        gkv_far,
+        gq,
+        gq_far,
+        media,
+        mean,
+        inv,
+        latents,
         grad_middle.reshape(images, latent_rows, width),
-        query_weight, key_weight, value_weight, weights_far, vectors[0], vectors[2],
+        (query_weight, key_weight, value_weight, weights_far, vectors[0], vectors[2]),
     )
     vec = jnp.sum(jnp.concatenate([vec, feed_vec], 0), 1)
-    vec = links.total(jnp.concatenate([vec, jnp.zeros((2, width), SINGLE)], 0))
+    vec = jnp.concatenate([vec, jnp.zeros((2, width), SINGLE)], 0)
+    vec_steps = [1 << at for at in reversed(range(bits))]
+
+    steps = len(wide_orders[0])
+    done = vec
+    for step in range(steps - 1):
+        down_leave, down_keep = links.halve(down_come, after(down_keep, done))
+        down_come = links.stage(down_leave, wide_orders, step + 1)
+        up_leave, up_keep = links.halve(up_come, after(up_keep, down_leave))
+        up_come = links.stage(up_leave, wide_orders, step + 1)
+        done = up_leave
+    vec_come = links.send(after(vec, done), vec_steps[0], vec_steps[0])
+    for step in range(2, bits):
+        small_leave, small_keep = links.halve(small_come, after(small_keep, done))
+        small_come = links.stage(small_leave, small_orders, step)
+        done = small_leave
+        vec = after(vec, done) + vec_come
+        vec_come = links.send(vec, vec_steps[step - 1], vec_steps[step - 1])
+        if step == 2:
+            result = (after(middle, done) + (feed_out + feed_far)).astype(HALF)
+            done = result
+            hops = [near_bit * (at & 1) + far_bit * (at >> 1) for at in range(GROUP)]
+            mixed = after(down_keep, result) + down_come
+            down_pieces = [mixed[0]] + [links.send(mixed[at], hops[at], hops[at]) for at in range(1, GROUP)]
+            done = mixed
+    mixed = after(up_keep, done) + up_come
+    up_pieces = [mixed[0]] + [links.send(mixed[at], hops[at], hops[at]) for at in range(1, GROUP)]
+    vec = after(vec, mixed) + vec_come
+    vec = vec + links.send(vec, vec_steps[-1], vec_steps[-1])
     vec = lax.dynamic_slice_in_dim(vec, links.row * share, share, 1)
-
-    feed_out = dot(hidden, down_weight)
-    result = (middle + (feed_out + links.swap(feed_out))).astype(HALF)
+    small = (after(small_keep, vec) + small_come)[0]
+    down_pieces[0] = after(down_pieces[0], small)
+    grad_down = place_pieces(member, down_pieces)
+    up_pieces[0] = after(up_pieces[0], grad_down)
+    grad_up = place_pieces(member, up_pieces)
     return (
         result.reshape(latents.shape),
         grad_media,
@@ -660,7 +819,7 @@
         small[:, inner : 2 * inner],
         small[:, 3 * inner :].T,
         grad_up,
-        grad_down,
+        grad_down.T,
     ) + tuple(vec[at] for at in range(6))
 
 

time: 227 us -> 206 us (0.907)
  waiting for transfers between devices: 66 us -> 45 us
    ppermute x17 -> x26, waiting for transfers between devices: 62.7 us -> 42 us  [send(): return lax.ppermute(array, ('dp', 'tensor'), pairs)]
    ppermute x17 -> x26, starting transfers between devices: 33.4 us -> 34.4 us  [send(): return lax.ppermute(array, ('dp', 'tensor'), pairs)]
    unnamed x42 -> x56, local copies, waits for them, and re-layouts: 5.13 us -> 4.51 us
  transfers between devices with their start and end apart: 27 -> 40, of which waited for: 11 -> 12; matrix products, arithmetic and copies ran while one was open for 12% -> 11% of each run, Pallas kernels for 30% -> 45%
where the time goes in v3:
time: 206 us; the launch traced here: 204 us
  Pallas kernels  93.9 us (46%)
  waiting for transfers between devices  45 us (22%)
  starting transfers between devices  37 us (18%)
  other arithmetic  19.8 us (10%)
  local copies, waits for them, and re-layouts  7.16 us (3%)
    pallas_call x10, Pallas kernels, call(): pl.pallas_call(body, out_shape=shapes, grid_spec=pltpu.PrefetchScalarGrid...  93.9 us
    ppermute x26, waiting for transfers between devices, send(): return lax.ppermute(array, ('dp', 'tensor'), pairs)  42 us
    ppermute x26, starting transfers between devices, send(): return lax.ppermute(array, ('dp', 'tensor'), pairs)  34.4 us
    add x5, other arithmetic, halve(): return (keep[:half] + come[:half], keep[half:] + come[half:])  11 us
    unnamed x56, local copies, waits for them, and re-layouts  4.51 us
  transfers between devices with their start and end apart: 40, of which 12 were waited for; matrix products, arithmetic and copies ran while one was open for 11% of the time, Pallas kernels for 45%

profile of v3, /device:TPU:0, one launch (start us, length us, event | category | flops | bytes accessed | tf_op | source)
XLA Modules:
  0.0 203.9 jit_solution(14180032652525102639)
XLA Ops:
  0.6 1.0 dynamic-slice_convert_fusion
  1.7 4.1 %collective-permute-start = (f32[128,1024]{1,0:T(8,128)S(1)}, f32[128,1024]{1,0:T(8,128)S(1)}, u32[]{:S(2)}, u32[]{:S(2)}) collective-permute-start(f32[128,1024]{1,0:T(8,128)S(1)} %dynamic-slice_convert_fusion), channel_id=1, source_target_pairs={{0,16},{1,17},{2,18},{3,19},{4,20},{5,21},{6,22},{7,23},{8,24},{9,... | collective-permute-start | bytes 1572872 | tf_op jit(solution)/shard_map/ppermute | solution.py:611
  5.8 14.4 %attend.1 = (bf16[4,640,1024]{2,1,0:T(8,128)(2,1)}, bf16[4,64,256]{2,1,0:T(8,128)(2,1)}, bf16[4,640,256]{2,1,0:T(8,128)(2,1)}, bf16[4,640,256]{2,1,0:T(8,128)(2,...) custom-call(s32[4]{0:T(128)} %buckets_ref.1, ...), custom_call_target="tpu_custom_call" | custom-call | flops 3355443200 | bytes 19171328 | tf_op jit(solution)/shard_map/attend/pallas_call | solution.py:73
  20.2 8.7 %collective-permute-done.refs_12_ = f32[128,1024]{1,0:T(8,128)S(1)} collective-permute-done((f32[128,1024]{1,0:T(8,128)S(1)}, f32[128,1024]{1,0:T(8,128)S(1)}, u32[]{:S(2)}, u32[]{:S(2)}) %collective-permute-start) | collective-permute-done | bytes 524320 | tf_op jit(solution)/shard_map/ppermute | solution.py:611
  29.0 1.5 collective-permute-start.2
  30.7 1.9 maximum_convert_fusion
  32.6 1.0 copy-done.10
  33.7 3.7 %middle.1 = (f32[256,1024]{1,0:T(8,128)}, bf16[256,1024]{1,0:T(8,128)(2,1)}, f32[128,1024]{1,0:T(8,128)}, f32[64,1024]{1,0:T(8,128)}, f32[64,1024]{1,0:T(8,128)}) custom-call(s32[1]{0:T(128)} %bitcast.core_ref, bf16[256,1024]{1,0:T(8,128)(2,1)} %bitcast.55, f32[256,1024]{1,0:T(8,128)} %bitcast.58, f32[256,1024]{1,0:T(8,128)} %copy-done.10, ...), custom_call_target="tpu_custom_call" | custom-call | bytes 5251072 | tf_op jit(solution)/shard_map/middle/pallas_call | solution.py:73
  37.4 6.2 %collective-permute-done.2.refs_10_ = f32[128,1024]{1,0:T(8,128)} collective-permute-done((f32[128,1024]{1,0:T(8,128)}, f32[128,1024]{1,0:T(8,128)}, u32[]{:S(2)}, u32[]{:S(2)}) %collective-permute-start.2) | collective-permute-done | bytes 524320 | tf_op jit(solution)/shard_map/ppermute | solution.py:611
  43.6 1.6 collective-permute-start.5
  45.4 10.1 %feed.1 = (bf16[256,2048]{1,0:T(8,128)(2,1)}, bf16[256,2048]{1,0:T(8,128)(2,1)}, f32[256,1024]{1,0:T(8,128)}, f32[256,1024]{1,0:T(8,128)}) custom-call(bf16[256,1024]{1,0:T(8,128)(2,1)} %get-tuple-element.106.low_ref.refs_17_, bf16[256,1024]{1,0:T(8,128)(2,1)} %bitcast.51, bf16[1024,2048]{1,0:T(8,128)(2,1)} %refs_16_.1, bf16[2048,1024]{1,0:T(8,128)(2,1)} %down_ref.3), custom_call_target="tpu_custom_call" | custom-call | flops 4294967296 | bytes 13631488 | tf_op jit(solution)/shard_map/feed/pallas_call | solution.py:73
  55.5 5.1 %collective-permute-done.4.refs_2_ = f32[64,1024]{1,0:T(8,128)S(1)} collective-permute-done((f32[64,1024]{1,0:T(8,128)}, f32[64,1024]{1,0:T(8,128)S(1)}, u32[]{:S(2)}, u32[]{:S(2)}) %collective-permute-start.4) | collective-permute-done | bytes 262176 | tf_op jit(solution)/shard_map/ppermute | solution.py:611
  61.5 1.5 collective-permute-start.10
  63.8 10.5 %back.1 = (f32[256,1024]{1,0:T(8,128)}, bf16[256,1024]{1,0:T(8,128)(2,1)}, bf16[4,640,512]{2,1,0:T(8,128)(2,1)}, f32[4,640,512]{2,1,0:T(8,128)}, bf16[4,64,256]{...) custom-call(f32[256,1024]{1,0:T(8,128)} %get-tuple-element.162.mid_ref, ...), custom_call_target="tpu_custom_call" | custom-call | flops 1677721600 | bytes 19468288 | tf_op jit(solution)/shard_map/back/pallas_call | solution.py:73
  74.3 1.7 collective-permute-done.9.refs_3_
  76.0 5.0 %collective-permute-done.10.refs_6_ = f32[64,1024]{1,0:T(8,128)} collective-permute-done((f32[64,1024]{1,0:T(8,128)S(1)}, f32[64,1024]{1,0:T(8,128)}, u32[]{:S(2)}, u32[]{:S(2)}) %collective-permute-start.10) | collective-permute-done | bytes 262176 | tf_op jit(solution)/shard_map/ppermute | solution.py:611
  83.1 11.4 %small_grad.1 = (f32[8,64,1024]{2,1,0:T(8,128)}, f32[8,64,1024]{2,1,0:T(8,128)}) custom-call(s32[16]{0:T(128)} %broadcast_select_fusion.1.place_ref, bf16[2560,1024]{1,0:T(8,128)(2,1)} %bitcast.71, bf16[256,1024]{1,0:T(8,128)(2,1)} %get-tuple-element.124.gb_ref, bf16[2560,512]{1,0:T(8,128)(2,1)} %bitcast.54, bf16[256,256]{1,0:T(8,128)(2,1)} %bitcast.61, ...), custom_call_target="tpu_custom_call" | custom-call | flops 2684354560 | bytes 12845056 | tf_op jit(solution)/shard_map/small_grad/pallas_call | solution.py:73
  94.6 1.6 collective-permute-start.22
  97.7 2.2 %collective-permute-done.18.refs_9_ = f32[64,1024]{1,0:T(8,128)S(1)} collective-permute-done((f32[64,1024]{1,0:T(8,128)S(1)}, f32[64,1024]{1,0:T(8,128)S(1)}, u32[]{:S(2)}, u32[]{:S(2)}) %collective-permute-start.18) | collective-permute-done | bytes 262176 | tf_op jit(solution)/shard_map/ppermute | solution.py:604
  100.8 11.1 %down_side.1 = (f32[8,64,512]{2,1,0:T(8,128)}, f32[8,64,512]{2,1,0:T(8,128)}, bf16[1024,1024]{1,0:T(8,128)(2,1)}, bf16[1024,1024]{1,0:T(8,128)(2,1)}, f32[768,512]{1,0:T(8,128)}) custom-call(s32[1]{0:T(128)} %bitcast.14.member_ref, s32[16]{0:T(128)} %broadcast_select_fusion.place_ref, f32[128,1024]{1,0:T(8,128)} %collective-permute-done.5.refs_0_, ...), custom_call_target="tpu_custom_call" | custom-call | bytes 20447232 | tf_op jit(solution)/shard_map/down_side/pallas_call | solution.py:73
  111.9 1.6 collective-permute-start.23
  113.5 8.3 %up_side.1 = (f32[8,64,512]{2,1,0:T(8,128)}, f32[8,64,512]{2,1,0:T(8,128)}) custom-call(s32[1]{0:T(128)} %bitcast.14.member_ref, s32[16]{0:T(128)} %broadcast_select_fusion.place_ref, bf16[1024,1024]{1,0:T(8,128)(2,1)} %get-tuple-element.140.fl_ref, bf16[1024,1024]{1,0:T(8,128)(2,1)} %get-tuple-element.141.cl_ref, f32[768,512]{1,0:T(8,128)} %get-tuple-element.142.slope_ref, ...), custom_call_target="tpu_custom_call" | custom-call | bytes 13107200 | tf_op jit(solution)/shard_map/up_side/pallas_call | solution.py:73
  122.3 3.0 %slice_add_fusion.1 = (f32[4,64,1024]{2,1,0:T(8,128)S(1)}, f32[4,64,1024]{2,1,0:T(8,128)}) fusion(f32[8,64,1024]{2,1,0:T(8,128)} %collective-permute-done.22, f32[8,64,1024]{2,1,0:T(8,128)S(1)} %copy-done.2), kind=kLoop, calls=%fused_computation.2 | loop fusion | flops 524288 | bytes 6291456 | tf_op jit(solution)/shard_map/add | solution.py:633
  125.9 20.5 %inputs_back.1 = (bf16[4,576,1024]{2,1,0:T(8,128)(2,1)}, bf16[4,64,1024]{2,1,0:T(8,128)(2,1)}, f32[4,8,1024]{2,1,0:T(8,128)}) custom-call(bf16[4,640,512]{2,1,0:T(8,128)(2,1)} %get-tuple-element.153.gkv_ref, f32[4,640,512]{2,1,0:T(8,128)} %collective-permute-done.17.gkv_far_ref, bf16[4,64,256]{2,1,0:T(8,128)(2,1)} %get-tuple-element.126.gq_ref, ...), custom_call_target="tpu_custom_call" | custom-call | flops 4831838208 | bytes 24668160 | tf_op jit(solution)/shard_map/inputs_back/pallas_call | solution.py:73
  146.4 1.0 maximum_reduce_fusion
  147.5 2.2 %slice_add_fusion.3 = (f32[4,64,512]{2,1,0:T(8,128)S(1)}, f32[4,64,512]{2,1,0:T(8,128)}) fusion(f32[8,64,512]{2,1,0:T(8,128)} %collective-permute-done.23, f32[8,64,512]{2,1,0:T(8,128)S(1)} %copy-done.8), kind=kLoop, calls=%fused_computation.5 | loop fusion | flops 262144 | bytes 3145728 | tf_op jit(solution)/shard_map/add | solution.py:633
  149.7 1.2 collective-permute-start.26
  150.9 2.3 %slice_add_fusion.2 = (f32[4,64,512]{2,1,0:T(8,128)S(1)}, f32[4,64,512]{2,1,0:T(8,128)}) fusion(f32[8,64,512]{2,1,0:T(8,128)} %collective-permute-done.24, f32[8,64,512]{2,1,0:T(8,128)S(1)} %copy-done.9), kind=kLoop, calls=%fused_computation.4 | loop fusion | flops 262144 | bytes 3145728 | tf_op jit(solution)/shard_map/add | solution.py:633
  153.3 2.3 %slice_add_fusion.4 = (f32[2,64,1024]{2,1,0:T(8,128)}, f32[2,64,1024]{2,1,0:T(8,128)}) fusion(f32[4,64,1024]{2,1,0:T(8,128)} %collective-permute-done.25, f32[4,64,1024]{2,1,0:T(8,128)S(1)} %get-tuple-element.161), kind=kLoop, calls=%fused_computation.6 | loop fusion | flops 262144 | bytes 3145728 | tf_op jit(solution)/shard_map/add | solution.py:633
  155.6 0.8 collective-permute-start.27
  156.4 1.2 collective-permute-start.30
  157.6 1.2 collective-permute-start.28
  158.8 2.5 %add_convert_fusion = bf16[256,1024]{1,0:T(8,128)(2,1)} fusion(f32[256,1024]{1,0:T(8,128)S(1)} %copy-done, f32[256,1024]{1,0:T(8,128)} %get-tuple-element.148, f32[256,1024]{1,0:T(8,128)} %collective-permute-done.21), kind=kLoop, calls=%fused_computation.3 | loop fusion | flops 786432 | bytes 3670016 | tf_op jit(solution)/shard_map/convert_element_type | solution.py:797
  161.4 1.1 add.124
  162.5 7.6 %collective-permute-done.28 = f32[8,1024]{1,0:T(8,128)S(1)} collective-permute-done((f32[8,1024]{1,0:T(8,128)S(1)}, f32[8,1024]{1,0:T(8,128)S(1)}, u32[]{:S(2)}, u32[]{:S(2)}) %collective-permute-start.28) | collective-permute-done | bytes 32800 | tf_op jit(solution)/shard_map/ppermute | solution.py:611
  170.1 3.7 %collective-permute-start.29 = (f32[8,1024]{1,0:T(8,128)S(1)}, f32[8,1024]{1,0:T(8,128)S(1)}, u32[]{:S(2)}, u32[]{:S(2)}) collective-permute-start(f32[8,1024]{1,0:T(8,128)S(1)} %add.126), channel_id=1, source_target_pairs={{0,8},{1,9},{2,10},{3,11},{4,12},{5,13},{6,14},{7,15},{8,0},{9,1},... | collective-permute-start | bytes 98312 | tf_op jit(solution)/shard_map/ppermute | solution.py:611
  173.8 1.1 slice_add_fusion.8
  174.9 0.8 collective-permute-done.29
  175.7 1.8 collective-permute-start.31
  178.2 2.7 %collective-permute-start.36 = (f32[64,512]{1,0:T(8,128)S(1)}, f32[64,512]{1,0:T(8,128)S(1)}, u32[]{:S(2)}, u32[]{:S(2)}) collective-permute-start(f32[64,512]{1,0:T(8,128)S(1)} %get-tuple-element.189), channel_id=1, source_target_pairs={{0,18},{1,19},{2,16},{3,17},{4,22},{5,23},{6,20},{7,21},{8,26},{9,... | collective-permute-start | bytes 393224 | tf_op jit(solution)/shard_map/ppermute | solution.py:611
  180.9 1.7 collective-permute-start.34
  182.9 1.0 collective-permute-start.32
  184.6 2.3 %collective-permute-done.32 = f32[8,1024]{1,0:T(8,128)S(1)} collective-permute-done((f32[8,1024]{1,0:T(8,128)S(1)}, f32[8,1024]{1,0:T(8,128)S(1)}, u32[]{:S(2)}, u32[]{:S(2)}) %collective-permute-start.32) | collective-permute-done | bytes 32800 | tf_op jit(solution)/shard_map/ppermute | solution.py:611
  186.9 3.4 %collective-permute-start.39 = (f32[64,512]{1,0:T(8,128)S(1)}, f32[64,512]{1,0:T(8,128)S(1)}, u32[]{:S(2)}, u32[]{:S(2)}) collective-permute-start(f32[64,512]{1,0:T(8,128)S(1)} %get-tuple-element.185), channel_id=1, source_target_pairs={{0,18},{1,19},{2,16},{3,17},{4,22},{5,23},{6,20},{7,21},{8,26},{9,... | collective-permute-start | bytes 393224 | tf_op jit(solution)/shard_map/ppermute | solution.py:611
  191.0 1.3 collective-permute-start.37
  193.7 1.9 place_pieces.2
  196.3 3.9 %collective-permute-done.39.refs_3_ = f32[64,512]{1,0:T(8,128)S(1)} collective-permute-done((f32[64,512]{1,0:T(8,128)S(1)}, f32[64,512]{1,0:T(8,128)S(1)}, u32[]{:S(2)}, u32[]{:S(2)}) %collective-permute-start.39) | collective-permute-done | bytes 131104 | tf_op jit(solution)/shard_map/ppermute | solution.py:611
  202.0 1.9 place_pieces.3
  (121 shorter events, 13.7 us)
Async XLA Ops:
  1.7 18.6 %copy-start.14 = (f32[128,1024]{1,0:T(8,128)}, f32[128,1024]{1,0:T(8,128)S(1)}, u32[]{:S(2)}) copy-start(f32[128,1024]{1,0:T(8,128)S(1)} %dynamic-slice_convert_fusion) | copy-start | bytes 1572868
  1.7 27.3 %collective-permute-start = (f32[128,1024]{1,0:T(8,128)S(1)}, f32[128,1024]{1,0:T(8,128)S(1)}, u32[]{:S(2)}, u32[]{:S(2)}) collective-permute-start(f32[128,1024]{1,0:T(8,128)S(1)} %dynamic-slice_convert_fusion), channel_id=1, source_target_pairs={{0,16},{1,17},{2,18},{3,19},{4,20},{5,21},{6,22},{7,23},{8,24},{9,... | collective-permute-start | bytes 1572872 | tf_op jit(solution)/shard_map/ppermute | solution.py:611
  5.8 24.9 %copy-start.3 = (bf16[1024,256]{1,0:T(8,128)(2,1)S(1)}, bf16[1024,256]{1,0:T(8,128)(2,1)}, u32[]{:S(2)}) copy-start(bf16[1024,256]{1,0:T(8,128)(2,1)} %wq_ref.3) | copy-start | bytes 1572868
  5.8 24.9 %copy-start.4 = (bf16[1024,256]{1,0:T(8,128)(2,1)S(1)}, bf16[1024,256]{1,0:T(8,128)(2,1)}, u32[]{:S(2)}) copy-start(bf16[1024,256]{1,0:T(8,128)(2,1)} %wk_ref.3) | copy-start | bytes 1572868
  5.8 24.9 %copy-start.5 = (bf16[1024,256]{1,0:T(8,128)(2,1)S(1)}, bf16[1024,256]{1,0:T(8,128)(2,1)}, u32[]{:S(2)}) copy-start(bf16[1024,256]{1,0:T(8,128)(2,1)} %wv_ref.3) | copy-start | bytes 1572868
  29.0 14.7 %copy-start.11 = (f32[128,1024]{1,0:T(8,128)}, f32[128,1024]{1,0:T(8,128)S(1)}, u32[]{:S(2)}) copy-start(f32[128,1024]{1,0:T(8,128)S(1)} %collective-permute-done.refs_12_) | copy-start | bytes 1572868
  29.0 3.7 %collective-permute-start.1 = (f32[256,1024]{1,0:T(8,128)}, f32[256,1024]{1,0:T(8,128)S(1)}, u32[]{:S(2)}, u32[]{:S(2)}) collective-permute-start(f32[256,1024]{1,0:T(8,128)} %bitcast.57), channel_id=1, source_target_pairs={{0,1},{1,0},{2,3},{3,2},{4,5},{5,4},{6,7},{7,6},{8,9},{9,8},{10,11... | collective-permute-start | bytes 3145736 | tf_op jit(solution)/shard_map/ppermute | solution.py:604
  29.0 14.7 %collective-permute-start.2 = (f32[128,1024]{1,0:T(8,128)}, f32[128,1024]{1,0:T(8,128)}, u32[]{:S(2)}, u32[]{:S(2)}) collective-permute-start(f32[128,1024]{1,0:T(8,128)} %copy-done.14), channel_id=1, source_target_pairs={{0,2},{1,3},{2,0},{3,1},{4,6},{5,7},{6,4},{7,5},{8,10},{9,11},{10,... | collective-permute-start | bytes 1572872 | tf_op jit(solution)/shard_map/ppermute | solution.py:611
  30.5 13.1 %collective-permute-start.3 = (f32[128,1024]{1,0:T(8,128)S(1)}, f32[128,1024]{1,0:T(8,128)}, u32[]{:S(2)}, u32[]{:S(2)}) collective-permute-start(f32[128,1024]{1,0:T(8,128)S(1)} %collective-permute-done.refs_12_), channel_id=1, source_target_pairs={{0,1},{1,0},{2,3},{3,2},{4,5},{5,4},{6,7},{7,6},{8,9},{9,8},{10,11... | collective-permute-start | bytes 1572872 | tf_op jit(solution)/shard_map/ppermute | solution.py:604
  43.6 17.1 %collective-permute-start.6 = (f32[1024,768]{1,0:T(8,128)}, f32[1024,768]{1,0:T(8,128)S(1)}, u32[]{:S(2)}, u32[]{:S(2)}) collective-permute-start(f32[1024,768]{1,0:T(8,128)} %maximum_convert_fusion), channel_id=1, source_target_pairs={{0,1},{1,0},{2,3},{3,2},{4,5},{5,4},{6,7},{7,6},{8,9},{9,8},{10,11... | collective-permute-start | bytes 9437192 | tf_op jit(solution)/shard_map/ppermute | solution.py:604
  43.6 17.1 %collective-permute-start.5 = (f32[128,1024]{1,0:T(8,128)}, f32[128,1024]{1,0:T(8,128)}, u32[]{:S(2)}, u32[]{:S(2)}) collective-permute-start(f32[128,1024]{1,0:T(8,128)} %get-tuple-element.109), channel_id=1, source_target_pairs={{0,2},{1,3},{2,0},{3,1},{4,6},{5,7},{6,4},{7,5},{8,10},{9,11},{10,... | collective-permute-start | bytes 1572872 | tf_op jit(solution)/shard_map/ppermute | solution.py:611
  45.2 15.5 %collective-permute-start.7 = (f32[128,1024]{1,0:T(8,128)}, f32[128,1024]{1,0:T(8,128)}, u32[]{:S(2)}, u32[]{:S(2)}) collective-permute-start(f32[128,1024]{1,0:T(8,128)} %collective-permute-done.2.refs_10_), channel_id=1, source_target_pairs={{0,1},{1,0},{2,3},{3,2},{4,5},{5,4},{6,7},{7,6},{8,9},{9,8},{10,11... | collective-permute-start | bytes 1572872 | tf_op jit(solution)/shard_map/ppermute | solution.py:604
  45.4 15.3 %collective-permute-start.4 = (f32[64,1024]{1,0:T(8,128)}, f32[64,1024]{1,0:T(8,128)S(1)}, u32[]{:S(2)}, u32[]{:S(2)}) collective-permute-start(f32[64,1024]{1,0:T(8,128)} %get-tuple-element.108), channel_id=1, source_target_pairs={{0,16},{1,17},{2,18},{3,19},{4,20},{5,21},{6,22},{7,23},{8,24},{9,... | collective-permute-start | bytes 786440 | tf_op jit(solution)/shard_map/ppermute | solution.py:611
  60.7 3.1 %collective-permute-start.8 = (f32[256,1024]{1,0:T(8,128)}, f32[256,1024]{1,0:T(8,128)}, u32[]{:S(2)}, u32[]{:S(2)}) collective-permute-start(f32[256,1024]{1,0:T(8,128)} %get-tuple-element.113.own_ref), channel_id=1, source_target_pairs={{0,1},{1,0},{2,3},{3,2},{4,5},{5,4},{6,7},{7,6},{8,9},{9,8},{10,11... | collective-permute-start | bytes 3145736 | tf_op jit(solution)/shard_map/ppermute | solution.py:604
  60.8 20.3 %collective-permute-start.11 = (f32[128,1024]{1,0:T(8,128)}, f32[128,1024]{1,0:T(8,128)}, u32[]{:S(2)}, u32[]{:S(2)}) collective-permute-start(f32[128,1024]{1,0:T(8,128)} %copy-done.11), channel_id=1, source_target_pairs={{0,2},{1,3},{2,0},{3,1},{4,6},{5,7},{6,4},{7,5},{8,10},{9,11},{10,... | collective-permute-start | bytes 1572872 | tf_op jit(solution)/shard_map/ppermute | solution.py:611
  61.3 14.7 %collective-permute-start.9 = (f32[64,1024]{1,0:T(8,128)}, f32[64,1024]{1,0:T(8,128)}, u32[]{:S(2)}, u32[]{:S(2)}) collective-permute-start(f32[64,1024]{1,0:T(8,128)} %get-tuple-element.120), channel_id=1, source_target_pairs={{0,16},{1,17},{2,18},{3,19},{4,20},{5,21},{6,22},{7,23},{8,24},{9,... | collective-permute-start | bytes 786440 | tf_op jit(solution)/shard_map/ppermute | solution.py:611
  61.3 14.7 %collective-permute-start.12 = (f32[64,1024]{1,0:T(8,128)S(1)}, f32[64,1024]{1,0:T(8,128)}, u32[]{:S(2)}, u32[]{:S(2)}) collective-permute-start(f32[64,1024]{1,0:T(8,128)S(1)} %collective-permute-done.4.refs_2_), channel_id=1, source_target_pairs={{0,1},{1,0},{2,3},{3,2},{4,5},{5,4},{6,7},{7,6},{8,9},{9,8},{10,11... | collective-permute-start | bytes 786440 | tf_op jit(solution)/shard_map/ppermute | solution.py:604
  61.5 19.6 %collective-permute-start.10 = (f32[64,1024]{1,0:T(8,128)S(1)}, f32[64,1024]{1,0:T(8,128)}, u32[]{:S(2)}, u32[]{:S(2)}) collective-permute-start(f32[64,1024]{1,0:T(8,128)S(1)} %collective-permute-done.4.refs_2_), channel_id=1, source_target_pairs={{0,2},{1,3},{2,0},{3,1},{4,6},{5,7},{6,4},{7,5},{8,10},{9,11},{10,... | collective-permute-start | bytes 786440 | tf_op jit(solution)/shard_map/ppermute | solution.py:611
  81.1 13.5 %collective-permute-start.17 = (f32[4,640,512]{2,1,0:T(8,128)}, f32[4,640,512]{2,1,0:T(8,128)}, u32[]{:S(2)}, u32[]{:S(2)}) collective-permute-start(f32[4,640,512]{2,1,0:T(8,128)} %get-tuple-element.136), channel_id=1, source_target_pairs={{0,1},{1,0},{2,3},{3,2},{4,5},{5,4},{6,7},{7,6},{8,9},{9,8},{10,11... | collective-permute-start | bytes 15728648 | tf_op jit(solution)/shard_map/ppermute | solution.py:604
  81.1 13.5 %collective-permute-start.13 = (f32[128,1024]{1,0:T(8,128)}, f32[128,1024]{1,0:T(8,128)S(1)}, u32[]{:S(2)}, u32[]{:S(2)}) collective-permute-start(f32[128,1024]{1,0:T(8,128)} %collective-permute-done.5.refs_0_), channel_id=1, source_target_pairs={{0,1},{1,0},{2,3},{3,2},{4,5},{5,4},{6,7},{7,6},{8,9},{9,8},{10,11... | collective-permute-start | bytes 1572872 | tf_op jit(solution)/shard_map/ppermute | solution.py:604
  81.6 13.0 %collective-permute-start.15 = (f32[64,1024]{1,0:T(8,128)}, f32[64,1024]{1,0:T(8,128)S(1)}, u32[]{:S(2)}, u32[]{:S(2)}) collective-permute-start(f32[64,1024]{1,0:T(8,128)} %collective-permute-done.9.refs_3_), channel_id=1, source_target_pairs={{0,2},{1,3},{2,0},{3,1},{4,6},{5,7},{6,4},{7,5},{8,10},{9,11},{10,... | collective-permute-start | bytes 786440 | tf_op jit(solution)/shard_map/ppermute | solution.py:611
  82.1 12.5 %collective-permute-start.14 = (f32[64,1024]{1,0:T(8,128)}, f32[64,1024]{1,0:T(8,128)S(1)}, u32[]{:S(2)}, u32[]{:S(2)}) collective-permute-start(f32[64,1024]{1,0:T(8,128)} %collective-permute-done.9.refs_3_), channel_id=1, source_target_pairs={{0,1},{1,0},{2,3},{3,2},{4,5},{5,4},{6,7},{7,6},{8,9},{9,8},{10,11... | collective-permute-start | bytes 786440 | tf_op jit(solution)/shard_map/ppermute | solution.py:604
  82.1 12.5 %collective-permute-start.16 = (f32[64,1024]{1,0:T(8,128)}, f32[64,1024]{1,0:T(8,128)S(1)}, u32[]{:S(2)}, u32[]{:S(2)}) collective-permute-start(f32[64,1024]{1,0:T(8,128)} %collective-permute-done.10.refs_6_), channel_id=1, source_target_pairs={{0,1},{1,0},{2,3},{3,2},{4,5},{5,4},{6,7},{7,6},{8,9},{9,8},{10,11... | collective-permute-start | bytes 786440 | tf_op jit(solution)/shard_map/ppermute | solution.py:604
  94.6 27.7 %collective-permute-start.22 = (f32[8,64,1024]{2,1,0:T(8,128)}, f32[8,64,1024]{2,1,0:T(8,128)}, u32[]{:S(2)}, u32[]{:S(2)}) collective-permute-start(f32[8,64,1024]{2,1,0:T(8,128)} %get-tuple-element.150), channel_id=1, source_target_pairs={{0,2},{1,9},{2,0},{3,11},{4,6},{5,13},{6,4},{7,15},{8,10},{9,1},{1... | collective-permute-start | bytes 6291464 | tf_op jit(solution)/shard_map/ppermute | solution.py:611
  96.2 26.1 %collective-permute-start.21 = (f32[256,1024]{1,0:T(8,128)S(1)}, f32[256,1024]{1,0:T(8,128)}, u32[]{:S(2)}, u32[]{:S(2)}) collective-permute-start(f32[256,1024]{1,0:T(8,128)S(1)} %copy-done.7), channel_id=1, source_target_pairs={{0,1},{1,0},{2,3},{3,2},{4,5},{5,4},{6,7},{7,6},{8,9},{9,8},{10,11... | collective-permute-start | bytes 3145736 | tf_op jit(solution)/shard_map/ppermute | solution.py:604
  96.2 3.8 %collective-permute-start.19 = (f32[128,1024]{1,0:T(8,128)}, f32[128,1024]{1,0:T(8,128)S(1)}, u32[]{:S(2)}, u32[]{:S(2)}) collective-permute-start(f32[128,1024]{1,0:T(8,128)} %collective-permute-done.11.refs_14_), channel_id=1, source_target_pairs={{0,1},{1,0},{2,3},{3,2},{4,5},{5,4},{6,7},{7,6},{8,9},{9,8},{10,11... | collective-permute-start | bytes 1572872 | tf_op jit(solution)/shard_map/ppermute | solution.py:604
  96.7 3.3 %collective-permute-start.18 = (f32[64,1024]{1,0:T(8,128)S(1)}, f32[64,1024]{1,0:T(8,128)S(1)}, u32[]{:S(2)}, u32[]{:S(2)}) collective-permute-start(f32[64,1024]{1,0:T(8,128)S(1)} %collective-permute-done.15.refs_7_), channel_id=1, source_target_pairs={{0,1},{1,0},{2,3},{3,2},{4,5},{5,4},{6,7},{7,6},{8,9},{9,8},{10,11... | collective-permute-start | bytes 786440 | tf_op jit(solution)/shard_map/ppermute | solution.py:604
  96.7 25.6 %collective-permute-start.20 = (f32[4,64,256]{2,1,0:T(8,128)}, f32[4,64,256]{2,1,0:T(8,128)S(1)}, u32[]{:S(2)}, u32[]{:S(2)}) collective-permute-start(f32[4,64,256]{2,1,0:T(8,128)} %get-tuple-element.147), channel_id=1, source_target_pairs={{0,1},{1,0},{2,3},{3,2},{4,5},{5,4},{6,7},{7,6},{8,9},{9,8},{10,11... | collective-permute-start | bytes 786440 | tf_op jit(solution)/shard_map/ppermute | solution.py:604
  111.9 35.5 %collective-permute-start.23 = (f32[8,64,512]{2,1,0:T(8,128)}, f32[8,64,512]{2,1,0:T(8,128)}, u32[]{:S(2)}, u32[]{:S(2)}) collective-permute-start(f32[8,64,512]{2,1,0:T(8,128)} %get-tuple-element.144), channel_id=1, source_target_pairs={{0,4},{1,9},{2,6},{3,11},{4,0},{5,13},{6,2},{7,15},{8,12},{9,1},{1... | collective-permute-start | bytes 3145736 | tf_op jit(solution)/shard_map/ppermute | solution.py:611
  121.8 29.1 %collective-permute-start.24 = (f32[8,64,512]{2,1,0:T(8,128)}, f32[8,64,512]{2,1,0:T(8,128)}, u32[]{:S(2)}, u32[]{:S(2)}) collective-permute-start(f32[8,64,512]{2,1,0:T(8,128)} %get-tuple-element.146), channel_id=1, source_target_pairs={{0,4},{1,9},{2,6},{3,11},{4,0},{5,13},{6,2},{7,15},{8,12},{9,1},{1... | collective-permute-start | bytes 3145736 | tf_op jit(solution)/shard_map/ppermute | solution.py:611
  125.3 27.9 %collective-permute-start.25 = (f32[4,64,1024]{2,1,0:T(8,128)}, f32[4,64,1024]{2,1,0:T(8,128)}, u32[]{:S(2)}, u32[]{:S(2)}) collective-permute-start(f32[4,64,1024]{2,1,0:T(8,128)} %get-tuple-element.176), channel_id=1, source_target_pairs={{0,16},{1,3},{2,18},{3,1},{4,20},{5,7},{6,22},{7,5},{8,24},{9,11},... | collective-permute-start | bytes 3145736 | tf_op jit(solution)/shard_map/ppermute | solution.py:611
  125.9 20.5 %copy-start.27 = (f32[2,8,1024]{2,1,0:T(8,128)S(1)}, f32[2,8,1024]{2,1,0:T(8,128)}, u32[]{:S(2)}) copy-start(f32[2,8,1024]{2,1,0:T(8,128)} %get-tuple-element.158) | copy-start | bytes 196612
  125.9 21.6 %copy-start.8 = (f32[8,64,512]{2,1,0:T(8,128)S(1)}, f32[8,64,512]{2,1,0:T(8,128)}, u32[]{:S(2)}) copy-start(f32[8,64,512]{2,1,0:T(8,128)} %get-tuple-element.159) | copy-start | bytes 3145732
  149.7 11.7 %collective-permute-start.26 = (f32[4,64,512]{2,1,0:T(8,128)}, f32[4,64,512]{2,1,0:T(8,128)}, u32[]{:S(2)}, u32[]{:S(2)}) collective-permute-start(f32[4,64,512]{2,1,0:T(8,128)} %get-tuple-element.180), channel_id=1, source_target_pairs={{0,8},{1,5},{2,10},{3,7},{4,12},{5,1},{6,14},{7,3},{8,0},{9,13},{1... | collective-permute-start | bytes 1572872 | tf_op jit(solution)/shard_map/ppermute | solution.py:611
  155.6 18.2 %collective-permute-start.27 = (f32[2,64,1024]{2,1,0:T(8,128)}, f32[2,64,1024]{2,1,0:T(8,128)}, u32[]{:S(2)}, u32[]{:S(2)}) collective-permute-start(f32[2,64,1024]{2,1,0:T(8,128)} %get-tuple-element.182), channel_id=1, source_target_pairs={{0,8},{1,5},{2,10},{3,7},{4,12},{5,1},{6,14},{7,3},{8,0},{9,13},{1... | collective-permute-start | bytes 1572872 | tf_op jit(solution)/shard_map/ppermute | solution.py:611
  156.4 17.4 %copy-start.6 = (f32[2,64,1024]{2,1,0:T(8,128)S(1)}, f32[2,64,1024]{2,1,0:T(8,128)}, u32[]{:S(2)}) copy-start(f32[2,64,1024]{2,1,0:T(8,128)} %get-tuple-element.166) | copy-start | bytes 1572868
  156.4 26.2 %collective-permute-start.30 = (f32[4,64,512]{2,1,0:T(8,128)}, f32[4,64,512]{2,1,0:T(8,128)S(1)}, u32[]{:S(2)}, u32[]{:S(2)}) collective-permute-start(f32[4,64,512]{2,1,0:T(8,128)} %get-tuple-element.178), channel_id=1, source_target_pairs={{0,8},{1,5},{2,10},{3,7},{4,12},{5,1},{6,14},{7,3},{8,0},{9,13},{1... | collective-permute-start | bytes 1572872 | tf_op jit(solution)/shard_map/ppermute | solution.py:611
  157.6 12.5 %collective-permute-start.28 = (f32[8,1024]{1,0:T(8,128)S(1)}, f32[8,1024]{1,0:T(8,128)S(1)}, u32[]{:S(2)}, u32[]{:S(2)}) collective-permute-start(f32[8,1024]{1,0:T(8,128)S(1)} %concatenate.11), channel_id=1, source_target_pairs={{0,16},{1,17},{2,18},{3,19},{4,20},{5,21},{6,22},{7,23},{8,24},{9,... | collective-permute-start | bytes 98312 | tf_op jit(solution)/shard_map/ppermute | solution.py:611
  170.1 5.6 %collective-permute-start.29 = (f32[8,1024]{1,0:T(8,128)S(1)}, f32[8,1024]{1,0:T(8,128)S(1)}, u32[]{:S(2)}, u32[]{:S(2)}) collective-permute-start(f32[8,1024]{1,0:T(8,128)S(1)} %add.126), channel_id=1, source_target_pairs={{0,8},{1,9},{2,10},{3,11},{4,12},{5,13},{6,14},{7,15},{8,0},{9,1},... | collective-permute-start | bytes 98312 | tf_op jit(solution)/shard_map/ppermute | solution.py:611
  175.7 7.2 %collective-permute-start.31 = (f32[8,1024]{1,0:T(8,128)S(1)}, f32[8,1024]{1,0:T(8,128)S(1)}, u32[]{:S(2)}, u32[]{:S(2)}) collective-permute-start(f32[8,1024]{1,0:T(8,128)S(1)} %add.128), channel_id=1, source_target_pairs={{0,4},{1,5},{2,6},{3,7},{4,0},{5,1},{6,2},{7,3},{8,12},{9,13},{10,... | collective-permute-start | bytes 98312 | tf_op jit(solution)/shard_map/ppermute | solution.py:611
  178.2 12.8 %collective-permute-start.36 = (f32[64,512]{1,0:T(8,128)S(1)}, f32[64,512]{1,0:T(8,128)S(1)}, u32[]{:S(2)}, u32[]{:S(2)}) collective-permute-start(f32[64,512]{1,0:T(8,128)S(1)} %get-tuple-element.189), channel_id=1, source_target_pairs={{0,18},{1,19},{2,16},{3,17},{4,22},{5,23},{6,20},{7,21},{8,26},{9,... | collective-permute-start | bytes 393224 | tf_op jit(solution)/shard_map/ppermute | solution.py:611
  180.9 11.4 %collective-permute-start.35 = (f32[64,512]{1,0:T(8,128)S(1)}, f32[64,512]{1,0:T(8,128)S(1)}, u32[]{:S(2)}, u32[]{:S(2)}) collective-permute-start(f32[64,512]{1,0:T(8,128)S(1)} %get-tuple-element.190), channel_id=1, source_target_pairs={{0,16},{1,17},{2,18},{3,19},{4,20},{5,21},{6,22},{7,23},{8,24},{9,... | collective-permute-start | bytes 393224 | tf_op jit(solution)/shard_map/ppermute | solution.py:611
  180.9 11.5 %collective-permute-start.34 = (f32[64,512]{1,0:T(8,128)S(1)}, f32[64,512]{1,0:T(8,128)S(1)}, u32[]{:S(2)}, u32[]{:S(2)}) collective-permute-start(f32[64,512]{1,0:T(8,128)S(1)} %get-tuple-element.191), channel_id=1, source_target_pairs={{0,2},{1,3},{2,0},{3,1},{4,6},{5,7},{6,4},{7,5},{8,10},{9,11},{10,... | collective-permute-start | bytes 393224 | tf_op jit(solution)/shard_map/ppermute | solution.py:611
  182.6 8.3 %collective-permute-start.33 = (f32[1,64,1024]{2,1,0:T(8,128)S(1)}, f32[1,64,1024]{2,1,0:T(8,128)S(1)}, u32[]{:S(2)}, u32[]{:S(2)}) collective-permute-start(f32[1,64,1024]{2,1,0:T(8,128)S(1)} %get-tuple-element.183), channel_id=1, source_target_pairs={{0,4},{1,17},{2,6},{3,19},{4,0},{5,21},{6,2},{7,23},{8,12},{9,25},... | collective-permute-start | bytes 786440 | tf_op jit(solution)/shard_map/ppermute | solution.py:611
  182.9 4.0 %collective-permute-start.32 = (f32[8,1024]{1,0:T(8,128)S(1)}, f32[8,1024]{1,0:T(8,128)S(1)}, u32[]{:S(2)}, u32[]{:S(2)}) collective-permute-start(f32[8,1024]{1,0:T(8,128)S(1)} %add.131), channel_id=1, source_target_pairs={{0,2},{1,3},{2,0},{3,1},{4,6},{5,7},{6,4},{7,5},{8,10},{9,11},{10,... | collective-permute-start | bytes 98312 | tf_op jit(solution)/shard_map/ppermute | solution.py:611
  186.9 13.3 %collective-permute-start.39 = (f32[64,512]{1,0:T(8,128)S(1)}, f32[64,512]{1,0:T(8,128)S(1)}, u32[]{:S(2)}, u32[]{:S(2)}) collective-permute-start(f32[64,512]{1,0:T(8,128)S(1)} %get-tuple-element.185), channel_id=1, source_target_pairs={{0,18},{1,19},{2,16},{3,17},{4,22},{5,23},{6,20},{7,21},{8,26},{9,... | collective-permute-start | bytes 393224 | tf_op jit(solution)/shard_map/ppermute | solution.py:611
  190.9 9.8 %collective-permute-start.38 = (f32[64,512]{1,0:T(8,128)S(1)}, f32[64,512]{1,0:T(8,128)S(1)}, u32[]{:S(2)}, u32[]{:S(2)}) collective-permute-start(f32[64,512]{1,0:T(8,128)S(1)} %get-tuple-element.186), channel_id=1, source_target_pairs={{0,16},{1,17},{2,18},{3,19},{4,20},{5,21},{6,22},{7,23},{8,24},{9,... | collective-permute-start | bytes 393224 | tf_op jit(solution)/shard_map/ppermute | solution.py:611
  191.0 9.7 %collective-permute-start.37 = (f32[64,512]{1,0:T(8,128)S(1)}, f32[64,512]{1,0:T(8,128)S(1)}, u32[]{:S(2)}, u32[]{:S(2)}) collective-permute-start(f32[64,512]{1,0:T(8,128)S(1)} %get-tuple-element.187), channel_id=1, source_target_pairs={{0,2},{1,3},{2,0},{3,1},{4,6},{5,7},{6,4},{7,5},{8,10},{9,11},{10,... | collective-permute-start | bytes 393224 | tf_op jit(solution)/shard_map/ppermute | solution.py:611
  (20 other events, 93.4 us)

commit v4 on v3

--- a/solution.py
+++ b/solution.py
@@ -185,8 +185,8 @@
         def _():
             send = low[which * half : (which + 1) * half].astype(SINGLE)
             send_ref[...] = send
-            first_ref[...] = send[: half // 2]
-            second_ref[...] = send[half // 2 :]
+            first_ref[...] = send[: first_ref.shape[0]]
+            second_ref[...] = send[first_ref.shape[0] :]
 
 
 def feed_body(low_ref, cot_ref, up_ref, down_ref, hidden_ref, grad_ref, part_ref, out_ref):
@@ -442,7 +442,7 @@
     share = send_ref.shape[1]
     inner = att_ref.shape[1]
     held = send_ref.shape[0]
-    per = LANES // share
+    per = WIDE // share
     keys_all = kv_ref.shape[0] // images
     latent = jnp.concatenate(
         [kv_ref[i * keys_all + patches : (i + 1) * keys_all] for i in range(images)], 0
@@ -475,10 +475,10 @@
     return call(
         functools.partial(small_grad_body, images=images, patches=patches),
         "small_grad",
-        (width // LANES,),
+        (width // WIDE,),
         [
-            (kv, pl.BlockSpec((rows, LANES), lambda at, p: (0, at))),
-            (gb, pl.BlockSpec((gb.shape[0], LANES), lambda at, p: (0, at))),
+            (kv, pl.BlockSpec((rows, WIDE), lambda at, p: (0, at))),
+            (gb, pl.BlockSpec((gb.shape[0], WIDE), lambda at, p: (0, at))),
         ]
         + [whole(a) for a in (gkv, gq, att)],
         [(shape, SINGLE, spec), (shape, SINGLE, spec)],
@@ -489,8 +489,8 @@
 
 def inputs_body(
     gkv_ref, gkv_far_ref, gq_ref, gq_far_ref, media_ref, mean_ref, inv_ref, latent_ref, gm_ref,
-    wq_ref, wk_ref, wv_ref, far_ref, mg_ref, lg_ref,
-    out_ref, late_ref, vec_ref, heads_ref, query_ref,
+    wq_ref, wk_ref, wv_ref, far_ref, mg_ref, lg_ref, before_ref,
+    out_ref, late_ref, sums_ref, heads_ref, query_ref, vec_ref,
 ):
     inner = wq_ref.shape[1]
     patches = media_ref.shape[1]
@@ -525,11 +525,23 @@
     vec_ref[2] += row_sums(product)
     vec_ref[3] += row_sums(upstream)
 
+    @pl.when(pl.program_id(0) == pl.num_programs(0) - 1)
+    def _():
+        for at in range(4):
+            sums_ref[at : at + 1] = jnp.sum(vec_ref[at], 0, keepdims=True)
+        if len(before_ref.shape) == 2:
+            sums_ref[:4] += before_ref[:4]
+            sums_ref[4:] = before_ref[4:]
+        else:
+            for at in range(2):
+                sums_ref[at + 4 : at + 5] = jnp.sum(before_ref[at], 0, keepdims=True)
+            sums_ref[6:] = jnp.zeros_like(sums_ref[6:])
+
 
 def inputs_back(first, count, held, gkv, gkv_far, gq, gq_far, media, mean, inv, latents, gm, weights):
     images, patches, width = media.shape
     inner = weights[0].shape[1]
-    vec = (4, 8, width)
+    vec = (8, width)
 
     def image(array):
         rest = (0,) * (array.ndim - 1)
@@ -551,9 +563,13 @@
         [
             (media.shape, HALF, image(media)),
             (latents.shape, HALF, image(latents)),
-            (vec, SINGLE, pl.BlockSpec(vec, lambda at: (0, 0, 0))),
+            (vec, SINGLE, pl.BlockSpec(vec, lambda at: (0, 0))),
         ],
-        scratch=[pltpu.VMEM((width, 4 * inner), HALF), pltpu.VMEM((width, 2 * inner), HALF)],
+        scratch=[
+            pltpu.VMEM((width, 4 * inner), HALF),
+            pltpu.VMEM((width, 2 * inner), HALF),
+            pltpu.VMEM((4, 8, width), SINGLE),
+        ],
         flops=8 * count * patches * width * inner,
         aliases={len(ins) - len(held) + i: i for i in range(len(held))},
     )
@@ -586,7 +602,7 @@
 
 def plan(bits):
     if bits == 4:
-        return (0, 3), ([1, 2], [2, 1]), ([0, 3, 2, 1], [2, 0, 1, 3])
+        return (0, 3), ([1, 2], [2, 1]), ([0, 3, 1, 2], [1, 0, 2, 3])
     top = bits - 1
     rest = list(range(2, top - 1))
     wide_ = ([top, top - 1] + rest, [top - 1, top] + rest)
@@ -625,12 +641,41 @@
             found.append(spot)
         return jnp.where(self.core == 0, found[0], found[1])
 
-    def stage(self, leave, orders, step):
-        return self.send(leave, 1 << orders[0][step], 1 << orders[1][step])
-
-    def halve(self, come, keep):
+class Halving:
+    def __init__(self, links, leave, keep, orders):
+        self.links, self.keep, self.orders = links, keep, orders
+        self.left = len(orders[0])
+        self.send(leave)
+
+    def send(self, leave):
+        zero, one = self.orders
+        self.come = self.links.send(leave, 1 << zero[-self.left], 1 << one[-self.left])
+
+    def advance(self, *done):
+        keep = after(self.keep, *done)
+        self.left -= 1
+        if not self.left:
+            return keep + self.come
         half = keep.shape[0] // 2
-        return keep[:half] + come[:half], keep[half:] + come[half:]
+        leave, self.keep = keep[:half] + self.come[:half], keep[half:] + self.come[half:]
+        self.send(leave)
+        return leave
+
+
+class Total:
+    def __init__(self, links, array, order):
+        self.links, self.array, self.order = links, array, list(order)
+        self.send()
+
+    def send(self):
+        hop = 1 << self.order.pop(0)
+        self.come = self.links.send(self.array, hop, hop)
+
+    def advance(self, *done):
+        self.array = after(self.array, *done) + self.come
+        if self.order:
+            self.send()
+        return self.array
 
 
 def local(
@@ -656,14 +701,19 @@
     cot = cotangent.reshape(rows, width)
     half = rows // 2
     cot_own = lax.dynamic_slice_in_dim(cot, links.core * half, half, 0).astype(SINGLE)
-    cot_far = links.send(cot_own, far_bit, far_bit)
+    cut = half // 8 * 5
+    cot_far_a = links.send(cot_own[:cut], far_bit, far_bit)
+    cot_near = links.send(cot_own, near_bit, near_bit)
     kv, q, k, v, probs, attended, branch, mean, inv = attend(
         buckets, media, latents, query_weight, key_weight, value_weight, output_weight, vectors
     )
-    branch, cot_own, cot_far = lax.optimization_barrier((branch, cot_own, cot_far))
+    branch, cot_own, cot_near, cot_far_a = lax.optimization_barrier(
+        (branch, cot_own, cot_near, cot_far_a)
+    )
     branch = branch.reshape(rows, width)
-    cot_near = links.send(cot_own, near_bit, near_bit)
-    cot_far_other = links.swap(cot_far)
+    cot_far_b = links.send(cot_own[cut:], far_bit, far_bit)
+    cot_both_a = links.send(cot_far_a, near_bit, near_bit)
+    cot_near_other = links.swap(cot_near)
     branch_far = links.swap(branch)
     weights_send = jnp.concatenate(
         [after(query_weight, branch), key_weight, value_weight], 1
@@ -687,34 +737,42 @@
             ((rows, width), HALF, pl.BlockSpec((rows, width), lambda at, c: (0, 0))),
             ((half, width), SINGLE, pl.BlockSpec((half, width), lambda at, c: (0, 0))),
         ]
-        + [((half // 2, width), SINGLE, pl.BlockSpec((half // 2, width), lambda at, c: (0, 0)))] * 2,
+        + [((r, width), SINGLE, pl.BlockSpec((r, width), lambda at, c: (0, 0))) for r in (half - cut, cut)],
         prefetch=(core,),
     )
-    low, low_send, low_first, cot_near, weights_send = lax.optimization_barrier(
-        (low, low_send, low_first, cot_near, weights_send, cot_far_other)
-    )[:5]
+    low, low_send, low_first, weights_send, cot_far_a, cot_far_b, cot_both_a = lax.optimization_barrier(
+        (low, low_send, low_first, weights_send, cot_far_a, cot_far_b, cot_both_a, cot_near_other)
+    )[:7]
     low_far_a = links.send(low_first, far_bit, far_bit)
-    low_near = links.send(low_send, near_bit, near_bit)
-    cot_near_other = links.swap(cot_near)
-    weights_far = links.swap(weights_send)
+    cot_both_b = links.send(cot_far_b, near_bit, near_bit)
+    cot_far_a_other, cot_both_a_other = links.swap(cot_far_a), links.swap(cot_both_a)
+    cot_far_b_other = links.swap(cot_far_b)
     hidden, grad_pre, part, feed_out = feed(low, cot, up_weight, down_weight)
-    part, low_far_a, low_near, cot_far, low_second = lax.optimization_barrier(
-        (part, low_far_a, low_near, cot_far, low_second, weights_far, cot_near_other)
-    )[:5]
+    part, low_far_a, low_send, low_second, weights_send, cot_both_b = lax.optimization_barrier(
+        (
+            part, low_far_a, low_send, low_second, weights_send, cot_both_b,
+            cot_far_a_other, cot_both_a_other, cot_far_b_other,
+        )
+    )[:6]
     part_far = links.swap(part)
     low_far_b = links.send(low_second, far_bit, far_bit)
+    low_near = links.send(low_send, near_bit, near_bit)
     low_both_a = links.send(low_far_a, near_bit, near_bit)
     low_far_a_other = links.swap(low_far_a)
-    cot_both = links.send(cot_far, near_bit, near_bit)
+    cot_both_b_other = links.swap(cot_both_b)
     grad_middle, grad_branch, gkv, gkv_send, gq, gq_send, feed_vec = back(
         middle, part, part_far, cot, gain, output_weight, q, k, v, probs
     )
-    grad_branch, gkv_send, low_far_b, low_both_a, low_near, cot_both = lax.optimization_barrier(
-        (grad_branch, gkv_send, low_far_b, low_both_a, low_near, cot_both, low_far_a_other)
-    )[:6]
+    grad_branch, gkv_send, low_near, low_far_b, low_both_a = lax.optimization_barrier(
+        (
+            grad_branch, gkv_send, low_near, low_far_b, low_both_a,
+            low_far_a_other, cot_both_b_other,
+        )
+    )[:5]
     low_both_b = links.send(low_far_b, near_bit, near_bit)
-    low_far_b_other, low_both_a_other = links.swap(low_far_b), links.swap(low_both_a)
-    gkv_far, low_near_other = links.swap(gkv_send), links.swap(low_near)
+    gkv_far = links.swap(gkv_send)
+    low_near_other, low_far_b_other = links.swap(low_near), links.swap(low_far_b)
+    low_both_a_other = links.swap(low_both_a)
     small_leave, small_keep = small_grad(
         links.places(small_orders, ()),
         kv.reshape(images * keys_all, width),
@@ -726,15 +784,16 @@
         images,
         patches,
     )
-    small_leave, feed_out, gq_send, low_both_b, cot_both = lax.optimization_barrier(
+    small_leave, low_both_b, gq_send, feed_out, weights_send = lax.optimization_barrier(
         (
-            small_leave, feed_out, gq_send, low_both_b, cot_both,
-            low_far_b_other, low_both_a_other, gkv_far, low_near_other,
+            small_leave, low_both_b, gq_send, feed_out, weights_send,
+            gkv_far, low_near_other, low_far_b_other, low_both_a_other,
         )
     )[:5]
-    low_both_b_other, cot_both_other = links.swap(low_both_b), links.swap(cot_both)
-    small_come = links.stage(small_leave, small_orders, 0)
-    gq_far, feed_far = links.swap(gq_send), links.swap(feed_out)
+    low_both_b_other = links.swap(low_both_b)
+    small = Halving(links, small_leave, small_keep, small_orders)
+    weights_far, gq_far = links.swap(weights_send), links.swap(gq_send)
+    feed_far = links.swap(feed_out)
     place = links.places(wide_orders, group)
     down_leave, down_keep, fl, cl, slope = down_side(
         member,
@@ -743,73 +802,72 @@
             low_near, low_near_other, low_far_a, low_far_b, low_far_a_other, low_far_b_other,
             low_both_a, low_both_b, low_both_a_other, low_both_b_other,
         ],
-        [cot_near, cot_near_other, cot_far, cot_far_other, cot_both, cot_both_other],
+        [
+            cot_near, cot_near_other, cot_far_a, cot_far_b, cot_far_a_other, cot_far_b_other,
+            cot_both_a, cot_both_b, cot_both_a_other, cot_both_b_other,
+        ],
         up_weight,
         low,
         cot,
         hidden,
         devices,
     )
-    down_come = links.stage(down_leave, wide_orders, 0)
+    down = Halving(links, down_leave, down_keep, wide_orders)
     up_leave, up_keep = up_side(
-        member, place, fl, cl, slope, down_weight, after(grad_pre, down_leave), devices
-    )
-    up_come = links.stage(up_leave, wide_orders, 0)
-    small_leave, small_keep = links.halve(
-        small_come, after(small_keep, up_leave, gq_far, feed_far)
-    )
-    small_come = links.stage(small_leave, small_orders, 1)
+        member,
+        place,
+        fl,
+        cl,
+        slope,
+        down_weight,
+        after(grad_pre, down_leave, weights_far, gq_far, feed_far),
+        devices,
+    )
+    up = Halving(links, up_leave, up_keep, wide_orders)
+    done = down.advance(small.advance(up_leave))
+    inputs = (gkv_far, gq, gq_far, media, mean, inv, latents)
+    inputs += (grad_middle.reshape(images, latent_rows, width),)
+    weights = (query_weight, key_weight, value_weight, weights_far, vectors[0], vectors[2])
+    part = images // 2
+    early = inputs_back(0, part, (), after(gkv, done), *inputs, weights + (feed_vec,))
+
+    hops = [near_bit * (at & 1) + far_bit * (at >> 1) for at in range(GROUP)]
+
+    def pieces(mixed):
+        return [mixed[0]] + [links.send(mixed[at], hops[at], hops[at]) for at in range(1, GROUP)]
+
+    done = early[2]
+    while down.left > 1:
+        done = down.advance(done)
+    mixed = down.advance(done)
+    down_pieces = pieces(mixed)
+    done = mixed
+    while up.left > 1:
+        done = up.advance(done)
     grad_media, grad_latents, vec = inputs_back(
-        0,
-        images,
-        (),
-        after(gkv, small_leave),
-        gkv_far,
-        gq,
-        gq_far,
-        media,
-        mean,
-        inv,
-        latents,
-        grad_middle.reshape(images, latent_rows, width),
-        (query_weight, key_weight, value_weight, weights_far, vectors[0], vectors[2]),
-    )
-    vec = jnp.sum(jnp.concatenate([vec, feed_vec], 0), 1)
-    vec = jnp.concatenate([vec, jnp.zeros((2, width), SINGLE)], 0)
-    vec_steps = [1 << at for at in reversed(range(bits))]
-
-    steps = len(wide_orders[0])
-    done = vec
-    for step in range(steps - 1):
-        down_leave, down_keep = links.halve(down_come, after(down_keep, done))
-        down_come = links.stage(down_leave, wide_orders, step + 1)
-        up_leave, up_keep = links.halve(up_come, after(up_keep, down_leave))
-        up_come = links.stage(up_leave, wide_orders, step + 1)
-        done = up_leave
-    vec_come = links.send(after(vec, done), vec_steps[0], vec_steps[0])
-    for step in range(2, bits):
-        small_leave, small_keep = links.halve(small_come, after(small_keep, done))
-        small_come = links.stage(small_leave, small_orders, step)
-        done = small_leave
-        vec = after(vec, done) + vec_come
-        vec_come = links.send(vec, vec_steps[step - 1], vec_steps[step - 1])
-        if step == 2:
-            result = (after(middle, done) + (feed_out + feed_far)).astype(HALF)
-            done = result
-            hops = [near_bit * (at & 1) + far_bit * (at >> 1) for at in range(GROUP)]
-            mixed = after(down_keep, result) + down_come
-            down_pieces = [mixed[0]] + [links.send(mixed[at], hops[at], hops[at]) for at in range(1, GROUP)]
-            done = mixed
-    mixed = after(up_keep, done) + up_come
-    up_pieces = [mixed[0]] + [links.send(mixed[at], hops[at], hops[at]) for at in range(1, GROUP)]
-    vec = after(vec, mixed) + vec_come
-    vec = vec + links.send(vec, vec_steps[-1], vec_steps[-1])
+        part, images - part, early[:2], after(gkv, done), *inputs, weights + (early[2],)
+    )
+    down_pieces = list(lax.optimization_barrier(tuple(down_pieces) + (vec,)))
+    vec = down_pieces.pop()
+    mixed = up.advance(vec)
+    up_pieces = pieces(mixed)
+    vec = Total(links, after(vec, mixed), [group[1], group[0]] + wide_orders[0])
+    done = small.advance(vec.array)
+    done = vec.advance(done, up_pieces[1])
+    done = result = (after(middle, done) + (feed_out + feed_far)).astype(HALF)
+    down_pieces[0] = after(down_pieces[0], done)
+    done = grad_down = place_pieces(member, down_pieces)
+    while small.left > 1:
+        done = small.advance(done)
+    done = vec.advance(done, up_pieces[2])
+    done = vec.advance(done, up_pieces[3])
+    while vec.order:
+        done = vec.advance(done)
+    vec = vec.advance(done)
     vec = lax.dynamic_slice_in_dim(vec, links.row * share, share, 1)
-    small = (after(small_keep, vec) + small_come)[0]
-    down_pieces[0] = after(down_pieces[0], small)
-    grad_down = place_pieces(member, down_pieces)
-    up_pieces[0] = after(up_pieces[0], grad_down)
+    up_pieces[0] = after(up_pieces[0], vec)
     grad_up = place_pieces(member, up_pieces)
+    small = small.advance(grad_up)[0]
     return (
         result.reshape(latents.shape),
         grad_media,

time: 206 us -> 193 us (0.937)
  waiting for transfers between devices: 45 us -> 30.8 us
  other arithmetic: 19.8 us -> 15.2 us
  Pallas kernels: 93.9 us -> 98.3 us
    ppermute x26 -> x28, waiting for transfers between devices: 42 us -> 23.5 us  [send(): return lax.ppermute(array, ('dp', 'tensor'), pairs)]
    pallas_call x10 -> x11, Pallas kernels: 93.9 us -> 98.3 us  [call(): pl.pallas_call(body, out_shape=shapes, grid_spec=pltpu.PrefetchScalarGrid...]
    ppermute x14 -> x16, waiting for transfers between devices: 3.01 us -> 7.34 us  [swap(): return lax.ppermute(array, 'tensor', [(0, 1), (1, 0)])]
    add x11, other arithmetic: 12.3 us -> 8.96 us  [the longest x3 6.45 us: advance(): keep[half:] + self.come[half:]]
    ppermute x26 -> x28, starting transfers between devices: 34.4 us -> 34.9 us  [send(): return lax.ppermute(array, ('dp', 'tensor'), pairs)]
    unnamed x56 -> x70, local copies, waits for them, and re-layouts: 4.51 us -> 4.52 us
  transfers between devices with their start and end apart: 40 -> 44, of which waited for: 12 -> 12; matrix products, arithmetic and copies ran while one was open for 11% -> 9% of each run, Pallas kernels for 45% -> 51%
where the time goes in v4:
time: 193 us; the launch traced here: 192 us
  Pallas kernels  98.3 us (51%)
  starting transfers between devices  38.8 us (20%)
  waiting for transfers between devices  30.8 us (16%)
  other arithmetic  15.2 us (8%)
  local copies, waits for them, and re-layouts  7.97 us (4%)
    pallas_call x11, Pallas kernels, call(): pl.pallas_call(body, out_shape=shapes, grid_spec=pltpu.PrefetchScalarGrid...  98.3 us
    ppermute x28, starting transfers between devices, send(): return lax.ppermute(array, ('dp', 'tensor'), pairs)  34.9 us
    ppermute x28, waiting for transfers between devices, send(): return lax.ppermute(array, ('dp', 'tensor'), pairs)  23.5 us
    ppermute x16, waiting for transfers between devices, swap(): return lax.ppermute(array, 'tensor', [(0, 1), (1, 0)])  7.34 us
    add x3, other arithmetic, advance(): keep[half:] + self.come[half:]  6.45 us
    unnamed x70, local copies, waits for them, and re-layouts  4.52 us
    ppermute x16, starting transfers between devices, swap(): return lax.ppermute(array, 'tensor', [(0, 1), (1, 0)])  3.87 us
  transfers between devices with their start and end apart: 44, of which 12 were waited for; matrix products, arithmetic and copies ran while one was open for 9% of the time, Pallas kernels for 51%

profile of v4, /device:TPU:0, one launch (start us, length us, event | category | flops | bytes accessed | tf_op | source)
XLA Modules:
  0.0 192.2 jit_solution(1897928930007098761)
XLA Ops:
  0.6 1.0 dynamic-slice_convert_fusion
  1.7 3.0 %collective-permute-start = (f32[128,1024]{1,0:T(8,128)S(1)}, f32[128,1024]{1,0:T(8,128)S(1)}, u32[]{:S(2)}, u32[]{:S(2)}) collective-permute-start(f32[128,1024]{1,0:T(8,128)S(1)} %dynamic-slice_convert_fusion), channel_id=1, source_target_pairs={{0,2},{1,3},{2,0},{3,1},{4,6},{5,7},{6,4},{7,5},{8,10},{9,11},{10,... | collective-permute-start | bytes 1572872 | tf_op jit(solution)/shard_map/ppermute | solution.py:627
  4.7 2.7 %collective-permute-start.1 = (f32[80,1024]{1,0:T(8,128)S(1)}, f32[80,1024]{1,0:T(8,128)S(1)}, u32[]{:S(2)}, u32[]{:S(2)}) collective-permute-start(f32[80,1024]{1,0:T(8,128)S(1)} %slice.160), channel_id=1, source_target_pairs={{0,16},{1,17},{2,18},{3,19},{4,20},{5,21},{6,22},{7,23},{8,24},{9,... | collective-permute-start | bytes 983048 | tf_op jit(solution)/shard_map/ppermute | solution.py:627
  7.4 14.5 %attend.1 = (bf16[4,640,1024]{2,1,0:T(8,128)(2,1)}, bf16[4,64,256]{2,1,0:T(8,128)(2,1)}, bf16[4,640,256]{2,1,0:T(8,128)(2,1)}, bf16[4,640,256]{2,1,0:T(8,128)(2,...) custom-call(s32[4]{0:T(128)} %buckets_ref.1, ...), custom_call_target="tpu_custom_call" | custom-call | flops 3355443200 | bytes 19171328 | tf_op jit(solution)/shard_map/attend/pallas_call | solution.py:73
  21.9 0.8 copy-done.10
  24.6 1.9 maximum_convert_fusion
  26.5 1.0 copy-done.9
  27.5 3.9 %middle.1 = (f32[256,1024]{1,0:T(8,128)}, bf16[256,1024]{1,0:T(8,128)(2,1)}, f32[128,1024]{1,0:T(8,128)}, f32[48,1024]{1,0:T(8,128)}, f32[80,1024]{1,0:T(8,128)}) custom-call(s32[1]{0:T(128)} %bitcast.core_ref, bf16[256,1024]{1,0:T(8,128)(2,1)} %bitcast.51, f32[256,1024]{1,0:T(8,128)} %bitcast.59, f32[256,1024]{1,0:T(8,128)} %copy-done.9, ...), custom_call_target="tpu_custom_call" | custom-call | bytes 5251072 | tf_op jit(solution)/shard_map/middle/pallas_call | solution.py:73
  31.4 5.1 %collective-permute-done.3.refs_13_ = f32[48,1024]{1,0:T(8,128)} collective-permute-done((f32[48,1024]{1,0:T(8,128)}, f32[48,1024]{1,0:T(8,128)}, u32[]{:S(2)}, u32[]{:S(2)}) %collective-permute-start.3) | collective-permute-done | bytes 196640 | tf_op jit(solution)/shard_map/ppermute | solution.py:627
  36.6 1.6 collective-permute-start.7
  38.6 10.0 %feed.1 = (bf16[256,2048]{1,0:T(8,128)(2,1)}, bf16[256,2048]{1,0:T(8,128)(2,1)}, f32[256,1024]{1,0:T(8,128)}, f32[256,1024]{1,0:T(8,128)}) custom-call(bf16[256,1024]{1,0:T(8,128)(2,1)} %get-tuple-element.119.low_ref.refs_21_, bf16[256,1024]{1,0:T(8,128)(2,1)} %bitcast.55, bf16[1024,2048]{1,0:T(8,128)(2,1)} %refs_20_.1, bf16[2048,1024]{1,0:T(8,128)(2,1)} %down_ref.3), custom_call_target="tpu_custom_call" | custom-call | flops 4294967296 | bytes 13631488 | tf_op jit(solution)/shard_map/feed/pallas_call | solution.py:73
  50.5 2.6 %collective-permute-start.13 = (f32[80,1024]{1,0:T(8,128)}, f32[80,1024]{1,0:T(8,128)S(1)}, u32[]{:S(2)}, u32[]{:S(2)}) collective-permute-start(f32[80,1024]{1,0:T(8,128)} %get-tuple-element.136), channel_id=1, source_target_pairs={{0,16},{1,17},{2,18},{3,19},{4,20},{5,21},{6,22},{7,23},{8,24},{9,... | collective-permute-start | bytes 983048 | tf_op jit(solution)/shard_map/ppermute | solution.py:627
  53.6 1.5 collective-permute-start.14
  55.1 10.5 %back.1 = (f32[256,1024]{1,0:T(8,128)}, bf16[256,1024]{1,0:T(8,128)(2,1)}, bf16[4,640,512]{2,1,0:T(8,128)(2,1)}, f32[4,640,512]{2,1,0:T(8,128)}, bf16[4,64,256]{...) custom-call(f32[256,1024]{1,0:T(8,128)} %get-tuple-element.187.mid_ref, ...), custom_call_target="tpu_custom_call" | custom-call | flops 1677721600 | bytes 19468288 | tf_op jit(solution)/shard_map/back/pallas_call | solution.py:73
  65.6 2.9 %collective-permute-done.14.refs_6_ = f32[48,1024]{1,0:T(8,128)S(1)} collective-permute-done((f32[48,1024]{1,0:T(8,128)S(1)}, f32[48,1024]{1,0:T(8,128)S(1)}, u32[]{:S(2)}, u32[]{:S(2)}) %collective-permute-start.14) | collective-permute-done | bytes 196640 | tf_op jit(solution)/shard_map/ppermute | solution.py:627
  69.1 1.4 collective-permute-start.19
  71.6 9.6 %small_grad.1 = (f32[8,64,1024]{2,1,0:T(8,128)}, f32[8,64,1024]{2,1,0:T(8,128)}) custom-call(s32[16]{0:T(128)} %broadcast_select_fusion.place_ref, bf16[2560,1024]{1,0:T(8,128)(2,1)} %bitcast.74, bf16[256,1024]{1,0:T(8,128)(2,1)} %get-tuple-element.143.gb_ref, bf16[2560,512]{1,0:T(8,128)(2,1)} %bitcast.50, bf16[256,256]{1,0:T(8,128)(2,1)} %bitcast.60, ...), custom_call_target="tpu_custom_call" | custom-call | flops 2684354560 | bytes 12845056 | tf_op jit(solution)/shard_map/small_grad/pallas_call | solution.py:73
  82.8 1.1 collective-permute-start.25
  84.5 5.6 %collective-permute-done.22.refs_9_ = f32[80,1024]{1,0:T(8,128)S(1)} collective-permute-done((f32[80,1024]{1,0:T(8,128)}, f32[80,1024]{1,0:T(8,128)S(1)}, u32[]{:S(2)}, u32[]{:S(2)}) %collective-permute-start.22) | collective-permute-done | bytes 327712 | tf_op jit(solution)/shard_map/ppermute | solution.py:620
  90.8 11.2 %down_side.1 = (f32[8,64,512]{2,1,0:T(8,128)}, f32[8,64,512]{2,1,0:T(8,128)}, bf16[1024,1024]{1,0:T(8,128)(2,1)}, bf16[1024,1024]{1,0:T(8,128)(2,1)}, f32[768,512]{1,0:T(8,128)}) custom-call(s32[1]{0:T(128)} %bitcast.10.member_ref, s32[16]{0:T(128)} %broadcast_select_fusion.1.place_ref, f32[128,1024]{1,0:T(8,128)} %copy-done.11, f32[128,1024]{1,0:T(8,128)} %copy-done.12, ...), custom_call_target="tpu_custom_call" | custom-call | bytes 20447232 | tf_op jit(solution)/shard_map/down_side/pallas_call | solution.py:73
  102.0 1.6 collective-permute-start.27
  103.5 1.7 collective-permute-done.24.gq_far_ref.refs_3_
  105.3 8.6 %up_side.1 = (f32[8,64,512]{2,1,0:T(8,128)}, f32[8,64,512]{2,1,0:T(8,128)}) custom-call(s32[1]{0:T(128)} %bitcast.10.member_ref, s32[16]{0:T(128)} %broadcast_select_fusion.1.place_ref, bf16[1024,1024]{1,0:T(8,128)(2,1)} %get-tuple-element.156.fl_ref, bf16[1024,1024]{1,0:T(8,128)(2,1)} %get-tuple-element.157.cl_ref, ...), custom_call_target="tpu_custom_call" | custom-call | bytes 13107200 | tf_op jit(solution)/shard_map/up_side/pallas_call | solution.py:73
  114.5 3.7 %slice_add_fusion = (f32[4,64,1024]{2,1,0:T(8,128)S(1)}, f32[4,64,1024]{2,1,0:T(8,128)}) fusion(f32[8,64,1024]{2,1,0:T(8,128)} %collective-permute-done.26, f32[8,64,1024]{2,1,0:T(8,128)} %get-tuple-element.166), kind=kLoop, calls=%fused_computation.1 | loop fusion | flops 524288 | bytes 6291456 | tf_op jit(solution)/shard_map/add | solution.py:660
  118.2 1.1 collective-permute-done.27
  119.4 2.2 %slice_add_fusion.6 = (f32[4,64,512]{2,1,0:T(8,128)}, f32[4,64,512]{2,1,0:T(8,128)S(1)}) fusion(f32[8,64,512]{2,1,0:T(8,128)} %collective-permute-done.27, f32[8,64,512]{2,1,0:T(8,128)S(1)} %copy-done.7), kind=kLoop, calls=%fused_computation.8 | loop fusion | flops 262144 | bytes 3145728 | tf_op jit(solution)/shard_map/add | solution.py:660
  122.1 2.6 %collective-permute-start.34 = (f32[4,64,1024]{2,1,0:T(8,128)}, f32[4,64,1024]{2,1,0:T(8,128)S(1)}, u32[]{:S(2)}, u32[]{:S(2)}) collective-permute-start(f32[4,64,1024]{2,1,0:T(8,128)} %get-tuple-element.202), channel_id=1, source_target_pairs={{0,16},{1,3},{2,18},{3,1},{4,20},{5,7},{6,22},{7,5},{8,24},{9,11},... | collective-permute-start | bytes 3145736 | tf_op jit(solution)/shard_map/ppermute | solution.py:627
  124.7 13.2 %inputs_back.2 = (bf16[4,576,1024]{2,1,0:T(8,128)(2,1)}, bf16[4,64,1024]{2,1,0:T(8,128)(2,1)}, f32[8,1024]{1,0:T(8,128)}) custom-call(bf16[4,640,512]{2,1,0:T(8,128)(2,1)} %get-tuple-element.178.gkv_ref.refs_0_, f32[4,640,512]{2,1,0:T(8,128)} %collective-permute-done.20.gkv_far_ref.refs_1_, bf16[4,64,256]{2,1,0:T(8,128)(2,1)} %get-tuple-element.145.gq_ref.refs_2_, ...), custom_call_target="tpu_custom_call" | custom-call | flops 2415919104 | bytes 24635392 | tf_op jit(solution)/shard_map/inputs_back/pallas_call | solution.py:73
  137.9 4.0 %collective-permute-done.28 = f32[4,64,512]{2,1,0:T(8,128)S(1)} collective-permute-done((f32[4,64,512]{2,1,0:T(8,128)}, f32[4,64,512]{2,1,0:T(8,128)S(1)}, u32[]{:S(2)}, u32[]{:S(2)}) %collective-permute-start.28) | collective-permute-done | bytes 524320 | tf_op jit(solution)/shard_map/ppermute | solution.py:627
  142.1 2.6 %slice_add_fusion.4 = (f32[4,64,512]{2,1,0:T(8,128)S(1)}, f32[4,64,512]{2,1,0:T(8,128)}) fusion(f32[8,64,512]{2,1,0:T(8,128)} %collective-permute-done.32, f32[8,64,512]{2,1,0:T(8,128)} %get-tuple-element.177), kind=kLoop, calls=%fused_computation.6 | loop fusion | flops 262144 | bytes 3145728 | tf_op jit(solution)/shard_map/add | solution.py:660
  144.6 0.8 slice_bitcast_fusion.4
  145.4 1.7 collective-permute-start.31
  147.1 1.1 collective-permute-start.30
  148.3 1.5 collective-permute-start.29
  149.8 13.0 %inputs_back.3 = (bf16[4,576,1024]{2,1,0:T(8,128)(2,1)}, bf16[4,64,1024]{2,1,0:T(8,128)(2,1)}, f32[8,1024]{1,0:T(8,128)}) custom-call(bf16[4,640,512]{2,1,0:T(8,128)(2,1)} %get-tuple-element.178.gkv_ref.refs_0_, f32[4,640,512]{2,1,0:T(8,128)} %collective-permute-done.20.gkv_far_ref.refs_1_, ...), custom_call_target="tpu_custom_call", output_to_operand_aliasing={{0}: (16, {}), {1}: (17, {})} | custom-call | flops 2415919104 | bytes 29845504 | tf_op jit(solution)/shard_map/inputs_back/pallas_call | solution.py:73
  165.0 1.8 collective-permute-start.36
  166.9 1.9 %collective-permute-start.40 = (f32[64,512]{1,0:T(8,128)S(1)}, f32[64,512]{1,0:T(8,128)S(1)}, u32[]{:S(2)}, u32[]{:S(2)}) collective-permute-start(f32[64,512]{1,0:T(8,128)S(1)} %get-tuple-element.211), channel_id=1, source_target_pairs={{0,18},{1,19},{2,16},{3,17},{4,22},{5,23},{6,20},{7,21},{8,26},{9,... | collective-permute-start | bytes 393224 | tf_op jit(solution)/shard_map/ppermute | solution.py:627
  168.8 1.8 collective-permute-start.38
  170.6 1.2 collective-permute-done.36
  172.1 2.3 %add_convert_fusion = bf16[256,1024]{1,0:T(8,128)(2,1)} fusion(f32[256,1024]{1,0:T(8,128)S(1)} %copy-done.4, f32[256,1024]{1,0:T(8,128)S(1)} %copy-done.6, f32[256,1024]{1,0:T(8,128)} %collective-permute-done.25), kind=kLoop, calls=%fused_computation.3 | loop fusion | flops 786432 | bytes 3670016 | tf_op jit(solution)/shard_map/convert_element_type | solution.py:857
  174.3 1.9 place_pieces.2
  176.3 2.2 %collective-permute-done.38.refs_2_ = f32[64,512]{1,0:T(8,128)S(1)} collective-permute-done((f32[64,512]{1,0:T(8,128)S(1)}, f32[64,512]{1,0:T(8,128)S(1)}, u32[]{:S(2)}, u32[]{:S(2)}) %collective-permute-start.38) | collective-permute-done | bytes 131104 | tf_op jit(solution)/shard_map/ppermute | solution.py:627
  178.6 1.8 collective-permute-start.41
  180.4 2.2 %collective-permute-done.41 = f32[8,1024]{1,0:T(8,128)S(1)} collective-permute-done((f32[8,1024]{1,0:T(8,128)S(1)}, f32[8,1024]{1,0:T(8,128)S(1)}, u32[]{:S(2)}, u32[]{:S(2)}) %collective-permute-start.41) | collective-permute-done | bytes 32800 | tf_op jit(solution)/shard_map/ppermute | solution.py:627
  182.6 2.0 %collective-permute-start.43 = (f32[1,64,1024]{2,1,0:T(8,128)S(1)}, f32[1,64,1024]{2,1,0:T(8,128)S(1)}, u32[]{:S(2)}, u32[]{:S(2)}) collective-permute-start(f32[1,64,1024]{2,1,0:T(8,128)S(1)} %get-tuple-element.209), channel_id=1, source_target_pairs={{0,8},{1,17},{2,10},{3,19},{4,12},{5,21},{6,14},{7,23},{8,0},{9,25... | collective-permute-start | bytes 786440 | tf_op jit(solution)/shard_map/ppermute | solution.py:627
  184.6 1.9 collective-permute-done.42
  186.6 1.9 %place_pieces.3 = f32[64,2048]{1,0:T(8,128)} custom-call(s32[1]{0:T(128)} %bitcast.10.member_ref, f32[64,512]{1,0:T(8,128)} %get-tuple-element.199.refs_0_, f32[64,512]{1,0:T(8,128)} %copy-done.28, f32[64,512]{1,0:T(8,128)} %copy-done.32, f32[64,512]{1,0:T(8,128)} %copy-done.31), custom_call_target="tpu_custom_call" | custom-call | bytes 1048576 | tf_op jit(solution)/shard_map/place_pieces/pallas_call | solution.py:73
  189.0 2.4 %collective-permute-done.43 = f32[1,64,1024]{2,1,0:T(8,128)S(1)} collective-permute-done((f32[1,64,1024]{2,1,0:T(8,128)S(1)}, f32[1,64,1024]{2,1,0:T(8,128)S(1)}, u32[]{:S(2)}, u32[]{:S(2)}) %collective-permute-start.43) | collective-permute-done | bytes 262176 | tf_op jit(solution)/shard_map/ppermute | solution.py:627
  (144 shorter events, 14.3 us)
Async XLA Ops:
  1.7 20.3 %collective-permute-start = (f32[128,1024]{1,0:T(8,128)S(1)}, f32[128,1024]{1,0:T(8,128)S(1)}, u32[]{:S(2)}, u32[]{:S(2)}) collective-permute-start(f32[128,1024]{1,0:T(8,128)S(1)} %dynamic-slice_convert_fusion), channel_id=1, source_target_pairs={{0,2},{1,3},{2,0},{3,1},{4,6},{5,7},{6,4},{7,5},{8,10},{9,11},{10,... | collective-permute-start | bytes 1572872 | tf_op jit(solution)/shard_map/ppermute | solution.py:627
  4.7 17.2 %collective-permute-start.1 = (f32[80,1024]{1,0:T(8,128)S(1)}, f32[80,1024]{1,0:T(8,128)S(1)}, u32[]{:S(2)}, u32[]{:S(2)}) collective-permute-start(f32[80,1024]{1,0:T(8,128)S(1)} %slice.160), channel_id=1, source_target_pairs={{0,16},{1,17},{2,18},{3,19},{4,20},{5,21},{6,22},{7,23},{8,24},{9,... | collective-permute-start | bytes 983048 | tf_op jit(solution)/shard_map/ppermute | solution.py:627
  7.4 17.2 %copy-start.3 = (bf16[1024,256]{1,0:T(8,128)(2,1)S(1)}, bf16[1024,256]{1,0:T(8,128)(2,1)}, u32[]{:S(2)}) copy-start(bf16[1024,256]{1,0:T(8,128)(2,1)} %refs_11_.1) | copy-start | bytes 1572868
  21.9 26.7 %copy-start.13 = (f32[80,1024]{1,0:T(8,128)}, f32[80,1024]{1,0:T(8,128)S(1)}, u32[]{:S(2)}) copy-start(f32[80,1024]{1,0:T(8,128)S(1)} %collective-permute-done.1.refs_12_) | copy-start | bytes 983044
  22.8 3.7 %collective-permute-start.2 = (f32[256,1024]{1,0:T(8,128)}, f32[256,1024]{1,0:T(8,128)S(1)}, u32[]{:S(2)}, u32[]{:S(2)}) collective-permute-start(f32[256,1024]{1,0:T(8,128)} %bitcast.58), channel_id=1, source_target_pairs={{0,1},{1,0},{2,3},{3,2},{4,5},{5,4},{6,7},{7,6},{8,9},{9,8},{10,11... | collective-permute-start | bytes 3145736 | tf_op jit(solution)/shard_map/ppermute | solution.py:620
  22.8 13.7 %collective-permute-start.5 = (f32[128,1024]{1,0:T(8,128)}, f32[128,1024]{1,0:T(8,128)}, u32[]{:S(2)}, u32[]{:S(2)}) collective-permute-start(f32[128,1024]{1,0:T(8,128)} %copy-done.10), channel_id=1, source_target_pairs={{0,1},{1,0},{2,3},{3,2},{4,5},{5,4},{6,7},{7,6},{8,9},{9,8},{10,11... | collective-permute-start | bytes 1572872 | tf_op jit(solution)/shard_map/ppermute | solution.py:620
  23.3 13.2 %collective-permute-start.4 = (f32[80,1024]{1,0:T(8,128)S(1)}, f32[80,1024]{1,0:T(8,128)}, u32[]{:S(2)}, u32[]{:S(2)}) collective-permute-start(f32[80,1024]{1,0:T(8,128)S(1)} %collective-permute-done.1.refs_12_), channel_id=1, source_target_pairs={{0,2},{1,3},{2,0},{3,1},{4,6},{5,7},{6,4},{7,5},{8,10},{9,11},{10,... | collective-permute-start | bytes 983048 | tf_op jit(solution)/shard_map/ppermute | solution.py:627
  24.5 12.0 %collective-permute-start.3 = (f32[48,1024]{1,0:T(8,128)}, f32[48,1024]{1,0:T(8,128)}, u32[]{:S(2)}, u32[]{:S(2)}) collective-permute-start(f32[48,1024]{1,0:T(8,128)} %slice.121), channel_id=1, source_target_pairs={{0,16},{1,17},{2,18},{3,19},{4,20},{5,21},{6,22},{7,23},{8,24},{9,... | collective-permute-start | bytes 589832 | tf_op jit(solution)/shard_map/ppermute | solution.py:627
  36.5 12.5 %collective-permute-start.10 = (f32[48,1024]{1,0:T(8,128)}, f32[48,1024]{1,0:T(8,128)S(1)}, u32[]{:S(2)}, u32[]{:S(2)}) collective-permute-start(f32[48,1024]{1,0:T(8,128)} %collective-permute-done.3.refs_13_), channel_id=1, source_target_pairs={{0,1},{1,0},{2,3},{3,2},{4,5},{5,4},{6,7},{7,6},{8,9},{9,8},{10,11... | collective-permute-start | bytes 589832 | tf_op jit(solution)/shard_map/ppermute | solution.py:620
  36.6 12.4 %collective-permute-start.7 = (f32[48,1024]{1,0:T(8,128)}, f32[48,1024]{1,0:T(8,128)S(1)}, u32[]{:S(2)}, u32[]{:S(2)}) collective-permute-start(f32[48,1024]{1,0:T(8,128)} %collective-permute-done.3.refs_13_), channel_id=1, source_target_pairs={{0,2},{1,3},{2,0},{3,1},{4,6},{5,7},{6,4},{7,5},{8,10},{9,11},{10,... | collective-permute-start | bytes 589832 | tf_op jit(solution)/shard_map/ppermute | solution.py:627
  38.1 10.9 %collective-permute-start.6 = (f32[48,1024]{1,0:T(8,128)}, f32[48,1024]{1,0:T(8,128)S(1)}, u32[]{:S(2)}, u32[]{:S(2)}) collective-permute-start(f32[48,1024]{1,0:T(8,128)} %get-tuple-element.121), channel_id=1, source_target_pairs={{0,16},{1,17},{2,18},{3,19},{4,20},{5,21},{6,22},{7,23},{8,24},{9,... | collective-permute-start | bytes 589832 | tf_op jit(solution)/shard_map/ppermute | solution.py:627
  38.1 10.9 %collective-permute-start.8 = (f32[80,1024]{1,0:T(8,128)S(1)}, f32[80,1024]{1,0:T(8,128)S(1)}, u32[]{:S(2)}, u32[]{:S(2)}) collective-permute-start(f32[80,1024]{1,0:T(8,128)S(1)} %collective-permute-done.1.refs_12_), channel_id=1, source_target_pairs={{0,1},{1,0},{2,3},{3,2},{4,5},{5,4},{6,7},{7,6},{8,9},{9,8},{10,11... | collective-permute-start | bytes 983048 | tf_op jit(solution)/shard_map/ppermute | solution.py:620
  38.3 10.8 %collective-permute-start.9 = (f32[80,1024]{1,0:T(8,128)}, f32[80,1024]{1,0:T(8,128)S(1)}, u32[]{:S(2)}, u32[]{:S(2)}) collective-permute-start(f32[80,1024]{1,0:T(8,128)} %collective-permute-done.4.refs_16_), channel_id=1, source_target_pairs={{0,1},{1,0},{2,3},{3,2},{4,5},{5,4},{6,7},{7,6},{8,9},{9,8},{10,11... | collective-permute-start | bytes 983048 | tf_op jit(solution)/shard_map/ppermute | solution.py:620
  49.0 20.1 %copy-start.22 = (f32[48,1024]{1,0:T(8,128)}, f32[48,1024]{1,0:T(8,128)S(1)}, u32[]{:S(2)}) copy-start(f32[48,1024]{1,0:T(8,128)S(1)} %collective-permute-done.6.refs_2_) | copy-start | bytes 589828
  49.0 20.1 %copy-start.21 = (f32[48,1024]{1,0:T(8,128)}, f32[48,1024]{1,0:T(8,128)S(1)}, u32[]{:S(2)}) copy-start(f32[48,1024]{1,0:T(8,128)S(1)} %collective-permute-done.7.refs_17_) | copy-start | bytes 589828
  49.9 3.7 %collective-permute-start.11 = (f32[256,1024]{1,0:T(8,128)}, f32[256,1024]{1,0:T(8,128)S(1)}, u32[]{:S(2)}, u32[]{:S(2)}) collective-permute-start(f32[256,1024]{1,0:T(8,128)} %get-tuple-element.128.own_ref), channel_id=1, source_target_pairs={{0,1},{1,0},{2,3},{3,2},{4,5},{5,4},{6,7},{7,6},{8,9},{9,8},{10,11... | collective-permute-start | bytes 3145736 | tf_op jit(solution)/shard_map/ppermute | solution.py:620
  50.0 18.5 %collective-permute-start.12 = (f32[128,1024]{1,0:T(8,128)S(1)}, f32[128,1024]{1,0:T(8,128)S(1)}, u32[]{:S(2)}, u32[]{:S(2)}) collective-permute-start(f32[128,1024]{1,0:T(8,128)S(1)} %copy-done.34), channel_id=1, source_target_pairs={{0,2},{1,3},{2,0},{3,1},{4,6},{5,7},{6,4},{7,5},{8,10},{9,11},{10,... | collective-permute-start | bytes 1572872 | tf_op jit(solution)/shard_map/ppermute | solution.py:627
  50.5 18.0 %collective-permute-start.13 = (f32[80,1024]{1,0:T(8,128)}, f32[80,1024]{1,0:T(8,128)S(1)}, u32[]{:S(2)}, u32[]{:S(2)}) collective-permute-start(f32[80,1024]{1,0:T(8,128)} %get-tuple-element.136), channel_id=1, source_target_pairs={{0,16},{1,17},{2,18},{3,19},{4,20},{5,21},{6,22},{7,23},{8,24},{9,... | collective-permute-start | bytes 983048 | tf_op jit(solution)/shard_map/ppermute | solution.py:627
  53.1 12.5 %collective-permute-start.16 = (f32[48,1024]{1,0:T(8,128)S(1)}, f32[48,1024]{1,0:T(8,128)S(1)}, u32[]{:S(2)}, u32[]{:S(2)}) collective-permute-start(f32[48,1024]{1,0:T(8,128)S(1)} %collective-permute-done.7.refs_17_), channel_id=1, source_target_pairs={{0,1},{1,0},{2,3},{3,2},{4,5},{5,4},{6,7},{7,6},{8,9},{9,8},{10,11... | collective-permute-start | bytes 589832 | tf_op jit(solution)/shard_map/ppermute | solution.py:620
  53.1 12.5 %collective-permute-start.15 = (f32[48,1024]{1,0:T(8,128)S(1)}, f32[48,1024]{1,0:T(8,128)S(1)}, u32[]{:S(2)}, u32[]{:S(2)}) collective-permute-start(f32[48,1024]{1,0:T(8,128)S(1)} %collective-permute-done.6.refs_2_), channel_id=1, source_target_pairs={{0,1},{1,0},{2,3},{3,2},{4,5},{5,4},{6,7},{7,6},{8,9},{9,8},{10,11... | collective-permute-start | bytes 589832 | tf_op jit(solution)/shard_map/ppermute | solution.py:620
  53.6 14.9 %collective-permute-start.14 = (f32[48,1024]{1,0:T(8,128)S(1)}, f32[48,1024]{1,0:T(8,128)S(1)}, u32[]{:S(2)}, u32[]{:S(2)}) collective-permute-start(f32[48,1024]{1,0:T(8,128)S(1)} %collective-permute-done.6.refs_2_), channel_id=1, source_target_pairs={{0,2},{1,3},{2,0},{3,1},{4,6},{5,7},{6,4},{7,5},{8,10},{9,11},{10,... | collective-permute-start | bytes 589832 | tf_op jit(solution)/shard_map/ppermute | solution.py:627
  68.5 12.7 %collective-permute-start.20 = (f32[4,640,512]{2,1,0:T(8,128)}, f32[4,640,512]{2,1,0:T(8,128)}, u32[]{:S(2)}, u32[]{:S(2)}) collective-permute-start(f32[4,640,512]{2,1,0:T(8,128)} %get-tuple-element.151), channel_id=1, source_target_pairs={{0,1},{1,0},{2,3},{3,2},{4,5},{5,4},{6,7},{7,6},{8,9},{9,8},{10,11... | collective-permute-start | bytes 15728648 | tf_op jit(solution)/shard_map/ppermute | solution.py:620
  68.6 12.6 %collective-permute-start.17 = (f32[128,1024]{1,0:T(8,128)S(1)}, f32[128,1024]{1,0:T(8,128)S(1)}, u32[]{:S(2)}, u32[]{:S(2)}) collective-permute-start(f32[128,1024]{1,0:T(8,128)S(1)} %collective-permute-done.12.refs_0_), channel_id=1, source_target_pairs={{0,1},{1,0},{2,3},{3,2},{4,5},{5,4},{6,7},{7,6},{8,9},{9,8},{10,11... | collective-permute-start | bytes 1572872 | tf_op jit(solution)/shard_map/ppermute | solution.py:620
  69.1 12.1 %collective-permute-start.19 = (f32[80,1024]{1,0:T(8,128)S(1)}, f32[80,1024]{1,0:T(8,128)S(1)}, u32[]{:S(2)}, u32[]{:S(2)}) collective-permute-start(f32[80,1024]{1,0:T(8,128)S(1)} %collective-permute-done.13.refs_3_), channel_id=1, source_target_pairs={{0,2},{1,3},{2,0},{3,1},{4,6},{5,7},{6,4},{7,5},{8,10},{9,11},{10,... | collective-permute-start | bytes 983048 | tf_op jit(solution)/shard_map/ppermute | solution.py:627
  70.5 10.7 %collective-permute-start.18 = (f32[80,1024]{1,0:T(8,128)S(1)}, f32[80,1024]{1,0:T(8,128)S(1)}, u32[]{:S(2)}, u32[]{:S(2)}) collective-permute-start(f32[80,1024]{1,0:T(8,128)S(1)} %collective-permute-done.13.refs_3_), channel_id=1, source_target_pairs={{0,1},{1,0},{2,3},{3,2},{4,5},{5,4},{6,7},{7,6},{8,9},{9,8},{10,11... | collective-permute-start | bytes 983048 | tf_op jit(solution)/shard_map/ppermute | solution.py:620
  71.1 10.1 %collective-permute-start.21 = (f32[48,1024]{1,0:T(8,128)S(1)}, f32[48,1024]{1,0:T(8,128)S(1)}, u32[]{:S(2)}, u32[]{:S(2)}) collective-permute-start(f32[48,1024]{1,0:T(8,128)S(1)} %collective-permute-done.14.refs_6_), channel_id=1, source_target_pairs={{0,1},{1,0},{2,3},{3,2},{4,5},{5,4},{6,7},{7,6},{8,9},{9,8},{10,11... | collective-permute-start | bytes 589832 | tf_op jit(solution)/shard_map/ppermute | solution.py:620
  82.2 23.0 %collective-permute-start.23 = (f32[1024,768]{1,0:T(8,128)}, f32[1024,768]{1,0:T(8,128)S(1)}, u32[]{:S(2)}, u32[]{:S(2)}) collective-permute-start(f32[1024,768]{1,0:T(8,128)} %maximum_convert_fusion), channel_id=1, source_target_pairs={{0,1},{1,0},{2,3},{3,2},{4,5},{5,4},{6,7},{7,6},{8,9},{9,8},{10,11... | collective-permute-start | bytes 9437192 | tf_op jit(solution)/shard_map/ppermute | solution.py:620
  82.2 32.3 %collective-permute-start.26 = (f32[8,64,1024]{2,1,0:T(8,128)}, f32[8,64,1024]{2,1,0:T(8,128)}, u32[]{:S(2)}, u32[]{:S(2)}) collective-permute-start(f32[8,64,1024]{2,1,0:T(8,128)} %get-tuple-element.167), channel_id=1, source_target_pairs={{0,2},{1,5},{2,0},{3,7},{4,6},{5,1},{6,4},{7,3},{8,10},{9,13},{10,... | collective-permute-start | bytes 6291464 | tf_op jit(solution)/shard_map/ppermute | solution.py:627
  82.8 22.4 %collective-permute-start.25 = (f32[256,1024]{1,0:T(8,128)}, f32[256,1024]{1,0:T(8,128)}, u32[]{:S(2)}, u32[]{:S(2)}) collective-permute-start(f32[256,1024]{1,0:T(8,128)} %get-tuple-element.163), channel_id=1, source_target_pairs={{0,1},{1,0},{2,3},{3,2},{4,5},{5,4},{6,7},{7,6},{8,9},{9,8},{10,11... | collective-permute-start | bytes 3145736 | tf_op jit(solution)/shard_map/ppermute | solution.py:620
  84.0 6.1 %collective-permute-start.22 = (f32[80,1024]{1,0:T(8,128)}, f32[80,1024]{1,0:T(8,128)S(1)}, u32[]{:S(2)}, u32[]{:S(2)}) collective-permute-start(f32[80,1024]{1,0:T(8,128)} %copy-done.17), channel_id=1, source_target_pairs={{0,1},{1,0},{2,3},{3,2},{4,5},{5,4},{6,7},{7,6},{8,9},{9,8},{10,11... | collective-permute-start | bytes 983048 | tf_op jit(solution)/shard_map/ppermute | solution.py:620
  102.0 17.4 %collective-permute-start.27 = (f32[8,64,512]{2,1,0:T(8,128)}, f32[8,64,512]{2,1,0:T(8,128)}, u32[]{:S(2)}, u32[]{:S(2)}) collective-permute-start(f32[8,64,512]{2,1,0:T(8,128)} %get-tuple-element.160), channel_id=1, source_target_pairs={{0,4},{1,9},{2,6},{3,11},{4,0},{5,13},{6,2},{7,15},{8,12},{9,1},{1... | collective-permute-start | bytes 3145736 | tf_op jit(solution)/shard_map/ppermute | solution.py:627
  103.5 1.7 collective-permute-start.24
  113.9 28.1 %collective-permute-start.32 = (f32[8,64,512]{2,1,0:T(8,128)}, f32[8,64,512]{2,1,0:T(8,128)}, u32[]{:S(2)}, u32[]{:S(2)}) collective-permute-start(f32[8,64,512]{2,1,0:T(8,128)} %get-tuple-element.165), channel_id=1, source_target_pairs={{0,4},{1,9},{2,6},{3,11},{4,0},{5,13},{6,2},{7,15},{8,12},{9,1},{1... | collective-permute-start | bytes 3145736 | tf_op jit(solution)/shard_map/ppermute | solution.py:627
  121.6 20.4 %collective-permute-start.28 = (f32[4,64,512]{2,1,0:T(8,128)}, f32[4,64,512]{2,1,0:T(8,128)S(1)}, u32[]{:S(2)}, u32[]{:S(2)}) collective-permute-start(f32[4,64,512]{2,1,0:T(8,128)} %get-tuple-element.207), channel_id=1, source_target_pairs={{0,8},{1,5},{2,10},{3,7},{4,12},{5,1},{6,14},{7,3},{8,0},{9,13},{1... | collective-permute-start | bytes 1572872 | tf_op jit(solution)/shard_map/ppermute | solution.py:627
  122.1 40.9 %collective-permute-start.34 = (f32[4,64,1024]{2,1,0:T(8,128)}, f32[4,64,1024]{2,1,0:T(8,128)S(1)}, u32[]{:S(2)}, u32[]{:S(2)}) collective-permute-start(f32[4,64,1024]{2,1,0:T(8,128)} %get-tuple-element.202), channel_id=1, source_target_pairs={{0,16},{1,3},{2,18},{3,1},{4,20},{5,7},{6,22},{7,5},{8,24},{9,11},... | collective-permute-start | bytes 3145736 | tf_op jit(solution)/shard_map/ppermute | solution.py:627
  144.6 18.3 %collective-permute-start.33 = (f32[4,64,512]{2,1,0:T(8,128)}, f32[4,64,512]{2,1,0:T(8,128)S(1)}, u32[]{:S(2)}, u32[]{:S(2)}) collective-permute-start(f32[4,64,512]{2,1,0:T(8,128)} %get-tuple-element.206), channel_id=1, source_target_pairs={{0,8},{1,5},{2,10},{3,7},{4,12},{5,1},{6,14},{7,3},{8,0},{9,13},{1... | collective-permute-start | bytes 1572872 | tf_op jit(solution)/shard_map/ppermute | solution.py:627
  145.4 17.4 %collective-permute-start.31 = (f32[64,512]{1,0:T(8,128)}, f32[64,512]{1,0:T(8,128)S(1)}, u32[]{:S(2)}, u32[]{:S(2)}) collective-permute-start(f32[64,512]{1,0:T(8,128)} %get-tuple-element.215), channel_id=1, source_target_pairs={{0,18},{1,19},{2,16},{3,17},{4,22},{5,23},{6,20},{7,21},{8,26},{9,... | collective-permute-start | bytes 393224 | tf_op jit(solution)/shard_map/ppermute | solution.py:627
  147.1 15.7 %collective-permute-start.30 = (f32[64,512]{1,0:T(8,128)}, f32[64,512]{1,0:T(8,128)S(1)}, u32[]{:S(2)}, u32[]{:S(2)}) collective-permute-start(f32[64,512]{1,0:T(8,128)} %get-tuple-element.216), channel_id=1, source_target_pairs={{0,16},{1,17},{2,18},{3,19},{4,20},{5,21},{6,22},{7,23},{8,24},{9,... | collective-permute-start | bytes 393224 | tf_op jit(solution)/shard_map/ppermute | solution.py:627
  148.3 14.6 %collective-permute-start.29 = (f32[64,512]{1,0:T(8,128)}, f32[64,512]{1,0:T(8,128)S(1)}, u32[]{:S(2)}, u32[]{:S(2)}) collective-permute-start(f32[64,512]{1,0:T(8,128)} %get-tuple-element.217), channel_id=1, source_target_pairs={{0,2},{1,3},{2,0},{3,1},{4,6},{5,7},{6,4},{7,5},{8,10},{9,11},{10,... | collective-permute-start | bytes 393224 | tf_op jit(solution)/shard_map/ppermute | solution.py:627
  163.2 13.1 %collective-permute-start.37 = (f32[2,64,1024]{2,1,0:T(8,128)S(1)}, f32[2,64,1024]{2,1,0:T(8,128)S(1)}, u32[]{:S(2)}, u32[]{:S(2)}) collective-permute-start(f32[2,64,1024]{2,1,0:T(8,128)S(1)} %get-tuple-element.204), channel_id=1, source_target_pairs={{0,4},{1,9},{2,6},{3,11},{4,0},{5,13},{6,2},{7,15},{8,12},{9,1},{1... | collective-permute-start | bytes 1572872 | tf_op jit(solution)/shard_map/ppermute | solution.py:627
  164.4 6.3 %collective-permute-start.35 = (f32[64,512]{1,0:T(8,128)S(1)}, f32[64,512]{1,0:T(8,128)S(1)}, u32[]{:S(2)}, u32[]{:S(2)}) collective-permute-start(f32[64,512]{1,0:T(8,128)S(1)} %get-tuple-element.214), channel_id=1, source_target_pairs={{0,2},{1,3},{2,0},{3,1},{4,6},{5,7},{6,4},{7,5},{8,10},{9,11},{10,... | collective-permute-start | bytes 393224 | tf_op jit(solution)/shard_map/ppermute | solution.py:627
  165.0 6.8 %collective-permute-start.36 = (f32[8,1024]{1,0:T(8,128)S(1)}, f32[8,1024]{1,0:T(8,128)S(1)}, u32[]{:S(2)}, u32[]{:S(2)}) collective-permute-start(f32[8,1024]{1,0:T(8,128)S(1)} %copy-done.33), channel_id=1, source_target_pairs={{0,16},{1,17},{2,18},{3,19},{4,20},{5,21},{6,22},{7,23},{8,24},{9,... | collective-permute-start | bytes 98312 | tf_op jit(solution)/shard_map/ppermute | solution.py:627
  166.9 13.5 %collective-permute-start.40 = (f32[64,512]{1,0:T(8,128)S(1)}, f32[64,512]{1,0:T(8,128)S(1)}, u32[]{:S(2)}, u32[]{:S(2)}) collective-permute-start(f32[64,512]{1,0:T(8,128)S(1)} %get-tuple-element.211), channel_id=1, source_target_pairs={{0,18},{1,19},{2,16},{3,17},{4,22},{5,23},{6,20},{7,21},{8,26},{9,... | collective-permute-start | bytes 393224 | tf_op jit(solution)/shard_map/ppermute | solution.py:627
  168.8 9.8 %collective-permute-start.38 = (f32[64,512]{1,0:T(8,128)S(1)}, f32[64,512]{1,0:T(8,128)S(1)}, u32[]{:S(2)}, u32[]{:S(2)}) collective-permute-start(f32[64,512]{1,0:T(8,128)S(1)} %get-tuple-element.212), channel_id=1, source_target_pairs={{0,16},{1,17},{2,18},{3,19},{4,20},{5,21},{6,22},{7,23},{8,24},{9,... | collective-permute-start | bytes 393224 | tf_op jit(solution)/shard_map/ppermute | solution.py:627
  171.9 6.7 %collective-permute-start.39 = (f32[8,1024]{1,0:T(8,128)S(1)}, f32[8,1024]{1,0:T(8,128)S(1)}, u32[]{:S(2)}, u32[]{:S(2)}) collective-permute-start(f32[8,1024]{1,0:T(8,128)S(1)} %add.122), channel_id=1, source_target_pairs={{0,2},{1,3},{2,0},{3,1},{4,6},{5,7},{6,4},{7,5},{8,10},{9,11},{10,... | collective-permute-start | bytes 98312 | tf_op jit(solution)/shard_map/ppermute | solution.py:627
  178.6 4.0 %collective-permute-start.41 = (f32[8,1024]{1,0:T(8,128)S(1)}, f32[8,1024]{1,0:T(8,128)S(1)}, u32[]{:S(2)}, u32[]{:S(2)}) collective-permute-start(f32[8,1024]{1,0:T(8,128)S(1)} %add.128), channel_id=1, source_target_pairs={{0,4},{1,5},{2,6},{3,7},{4,0},{5,1},{6,2},{7,3},{8,12},{9,13},{10,... | collective-permute-start | bytes 98312 | tf_op jit(solution)/shard_map/ppermute | solution.py:627
  182.6 3.9 %collective-permute-start.42 = (f32[8,1024]{1,0:T(8,128)S(1)}, f32[8,1024]{1,0:T(8,128)S(1)}, u32[]{:S(2)}, u32[]{:S(2)}) collective-permute-start(f32[8,1024]{1,0:T(8,128)S(1)} %add.129), channel_id=1, source_target_pairs={{0,8},{1,9},{2,10},{3,11},{4,12},{5,13},{6,14},{7,15},{8,0},{9,1},... | collective-permute-start | bytes 98312 | tf_op jit(solution)/shard_map/ppermute | solution.py:627
  182.6 8.8 %collective-permute-start.43 = (f32[1,64,1024]{2,1,0:T(8,128)S(1)}, f32[1,64,1024]{2,1,0:T(8,128)S(1)}, u32[]{:S(2)}, u32[]{:S(2)}) collective-permute-start(f32[1,64,1024]{2,1,0:T(8,128)S(1)} %get-tuple-element.209), channel_id=1, source_target_pairs={{0,8},{1,17},{2,10},{3,19},{4,12},{5,21},{6,14},{7,23},{8,0},{9,25... | collective-permute-start | bytes 786440 | tf_op jit(solution)/shard_map/ppermute | solution.py:627
  (31 other events, 193.8 us)

commit v5 on v4

--- a/solution.py
+++ b/solution.py
@@ -602,7 +602,7 @@
 
 def plan(bits):
     if bits == 4:
-        return (0, 3), ([1, 2], [2, 1]), ([0, 3, 1, 2], [1, 0, 2, 3])
+        return (0, 3), ([1, 2], [2, 1]), ([0, 1, 2, 3], [1, 0, 3, 2])
     top = bits - 1
     rest = list(range(2, top - 1))
     wide_ = ([top, top - 1] + rest, [top - 1, top] + rest)
@@ -740,20 +740,21 @@
         + [((r, width), SINGLE, pl.BlockSpec((r, width), lambda at, c: (0, 0))) for r in (half - cut, cut)],
         prefetch=(core,),
     )
-    low, low_send, low_first, weights_send, cot_far_a, cot_far_b, cot_both_a = lax.optimization_barrier(
-        (low, low_send, low_first, weights_send, cot_far_a, cot_far_b, cot_both_a, cot_near_other)
-    )[:7]
+    weights_far = links.swap(weights_send)
+    low, low_send, low_first, cot_far_a, cot_far_b, cot_both_a = lax.optimization_barrier(
+        (low, low_send, low_first, cot_far_a, cot_far_b, cot_both_a, cot_near_other, weights_far)
+    )[:6]
     low_far_a = links.send(low_first, far_bit, far_bit)
     cot_both_b = links.send(cot_far_b, near_bit, near_bit)
     cot_far_a_other, cot_both_a_other = links.swap(cot_far_a), links.swap(cot_both_a)
     cot_far_b_other = links.swap(cot_far_b)
     hidden, grad_pre, part, feed_out = feed(low, cot, up_weight, down_weight)
-    part, low_far_a, low_send, low_second, weights_send, cot_both_b = lax.optimization_barrier(
+    part, low_far_a, low_send, low_second, cot_both_b = lax.optimization_barrier(
         (
-            part, low_far_a, low_send, low_second, weights_send, cot_both_b,
+            part, low_far_a, low_send, low_second, cot_both_b,
             cot_far_a_other, cot_both_a_other, cot_far_b_other,
         )
-    )[:6]
+    )[:5]
     part_far = links.swap(part)
     low_far_b = links.send(low_second, far_bit, far_bit)
     low_near = links.send(low_send, near_bit, near_bit)
@@ -784,15 +785,15 @@
         images,
         patches,
     )
-    small_leave, low_both_b, gq_send, feed_out, weights_send = lax.optimization_barrier(
+    small_leave, low_both_b, gq_send, feed_out = lax.optimization_barrier(
         (
-            small_leave, low_both_b, gq_send, feed_out, weights_send,
+            small_leave, low_both_b, gq_send, feed_out,
             gkv_far, low_near_other, low_far_b_other, low_both_a_other,
         )
-    )[:5]
+    )[:4]
     low_both_b_other = links.swap(low_both_b)
     small = Halving(links, small_leave, small_keep, small_orders)
-    weights_far, gq_far = links.swap(weights_send), links.swap(gq_send)
+    gq_far = links.swap(gq_send)
     feed_far = links.swap(feed_out)
     place = links.places(wide_orders, group)
     down_leave, down_keep, fl, cl, slope = down_side(
@@ -813,57 +814,48 @@
         devices,
     )
     down = Halving(links, down_leave, down_keep, wide_orders)
-    up_leave, up_keep = up_side(
-        member,
-        place,
-        fl,
-        cl,
-        slope,
-        down_weight,
-        after(grad_pre, down_leave, weights_far, gq_far, feed_far),
-        devices,
-    )
-    up = Halving(links, up_leave, up_keep, wide_orders)
-    done = down.advance(small.advance(up_leave))
     inputs = (gkv_far, gq, gq_far, media, mean, inv, latents)
     inputs += (grad_middle.reshape(images, latent_rows, width),)
     weights = (query_weight, key_weight, value_weight, weights_far, vectors[0], vectors[2])
     part = images // 2
-    early = inputs_back(0, part, (), after(gkv, done), *inputs, weights + (feed_vec,))
+    early = inputs_back(0, part, (), after(gkv, down_leave), *inputs, weights + (feed_vec,))
+    done = down.advance(small.advance(early[2], feed_far))
+    up_leave, up_keep = up_side(
+        member, place, fl, cl, slope, down_weight, after(grad_pre, done), devices
+    )
 
     hops = [near_bit * (at & 1) + far_bit * (at >> 1) for at in range(GROUP)]
 
     def pieces(mixed):
         return [mixed[0]] + [links.send(mixed[at], hops[at], hops[at]) for at in range(1, GROUP)]
 
-    done = early[2]
+    done = up_leave
     while down.left > 1:
         done = down.advance(done)
     mixed = down.advance(done)
+    up = Halving(links, after(up_leave, mixed), up_keep, wide_orders)
     down_pieces = pieces(mixed)
-    done = mixed
+    grad_media, grad_latents, vec = inputs_back(
+        part, images - part, early[:2], after(gkv, mixed), *inputs, weights + (early[2],)
+    )
+    down_pieces = list(lax.optimization_barrier(tuple(down_pieces) + (vec,)))
+    done = vec = down_pieces.pop()
     while up.left > 1:
         done = up.advance(done)
-    grad_media, grad_latents, vec = inputs_back(
-        part, images - part, early[:2], after(gkv, done), *inputs, weights + (early[2],)
-    )
-    down_pieces = list(lax.optimization_barrier(tuple(down_pieces) + (vec,)))
-    vec = down_pieces.pop()
-    mixed = up.advance(vec)
+    vec = Total(links, after(vec, done), [group[1], group[0]] + wide_orders[0])
+    done = small.advance(vec.array)
+    done = result = (after(middle, done) + (feed_out + feed_far)).astype(HALF)
+    done = vec.advance(done)
+    mixed = up.advance(done)
     up_pieces = pieces(mixed)
-    vec = Total(links, after(vec, mixed), [group[1], group[0]] + wide_orders[0])
-    done = small.advance(vec.array)
-    done = vec.advance(done, up_pieces[1])
-    done = result = (after(middle, done) + (feed_out + feed_far)).astype(HALF)
+    done = vec.advance(mixed, up_pieces[1])
     down_pieces[0] = after(down_pieces[0], done)
     done = grad_down = place_pieces(member, down_pieces)
-    while small.left > 1:
-        done = small.advance(done)
-    done = vec.advance(done, up_pieces[2])
-    done = vec.advance(done, up_pieces[3])
     while vec.order:
         done = vec.advance(done)
-    vec = vec.advance(done)
+    while small.left > 1:
+        done = small.advance(done, up_pieces[2])
+    vec = vec.advance(done, up_pieces[3])
     vec = lax.dynamic_slice_in_dim(vec, links.row * share, share, 1)
     up_pieces[0] = after(up_pieces[0], vec)
     grad_up = place_pieces(member, up_pieces)

time: 193 us -> 193 us (level)
  starting transfers between devices: 38.8 us -> 41.5 us
    ppermute x28, starting transfers between devices: 34.9 us -> 38.3 us  [send(): return lax.ppermute(array, ('dp', 'tensor'), pairs)]
    unnamed x70 -> x64, local copies, waits for them, and re-layouts: 4.52 us -> 3.13 us
  transfers between devices with their start and end apart: 44 -> 44, of which waited for: 12 -> 14; matrix products, arithmetic and copies ran while one was open for 9% -> 7% of each run, Pallas kernels for 51% -> 51%
where the time goes in v5:
time: 193 us; the launch traced here: 192 us
  Pallas kernels  98.2 us (51%)
  starting transfers between devices  41.5 us (22%)
  waiting for transfers between devices  30.3 us (16%)
  other arithmetic  13.5 us (7%)
  local copies, waits for them, and re-layouts  7.46 us (4%)
    pallas_call x11, Pallas kernels, call(): pl.pallas_call(body, out_shape=shapes, grid_spec=pltpu.PrefetchScalarGrid...  98.2 us
    ppermute x28, starting transfers between devices, send(): return lax.ppermute(array, ('dp', 'tensor'), pairs)  38.3 us
    ppermute x28, waiting for transfers between devices, send(): return lax.ppermute(array, ('dp', 'tensor'), pairs)  22 us
    ppermute x16, waiting for transfers between devices, swap(): return lax.ppermute(array, 'tensor', [(0, 1), (1, 0)])  8.31 us
    add x3, other arithmetic, advance(): keep[half:] + self.come[half:]  5.53 us
  transfers between devices with their start and end apart: 44, of which 14 were waited for; matrix products, arithmetic and copies ran while one was open for 7% of the time, Pallas kernels for 51%

profile of v5, /device:TPU:0, one launch (start us, length us, event | category | flops | bytes accessed | tf_op | source)
XLA Modules:
  0.0 192.2 jit_solution(12462442524856051836)
XLA Ops:
  0.6 1.0 dynamic-slice_convert_fusion
  1.7 3.0 %collective-permute-start = (f32[128,1024]{1,0:T(8,128)S(1)}, f32[128,1024]{1,0:T(8,128)}, u32[]{:S(2)}, u32[]{:S(2)}) collective-permute-start(f32[128,1024]{1,0:T(8,128)S(1)} %dynamic-slice_convert_fusion), channel_id=1, source_target_pairs={{0,2},{1,3},{2,0},{3,1},{4,6},{5,7},{6,4},{7,5},{8,10},{9,11},{10,... | collective-permute-start | bytes 1572872 | tf_op jit(solution)/shard_map/ppermute | solution.py:627
  4.7 2.7 %collective-permute-start.1 = (f32[80,1024]{1,0:T(8,128)S(1)}, f32[80,1024]{1,0:T(8,128)S(1)}, u32[]{:S(2)}, u32[]{:S(2)}) collective-permute-start(f32[80,1024]{1,0:T(8,128)S(1)} %slice.160), channel_id=1, source_target_pairs={{0,16},{1,17},{2,18},{3,19},{4,20},{5,21},{6,22},{7,23},{8,24},{9,... | collective-permute-start | bytes 983048 | tf_op jit(solution)/shard_map/ppermute | solution.py:627
  7.4 14.5 %attend.1 = (bf16[4,640,1024]{2,1,0:T(8,128)(2,1)}, bf16[4,64,256]{2,1,0:T(8,128)(2,1)}, bf16[4,640,256]{2,1,0:T(8,128)(2,1)}, bf16[4,640,256]{2,1,0:T(8,128)(2,...) custom-call(s32[4]{0:T(128)} %buckets_ref.1, ...), custom_call_target="tpu_custom_call" | custom-call | flops 3355443200 | bytes 19171328 | tf_op jit(solution)/shard_map/attend/pallas_call | solution.py:73
  22.0 1.9 maximum_convert_fusion
  24.9 1.6 slice.121
  26.6 4.6 %collective-permute-done.2.far_ref = f32[256,1024]{1,0:T(8,128)S(1)} collective-permute-done((f32[256,1024]{1,0:T(8,128)S(1)}, f32[256,1024]{1,0:T(8,128)S(1)}, u32[]{:S(2)}, u32[]{:S(2)}) %collective-permute-start.2) | collective-permute-done | bytes 1048608 | tf_op jit(solution)/shard_map/ppermute | solution.py:620
  31.2 1.0 copy-done.14
  32.2 3.9 %middle.1 = (f32[256,1024]{1,0:T(8,128)}, bf16[256,1024]{1,0:T(8,128)(2,1)}, f32[128,1024]{1,0:T(8,128)}, f32[48,1024]{1,0:T(8,128)}, f32[80,1024]{1,0:T(8,128)}) custom-call(s32[1]{0:T(128)} %bitcast.core_ref, bf16[256,1024]{1,0:T(8,128)(2,1)} %bitcast.51, f32[256,1024]{1,0:T(8,128)} %bitcast.58, f32[256,1024]{1,0:T(8,128)} %copy-done.14, ...), custom_call_target="tpu_custom_call" | custom-call | bytes 5251072 | tf_op jit(solution)/shard_map/middle/pallas_call | solution.py:73
  36.1 2.9 %collective-permute-done.3.refs_13_ = f32[48,1024]{1,0:T(8,128)} collective-permute-done((f32[48,1024]{1,0:T(8,128)}, f32[48,1024]{1,0:T(8,128)}, u32[]{:S(2)}, u32[]{:S(2)}) %collective-permute-start.3) | collective-permute-done | bytes 196640 | tf_op jit(solution)/shard_map/ppermute | solution.py:627
  39.1 1.6 collective-permute-start.8
  41.2 10.0 %feed.1 = (bf16[256,2048]{1,0:T(8,128)(2,1)}, bf16[256,2048]{1,0:T(8,128)(2,1)}, f32[256,1024]{1,0:T(8,128)}, f32[256,1024]{1,0:T(8,128)}) custom-call(bf16[256,1024]{1,0:T(8,128)(2,1)} %get-tuple-element.118.low_ref.refs_21_, bf16[256,1024]{1,0:T(8,128)(2,1)} %bitcast.55, bf16[1024,2048]{1,0:T(8,128)(2,1)} %refs_20_.1, bf16[2048,1024]{1,0:T(8,128)(2,1)} %down_ref.3), custom_call_target="tpu_custom_call" | custom-call | flops 4294967296 | bytes 13631488 | tf_op jit(solution)/shard_map/feed/pallas_call | solution.py:73
  52.3 2.5 %collective-permute-start.14 = (f32[80,1024]{1,0:T(8,128)}, f32[80,1024]{1,0:T(8,128)S(1)}, u32[]{:S(2)}, u32[]{:S(2)}) collective-permute-start(f32[80,1024]{1,0:T(8,128)} %get-tuple-element.134), channel_id=1, source_target_pairs={{0,16},{1,17},{2,18},{3,19},{4,20},{5,21},{6,22},{7,23},{8,24},{9,... | collective-permute-start | bytes 983048 | tf_op jit(solution)/shard_map/ppermute | solution.py:627
  55.3 1.5 collective-permute-start.15
  56.8 10.5 %back.1 = (f32[256,1024]{1,0:T(8,128)}, bf16[256,1024]{1,0:T(8,128)(2,1)}, bf16[4,640,512]{2,1,0:T(8,128)(2,1)}, f32[4,640,512]{2,1,0:T(8,128)}, bf16[4,64,256]{...) custom-call(f32[256,1024]{1,0:T(8,128)} %get-tuple-element.181.mid_ref, ...), custom_call_target="tpu_custom_call" | custom-call | flops 1677721600 | bytes 19468288 | tf_op jit(solution)/shard_map/back/pallas_call | solution.py:73
  67.3 3.2 %collective-permute-done.15.refs_6_ = f32[48,1024]{1,0:T(8,128)} collective-permute-done((f32[48,1024]{1,0:T(8,128)}, f32[48,1024]{1,0:T(8,128)}, u32[]{:S(2)}, u32[]{:S(2)}) %collective-permute-start.15) | collective-permute-done | bytes 196640 | tf_op jit(solution)/shard_map/ppermute | solution.py:627
  71.2 1.1 collective-permute-start.20
  73.3 9.7 %small_grad.1 = (f32[8,64,1024]{2,1,0:T(8,128)}, f32[8,64,1024]{2,1,0:T(8,128)}) custom-call(s32[16]{0:T(128)} %broadcast_select_fusion.1.place_ref, bf16[2560,1024]{1,0:T(8,128)(2,1)} %bitcast.74, bf16[256,1024]{1,0:T(8,128)(2,1)} %get-tuple-element.137.gb_ref, bf16[2560,512]{1,0:T(8,128)(2,1)} %bitcast.50, bf16[256,256]{1,0:T(8,128)(2,1)} %bitcast.60, ...), custom_call_target="tpu_custom_call" | custom-call | flops 2684354560 | bytes 12845056 | tf_op jit(solution)/shard_map/small_grad/pallas_call | solution.py:73
  85.1 2.1 %collective-permute-done.23.refs_9_ = f32[80,1024]{1,0:T(8,128)S(1)} collective-permute-done((f32[80,1024]{1,0:T(8,128)S(1)}, f32[80,1024]{1,0:T(8,128)S(1)}, u32[]{:S(2)}, u32[]{:S(2)}) %collective-permute-start.23) | collective-permute-done | bytes 327712 | tf_op jit(solution)/shard_map/ppermute | solution.py:620
  87.9 11.3 %down_side.1 = (f32[8,64,512]{2,1,0:T(8,128)}, f32[8,64,512]{2,1,0:T(8,128)}, bf16[1024,1024]{1,0:T(8,128)(2,1)}, bf16[1024,1024]{1,0:T(8,128)(2,1)}, f32[768,512]{1,0:T(8,128)}) custom-call(s32[1]{0:T(128)} %bitcast.14.member_ref, s32[16]{0:T(128)} %broadcast_select_fusion.place_ref, f32[128,1024]{1,0:T(8,128)} %copy-done.15, f32[128,1024]{1,0:T(8,128)} %copy-done.16, ...), custom_call_target="tpu_custom_call" | custom-call | bytes 20447232 | tf_op jit(solution)/shard_map/down_side/pallas_call | solution.py:73
  99.3 1.6 collective-permute-start.27
  100.8 1.5 collective-permute-done.24.gq_far_ref.refs_3_
  103.1 13.1 %inputs_back.2 = (bf16[4,576,1024]{2,1,0:T(8,128)(2,1)}, bf16[4,64,1024]{2,1,0:T(8,128)(2,1)}, f32[8,1024]{1,0:T(8,128)}) custom-call(bf16[4,640,512]{2,1,0:T(8,128)(2,1)} %get-tuple-element.171.gkv_ref.refs_0_, f32[4,640,512]{2,1,0:T(8,128)} %collective-permute-done.21.gkv_far_ref.refs_1_, bf16[4,64,256]{2,1,0:T(8,128)(2,1)} %get-tuple-element.139.gq_ref.refs_2_, ...), custom_call_target="tpu_custom_call" | custom-call | flops 2415919104 | bytes 24635392 | tf_op jit(solution)/shard_map/inputs_back/pallas_call | solution.py:73
  116.2 3.0 %slice_add_fusion.1 = (f32[4,64,1024]{2,1,0:T(8,128)S(1)}, f32[4,64,1024]{2,1,0:T(8,128)}) fusion(f32[8,64,1024]{2,1,0:T(8,128)} %collective-permute-done.26, f32[8,64,1024]{2,1,0:T(8,128)S(1)} %copy-done.5), kind=kLoop, calls=%fused_computation.2 | loop fusion | flops 524288 | bytes 6291456 | tf_op jit(solution)/shard_map/add | solution.py:660
  119.8 1.4 slice_add_fusion.6
  122.1 8.4 %up_side.1 = (f32[8,64,512]{2,1,0:T(8,128)}, f32[8,64,512]{2,1,0:T(8,128)}) custom-call(s32[1]{0:T(128)} %bitcast.14.member_ref, s32[16]{0:T(128)} %broadcast_select_fusion.place_ref, bf16[1024,1024]{1,0:T(8,128)(2,1)} %get-tuple-element.164.fl_ref, bf16[1024,1024]{1,0:T(8,128)(2,1)} %get-tuple-element.165.cl_ref, f32[768,512]{1,0:T(8,128)} %get-tuple-element.166.slope_ref, ...), custom_call_target="tpu_custom_call" | custom-call | bytes 13107200 | tf_op jit(solution)/shard_map/up_side/pallas_call | solution.py:73
  130.6 1.5 collective-permute-start.32
  133.4 2.8 %collective-permute-start.31 = (f32[64,512]{1,0:T(8,128)}, f32[64,512]{1,0:T(8,128)S(1)}, u32[]{:S(2)}, u32[]{:S(2)}) collective-permute-start(f32[64,512]{1,0:T(8,128)} %get-tuple-element.211), channel_id=1, source_target_pairs={{0,18},{1,19},{2,16},{3,17},{4,22},{5,23},{6,20},{7,21},{8,26},{9,... | collective-permute-start | bytes 393224 | tf_op jit(solution)/shard_map/ppermute | solution.py:627
  136.2 1.0 collective-permute-start.30
  137.8 13.1 %inputs_back.3 = (bf16[4,576,1024]{2,1,0:T(8,128)(2,1)}, bf16[4,64,1024]{2,1,0:T(8,128)(2,1)}, f32[8,1024]{1,0:T(8,128)}) custom-call(bf16[4,640,512]{2,1,0:T(8,128)(2,1)} %get-tuple-element.171.gkv_ref.refs_0_, f32[4,640,512]{2,1,0:T(8,128)} %collective-permute-done.21.gkv_far_ref.refs_1_, ...), custom_call_target="tpu_custom_call", output_to_operand_aliasing={{0}: (16, {}), {1}: (17, {})} | custom-call | flops 2415919104 | bytes 29845504 | tf_op jit(solution)/shard_map/inputs_back/pallas_call | solution.py:73
  151.0 1.6 slice_add_fusion.2
  152.6 1.3 collective-permute-start.35
  153.8 2.0 %collective-permute-start.34 = (f32[8,1024]{1,0:T(8,128)S(1)}, f32[8,1024]{1,0:T(8,128)S(1)}, u32[]{:S(2)}, u32[]{:S(2)}) collective-permute-start(f32[8,1024]{1,0:T(8,128)S(1)} %copy-done.30), channel_id=1, source_target_pairs={{0,16},{1,17},{2,18},{3,19},{4,20},{5,21},{6,22},{7,23},{8,24},{9,... | collective-permute-start | bytes 98312 | tf_op jit(solution)/shard_map/ppermute | solution.py:627
  155.8 3.2 %collective-permute-done.33 = f32[4,64,1024]{2,1,0:T(8,128)S(1)} collective-permute-done((f32[4,64,1024]{2,1,0:T(8,128)}, f32[4,64,1024]{2,1,0:T(8,128)S(1)}, u32[]{:S(2)}, u32[]{:S(2)}) %collective-permute-start.33) | collective-permute-done | bytes 1048608 | tf_op jit(solution)/shard_map/ppermute | solution.py:627
  160.0 1.2 collective-permute-start.40
  161.2 2.3 %add_convert_fusion = bf16[256,1024]{1,0:T(8,128)(2,1)} fusion(f32[256,1024]{1,0:T(8,128)S(1)} %copy-done.4, f32[256,1024]{1,0:T(8,128)S(1)} %copy-done.9, f32[256,1024]{1,0:T(8,128)} %collective-permute-done.25), kind=kLoop, calls=%fused_computation.3 | loop fusion | flops 786432 | bytes 3670016 | tf_op jit(solution)/shard_map/convert_element_type | solution.py:847
  163.5 1.6 collective-permute-done.34
  165.1 1.0 collective-permute-done.35
  167.7 3.2 %collective-permute-start.39 = (f32[64,512]{1,0:T(8,128)S(1)}, f32[64,512]{1,0:T(8,128)S(1)}, u32[]{:S(2)}, u32[]{:S(2)}) collective-permute-start(f32[64,512]{1,0:T(8,128)S(1)} %get-tuple-element.209), channel_id=1, source_target_pairs={{0,16},{1,17},{2,18},{3,19},{4,20},{5,21},{6,22},{7,23},{8,24},{9,... | collective-permute-start | bytes 393224 | tf_op jit(solution)/shard_map/ppermute | solution.py:627
  171.9 2.9 %collective-permute-done.37 = f32[8,1024]{1,0:T(8,128)S(1)} collective-permute-done((f32[8,1024]{1,0:T(8,128)S(1)}, f32[8,1024]{1,0:T(8,128)S(1)}, u32[]{:S(2)}, u32[]{:S(2)}) %collective-permute-start.37) | collective-permute-done | bytes 32800 | tf_op jit(solution)/shard_map/ppermute | solution.py:627
  174.8 1.6 collective-permute-start.38
  176.4 1.1 collective-permute-start.41
  177.5 1.9 place_pieces.2
  179.4 2.3 %collective-permute-start.42 = (f32[8,1024]{1,0:T(8,128)S(1)}, f32[8,1024]{1,0:T(8,128)S(1)}, u32[]{:S(2)}, u32[]{:S(2)}) collective-permute-start(f32[8,1024]{1,0:T(8,128)S(1)} %add.127), channel_id=1, source_target_pairs={{0,8},{1,9},{2,10},{3,11},{4,12},{5,13},{6,14},{7,15},{8,0},{9,1},... | collective-permute-start | bytes 98312 | tf_op jit(solution)/shard_map/ppermute | solution.py:627
  181.8 1.0 collective-permute-start.43
  182.8 1.9 collective-permute-done.41.refs_3_
  185.3 1.9 place_pieces.3
  187.7 3.7 %collective-permute-done.43 = f32[1,64,1024]{2,1,0:T(8,128)S(1)} collective-permute-done((f32[1,64,1024]{2,1,0:T(8,128)S(1)}, f32[1,64,1024]{2,1,0:T(8,128)S(1)}, u32[]{:S(2)}, u32[]{:S(2)}) %collective-permute-start.43) | collective-permute-done | bytes 262176 | tf_op jit(solution)/shard_map/ppermute | solution.py:627
  (138 shorter events, 17.4 us)
Async XLA Ops:
  1.7 20.2 %copy-start.6 = (f32[128,1024]{1,0:T(8,128)}, f32[128,1024]{1,0:T(8,128)S(1)}, u32[]{:S(2)}) copy-start(f32[128,1024]{1,0:T(8,128)S(1)} %dynamic-slice_convert_fusion) | copy-start | bytes 1572868
  1.7 20.3 %collective-permute-start = (f32[128,1024]{1,0:T(8,128)S(1)}, f32[128,1024]{1,0:T(8,128)}, u32[]{:S(2)}, u32[]{:S(2)}) collective-permute-start(f32[128,1024]{1,0:T(8,128)S(1)} %dynamic-slice_convert_fusion), channel_id=1, source_target_pairs={{0,2},{1,3},{2,0},{3,1},{4,6},{5,7},{6,4},{7,5},{8,10},{9,11},{10,... | collective-permute-start | bytes 1572872 | tf_op jit(solution)/shard_map/ppermute | solution.py:627
  4.7 17.2 %collective-permute-start.1 = (f32[80,1024]{1,0:T(8,128)S(1)}, f32[80,1024]{1,0:T(8,128)S(1)}, u32[]{:S(2)}, u32[]{:S(2)}) collective-permute-start(f32[80,1024]{1,0:T(8,128)S(1)} %slice.160), channel_id=1, source_target_pairs={{0,16},{1,17},{2,18},{3,19},{4,20},{5,21},{6,22},{7,23},{8,24},{9,... | collective-permute-start | bytes 983048 | tf_op jit(solution)/shard_map/ppermute | solution.py:627
  21.9 18.7 %copy-start.17 = (f32[80,1024]{1,0:T(8,128)}, f32[80,1024]{1,0:T(8,128)S(1)}, u32[]{:S(2)}) copy-start(f32[80,1024]{1,0:T(8,128)S(1)} %collective-permute-done.1.refs_12_) | copy-start | bytes 983044
  23.9 15.1 %collective-permute-start.6 = (f32[1024,768]{1,0:T(8,128)}, f32[1024,768]{1,0:T(8,128)S(1)}, u32[]{:S(2)}, u32[]{:S(2)}) collective-permute-start(f32[1024,768]{1,0:T(8,128)} %maximum_convert_fusion), channel_id=1, source_target_pairs={{0,1},{1,0},{2,3},{3,2},{4,5},{5,4},{6,7},{7,6},{8,9},{9,8},{10,11... | collective-permute-start | bytes 9437192 | tf_op jit(solution)/shard_map/ppermute | solution.py:620
  23.9 7.4 %collective-permute-start.2 = (f32[256,1024]{1,0:T(8,128)S(1)}, f32[256,1024]{1,0:T(8,128)S(1)}, u32[]{:S(2)}, u32[]{:S(2)}) collective-permute-start(f32[256,1024]{1,0:T(8,128)S(1)} %bitcast.59), channel_id=1, source_target_pairs={{0,1},{1,0},{2,3},{3,2},{4,5},{5,4},{6,7},{7,6},{8,9},{9,8},{10,11... | collective-permute-start | bytes 3145736 | tf_op jit(solution)/shard_map/ppermute | solution.py:620
  24.4 14.6 %collective-permute-start.5 = (f32[128,1024]{1,0:T(8,128)}, f32[128,1024]{1,0:T(8,128)}, u32[]{:S(2)}, u32[]{:S(2)}) collective-permute-start(f32[128,1024]{1,0:T(8,128)} %collective-permute-done.refs_10_), channel_id=1, source_target_pairs={{0,1},{1,0},{2,3},{3,2},{4,5},{5,4},{6,7},{7,6},{8,9},{9,8},{10,11... | collective-permute-start | bytes 1572872 | tf_op jit(solution)/shard_map/ppermute | solution.py:620
  24.4 14.6 %collective-permute-start.4 = (f32[80,1024]{1,0:T(8,128)S(1)}, f32[80,1024]{1,0:T(8,128)}, u32[]{:S(2)}, u32[]{:S(2)}) collective-permute-start(f32[80,1024]{1,0:T(8,128)S(1)} %collective-permute-done.1.refs_12_), channel_id=1, source_target_pairs={{0,2},{1,3},{2,0},{3,1},{4,6},{5,7},{6,4},{7,5},{8,10},{9,11},{10,... | collective-permute-start | bytes 983048 | tf_op jit(solution)/shard_map/ppermute | solution.py:627
  26.5 12.5 %collective-permute-start.3 = (f32[48,1024]{1,0:T(8,128)}, f32[48,1024]{1,0:T(8,128)}, u32[]{:S(2)}, u32[]{:S(2)}) collective-permute-start(f32[48,1024]{1,0:T(8,128)} %slice.121), channel_id=1, source_target_pairs={{0,16},{1,17},{2,18},{3,19},{4,20},{5,21},{6,22},{7,23},{8,24},{9,... | collective-permute-start | bytes 589832 | tf_op jit(solution)/shard_map/ppermute | solution.py:627
  39.0 12.6 %collective-permute-start.11 = (f32[48,1024]{1,0:T(8,128)}, f32[48,1024]{1,0:T(8,128)}, u32[]{:S(2)}, u32[]{:S(2)}) collective-permute-start(f32[48,1024]{1,0:T(8,128)} %collective-permute-done.3.refs_13_), channel_id=1, source_target_pairs={{0,1},{1,0},{2,3},{3,2},{4,5},{5,4},{6,7},{7,6},{8,9},{9,8},{10,11... | collective-permute-start | bytes 589832 | tf_op jit(solution)/shard_map/ppermute | solution.py:620
  39.1 12.5 %collective-permute-start.8 = (f32[48,1024]{1,0:T(8,128)}, f32[48,1024]{1,0:T(8,128)}, u32[]{:S(2)}, u32[]{:S(2)}) collective-permute-start(f32[48,1024]{1,0:T(8,128)} %collective-permute-done.3.refs_13_), channel_id=1, source_target_pairs={{0,2},{1,3},{2,0},{3,1},{4,6},{5,7},{6,4},{7,5},{8,10},{9,11},{10,... | collective-permute-start | bytes 589832 | tf_op jit(solution)/shard_map/ppermute | solution.py:627
  40.6 11.0 %collective-permute-start.7 = (f32[48,1024]{1,0:T(8,128)}, f32[48,1024]{1,0:T(8,128)}, u32[]{:S(2)}, u32[]{:S(2)}) collective-permute-start(f32[48,1024]{1,0:T(8,128)} %get-tuple-element.120), channel_id=1, source_target_pairs={{0,16},{1,17},{2,18},{3,19},{4,20},{5,21},{6,22},{7,23},{8,24},{9,... | collective-permute-start | bytes 589832 | tf_op jit(solution)/shard_map/ppermute | solution.py:627
  40.6 11.0 %collective-permute-start.9 = (f32[80,1024]{1,0:T(8,128)S(1)}, f32[80,1024]{1,0:T(8,128)}, u32[]{:S(2)}, u32[]{:S(2)}) collective-permute-start(f32[80,1024]{1,0:T(8,128)S(1)} %collective-permute-done.1.refs_12_), channel_id=1, source_target_pairs={{0,1},{1,0},{2,3},{3,2},{4,5},{5,4},{6,7},{7,6},{8,9},{9,8},{10,11... | collective-permute-start | bytes 983048 | tf_op jit(solution)/shard_map/ppermute | solution.py:620
  40.8 10.8 %collective-permute-start.10 = (f32[80,1024]{1,0:T(8,128)}, f32[80,1024]{1,0:T(8,128)}, u32[]{:S(2)}, u32[]{:S(2)}) collective-permute-start(f32[80,1024]{1,0:T(8,128)} %collective-permute-done.4.refs_16_), channel_id=1, source_target_pairs={{0,1},{1,0},{2,3},{3,2},{4,5},{5,4},{6,7},{7,6},{8,9},{9,8},{10,11... | collective-permute-start | bytes 983048 | tf_op jit(solution)/shard_map/ppermute | solution.py:620
  51.6 3.7 %collective-permute-start.12 = (f32[256,1024]{1,0:T(8,128)}, f32[256,1024]{1,0:T(8,128)S(1)}, u32[]{:S(2)}, u32[]{:S(2)}) collective-permute-start(f32[256,1024]{1,0:T(8,128)} %get-tuple-element.126.own_ref), channel_id=1, source_target_pairs={{0,1},{1,0},{2,3},{3,2},{4,5},{5,4},{6,7},{7,6},{8,9},{9,8},{10,11... | collective-permute-start | bytes 3145736 | tf_op jit(solution)/shard_map/ppermute | solution.py:620
  51.7 18.8 %collective-permute-start.13 = (f32[128,1024]{1,0:T(8,128)}, f32[128,1024]{1,0:T(8,128)S(1)}, u32[]{:S(2)}, u32[]{:S(2)}) collective-permute-start(f32[128,1024]{1,0:T(8,128)} %get-tuple-element.133), channel_id=1, source_target_pairs={{0,2},{1,3},{2,0},{3,1},{4,6},{5,7},{6,4},{7,5},{8,10},{9,11},{10,... | collective-permute-start | bytes 1572872 | tf_op jit(solution)/shard_map/ppermute | solution.py:627
  52.3 18.3 %collective-permute-start.14 = (f32[80,1024]{1,0:T(8,128)}, f32[80,1024]{1,0:T(8,128)S(1)}, u32[]{:S(2)}, u32[]{:S(2)}) collective-permute-start(f32[80,1024]{1,0:T(8,128)} %get-tuple-element.134), channel_id=1, source_target_pairs={{0,16},{1,17},{2,18},{3,19},{4,20},{5,21},{6,22},{7,23},{8,24},{9,... | collective-permute-start | bytes 983048 | tf_op jit(solution)/shard_map/ppermute | solution.py:627
  54.8 12.5 %collective-permute-start.17 = (f32[48,1024]{1,0:T(8,128)}, f32[48,1024]{1,0:T(8,128)S(1)}, u32[]{:S(2)}, u32[]{:S(2)}) collective-permute-start(f32[48,1024]{1,0:T(8,128)} %collective-permute-done.8.refs_17_), channel_id=1, source_target_pairs={{0,1},{1,0},{2,3},{3,2},{4,5},{5,4},{6,7},{7,6},{8,9},{9,8},{10,11... | collective-permute-start | bytes 589832 | tf_op jit(solution)/shard_map/ppermute | solution.py:620
  54.8 12.5 %collective-permute-start.16 = (f32[48,1024]{1,0:T(8,128)}, f32[48,1024]{1,0:T(8,128)S(1)}, u32[]{:S(2)}, u32[]{:S(2)}) collective-permute-start(f32[48,1024]{1,0:T(8,128)} %collective-permute-done.7.refs_2_), channel_id=1, source_target_pairs={{0,1},{1,0},{2,3},{3,2},{4,5},{5,4},{6,7},{7,6},{8,9},{9,8},{10,11... | collective-permute-start | bytes 589832 | tf_op jit(solution)/shard_map/ppermute | solution.py:620
  55.3 15.3 %collective-permute-start.15 = (f32[48,1024]{1,0:T(8,128)}, f32[48,1024]{1,0:T(8,128)}, u32[]{:S(2)}, u32[]{:S(2)}) collective-permute-start(f32[48,1024]{1,0:T(8,128)} %collective-permute-done.7.refs_2_), channel_id=1, source_target_pairs={{0,2},{1,3},{2,0},{3,1},{4,6},{5,7},{6,4},{7,5},{8,10},{9,11},{10,... | collective-permute-start | bytes 589832 | tf_op jit(solution)/shard_map/ppermute | solution.py:627
  67.3 15.7 %copy-start.22 = (f32[48,1024]{1,0:T(8,128)}, f32[48,1024]{1,0:T(8,128)S(1)}, u32[]{:S(2)}) copy-start(f32[48,1024]{1,0:T(8,128)S(1)} %collective-permute-done.17.refs_19_) | copy-start | bytes 589828
  67.3 15.7 %copy-start.23 = (f32[48,1024]{1,0:T(8,128)}, f32[48,1024]{1,0:T(8,128)S(1)}, u32[]{:S(2)}) copy-start(f32[48,1024]{1,0:T(8,128)S(1)} %collective-permute-done.16.refs_4_) | copy-start | bytes 589828
  70.6 12.5 %collective-permute-start.21 = (f32[4,640,512]{2,1,0:T(8,128)}, f32[4,640,512]{2,1,0:T(8,128)}, u32[]{:S(2)}, u32[]{:S(2)}) collective-permute-start(f32[4,640,512]{2,1,0:T(8,128)} %get-tuple-element.148), channel_id=1, source_target_pairs={{0,1},{1,0},{2,3},{3,2},{4,5},{5,4},{6,7},{7,6},{8,9},{9,8},{10,11... | collective-permute-start | bytes 15728648 | tf_op jit(solution)/shard_map/ppermute | solution.py:620
  70.7 12.4 %collective-permute-start.18 = (f32[128,1024]{1,0:T(8,128)S(1)}, f32[128,1024]{1,0:T(8,128)S(1)}, u32[]{:S(2)}, u32[]{:S(2)}) collective-permute-start(f32[128,1024]{1,0:T(8,128)S(1)} %collective-permute-done.13.refs_0_), channel_id=1, source_target_pairs={{0,1},{1,0},{2,3},{3,2},{4,5},{5,4},{6,7},{7,6},{8,9},{9,8},{10,11... | collective-permute-start | bytes 1572872 | tf_op jit(solution)/shard_map/ppermute | solution.py:620
  71.2 11.9 %collective-permute-start.20 = (f32[80,1024]{1,0:T(8,128)S(1)}, f32[80,1024]{1,0:T(8,128)S(1)}, u32[]{:S(2)}, u32[]{:S(2)}) collective-permute-start(f32[80,1024]{1,0:T(8,128)S(1)} %collective-permute-done.14.refs_3_), channel_id=1, source_target_pairs={{0,2},{1,3},{2,0},{3,1},{4,6},{5,7},{6,4},{7,5},{8,10},{9,11},{10,... | collective-permute-start | bytes 983048 | tf_op jit(solution)/shard_map/ppermute | solution.py:627
  72.3 10.8 %collective-permute-start.19 = (f32[80,1024]{1,0:T(8,128)S(1)}, f32[80,1024]{1,0:T(8,128)S(1)}, u32[]{:S(2)}, u32[]{:S(2)}) collective-permute-start(f32[80,1024]{1,0:T(8,128)S(1)} %collective-permute-done.14.refs_3_), channel_id=1, source_target_pairs={{0,1},{1,0},{2,3},{3,2},{4,5},{5,4},{6,7},{7,6},{8,9},{9,8},{10,11... | collective-permute-start | bytes 983048 | tf_op jit(solution)/shard_map/ppermute | solution.py:620
  72.8 10.2 %collective-permute-start.22 = (f32[48,1024]{1,0:T(8,128)}, f32[48,1024]{1,0:T(8,128)}, u32[]{:S(2)}, u32[]{:S(2)}) collective-permute-start(f32[48,1024]{1,0:T(8,128)} %collective-permute-done.15.refs_6_), channel_id=1, source_target_pairs={{0,1},{1,0},{2,3},{3,2},{4,5},{5,4},{6,7},{7,6},{8,9},{9,8},{10,11... | collective-permute-start | bytes 589832 | tf_op jit(solution)/shard_map/ppermute | solution.py:620
  83.1 33.1 %collective-permute-start.26 = (f32[8,64,1024]{2,1,0:T(8,128)}, f32[8,64,1024]{2,1,0:T(8,128)}, u32[]{:S(2)}, u32[]{:S(2)}) collective-permute-start(f32[8,64,1024]{2,1,0:T(8,128)} %get-tuple-element.161), channel_id=1, source_target_pairs={{0,2},{1,5},{2,0},{3,7},{4,6},{5,1},{6,4},{7,3},{8,10},{9,13},{10,... | collective-permute-start | bytes 6291464 | tf_op jit(solution)/shard_map/ppermute | solution.py:627
  84.1 32.1 %collective-permute-start.25 = (f32[256,1024]{1,0:T(8,128)S(1)}, f32[256,1024]{1,0:T(8,128)}, u32[]{:S(2)}, u32[]{:S(2)}) collective-permute-start(f32[256,1024]{1,0:T(8,128)S(1)} %copy-done.8), channel_id=1, source_target_pairs={{0,1},{1,0},{2,3},{3,2},{4,5},{5,4},{6,7},{7,6},{8,9},{9,8},{10,11... | collective-permute-start | bytes 3145736 | tf_op jit(solution)/shard_map/ppermute | solution.py:620
  84.4 2.8 %collective-permute-start.23 = (f32[80,1024]{1,0:T(8,128)S(1)}, f32[80,1024]{1,0:T(8,128)S(1)}, u32[]{:S(2)}, u32[]{:S(2)}) collective-permute-start(f32[80,1024]{1,0:T(8,128)S(1)} %collective-permute-done.20.refs_7_), channel_id=1, source_target_pairs={{0,1},{1,0},{2,3},{3,2},{4,5},{5,4},{6,7},{7,6},{8,9},{9,8},{10,11... | collective-permute-start | bytes 983048 | tf_op jit(solution)/shard_map/ppermute | solution.py:620
  99.3 20.5 %collective-permute-start.27 = (f32[8,64,512]{2,1,0:T(8,128)}, f32[8,64,512]{2,1,0:T(8,128)}, u32[]{:S(2)}, u32[]{:S(2)}) collective-permute-start(f32[8,64,512]{2,1,0:T(8,128)} %get-tuple-element.151), channel_id=1, source_target_pairs={{0,4},{1,9},{2,6},{3,11},{4,0},{5,13},{6,2},{7,15},{8,12},{9,1},{1... | collective-permute-start | bytes 3145736 | tf_op jit(solution)/shard_map/ppermute | solution.py:627
  100.8 1.5 collective-permute-start.24
  121.2 9.3 %collective-permute-start.28 = (f32[4,64,512]{2,1,0:T(8,128)S(1)}, f32[4,64,512]{2,1,0:T(8,128)S(1)}, u32[]{:S(2)}, u32[]{:S(2)}) collective-permute-start(f32[4,64,512]{2,1,0:T(8,128)S(1)} %get-tuple-element.203), channel_id=1, source_target_pairs={{0,8},{1,5},{2,10},{3,7},{4,12},{5,1},{6,14},{7,3},{8,0},{9,13},{1... | collective-permute-start | bytes 1572872 | tf_op jit(solution)/shard_map/ppermute | solution.py:627
  130.6 20.4 %collective-permute-start.32 = (f32[8,64,512]{2,1,0:T(8,128)}, f32[8,64,512]{2,1,0:T(8,128)}, u32[]{:S(2)}, u32[]{:S(2)}) collective-permute-start(f32[8,64,512]{2,1,0:T(8,128)} %get-tuple-element.178), channel_id=1, source_target_pairs={{0,4},{1,9},{2,6},{3,11},{4,0},{5,13},{6,2},{7,15},{8,12},{9,1},{1... | collective-permute-start | bytes 3145736 | tf_op jit(solution)/shard_map/ppermute | solution.py:627
  132.1 26.9 %collective-permute-start.33 = (f32[4,64,1024]{2,1,0:T(8,128)}, f32[4,64,1024]{2,1,0:T(8,128)S(1)}, u32[]{:S(2)}, u32[]{:S(2)}) collective-permute-start(f32[4,64,1024]{2,1,0:T(8,128)} %get-tuple-element.198), channel_id=1, source_target_pairs={{0,4},{1,3},{2,6},{3,1},{4,0},{5,7},{6,2},{7,5},{8,12},{9,11},{10,... | collective-permute-start | bytes 3145736 | tf_op jit(solution)/shard_map/ppermute | solution.py:627
  133.4 17.5 %collective-permute-start.31 = (f32[64,512]{1,0:T(8,128)}, f32[64,512]{1,0:T(8,128)S(1)}, u32[]{:S(2)}, u32[]{:S(2)}) collective-permute-start(f32[64,512]{1,0:T(8,128)} %get-tuple-element.211), channel_id=1, source_target_pairs={{0,18},{1,19},{2,16},{3,17},{4,22},{5,23},{6,20},{7,21},{8,26},{9,... | collective-permute-start | bytes 393224 | tf_op jit(solution)/shard_map/ppermute | solution.py:627
  136.2 14.7 %collective-permute-start.30 = (f32[64,512]{1,0:T(8,128)}, f32[64,512]{1,0:T(8,128)S(1)}, u32[]{:S(2)}, u32[]{:S(2)}) collective-permute-start(f32[64,512]{1,0:T(8,128)} %get-tuple-element.212), channel_id=1, source_target_pairs={{0,16},{1,17},{2,18},{3,19},{4,20},{5,21},{6,22},{7,23},{8,24},{9,... | collective-permute-start | bytes 393224 | tf_op jit(solution)/shard_map/ppermute | solution.py:627
  137.2 13.7 %collective-permute-start.29 = (f32[64,512]{1,0:T(8,128)}, f32[64,512]{1,0:T(8,128)S(1)}, u32[]{:S(2)}, u32[]{:S(2)}) collective-permute-start(f32[64,512]{1,0:T(8,128)} %get-tuple-element.213), channel_id=1, source_target_pairs={{0,2},{1,3},{2,0},{3,1},{4,6},{5,7},{6,4},{7,5},{8,10},{9,11},{10,... | collective-permute-start | bytes 393224 | tf_op jit(solution)/shard_map/ppermute | solution.py:627
  152.6 13.6 %collective-permute-start.35 = (f32[4,64,512]{2,1,0:T(8,128)S(1)}, f32[4,64,512]{2,1,0:T(8,128)S(1)}, u32[]{:S(2)}, u32[]{:S(2)}) collective-permute-start(f32[4,64,512]{2,1,0:T(8,128)S(1)} %get-tuple-element.200), channel_id=1, source_target_pairs={{0,8},{1,5},{2,10},{3,7},{4,12},{5,1},{6,14},{7,3},{8,0},{9,13},{1... | collective-permute-start | bytes 1572872 | tf_op jit(solution)/shard_map/ppermute | solution.py:627
  153.8 11.3 %collective-permute-start.34 = (f32[8,1024]{1,0:T(8,128)S(1)}, f32[8,1024]{1,0:T(8,128)S(1)}, u32[]{:S(2)}, u32[]{:S(2)}) collective-permute-start(f32[8,1024]{1,0:T(8,128)S(1)} %copy-done.30), channel_id=1, source_target_pairs={{0,16},{1,17},{2,18},{3,19},{4,20},{5,21},{6,22},{7,23},{8,24},{9,... | collective-permute-start | bytes 98312 | tf_op jit(solution)/shard_map/ppermute | solution.py:627
  160.0 21.7 %collective-permute-start.40 = (f32[2,64,1024]{2,1,0:T(8,128)}, f32[2,64,1024]{2,1,0:T(8,128)S(1)}, u32[]{:S(2)}, u32[]{:S(2)}) collective-permute-start(f32[2,64,1024]{2,1,0:T(8,128)} %get-tuple-element.202), channel_id=1, source_target_pairs={{0,8},{1,17},{2,10},{3,19},{4,12},{5,21},{6,14},{7,23},{8,0},{9,25... | collective-permute-start | bytes 1572872 | tf_op jit(solution)/shard_map/ppermute | solution.py:627
  166.9 5.0 %collective-permute-start.36 = (f32[64,512]{1,0:T(8,128)S(1)}, f32[64,512]{1,0:T(8,128)S(1)}, u32[]{:S(2)}, u32[]{:S(2)}) collective-permute-start(f32[64,512]{1,0:T(8,128)S(1)} %get-tuple-element.210), channel_id=1, source_target_pairs={{0,2},{1,3},{2,0},{3,1},{4,6},{5,7},{6,4},{7,5},{8,10},{9,11},{10,... | collective-permute-start | bytes 393224 | tf_op jit(solution)/shard_map/ppermute | solution.py:627
  167.7 14.0 %collective-permute-start.39 = (f32[64,512]{1,0:T(8,128)S(1)}, f32[64,512]{1,0:T(8,128)S(1)}, u32[]{:S(2)}, u32[]{:S(2)}) collective-permute-start(f32[64,512]{1,0:T(8,128)S(1)} %get-tuple-element.209), channel_id=1, source_target_pairs={{0,16},{1,17},{2,18},{3,19},{4,20},{5,21},{6,22},{7,23},{8,24},{9,... | collective-permute-start | bytes 393224 | tf_op jit(solution)/shard_map/ppermute | solution.py:627
  170.9 3.9 %collective-permute-start.37 = (f32[8,1024]{1,0:T(8,128)S(1)}, f32[8,1024]{1,0:T(8,128)S(1)}, u32[]{:S(2)}, u32[]{:S(2)}) collective-permute-start(f32[8,1024]{1,0:T(8,128)S(1)} %add.123), channel_id=1, source_target_pairs={{0,2},{1,3},{2,0},{3,1},{4,6},{5,7},{6,4},{7,5},{8,10},{9,11},{10,... | collective-permute-start | bytes 98312 | tf_op jit(solution)/shard_map/ppermute | solution.py:627
  174.8 4.6 %collective-permute-start.38 = (f32[8,1024]{1,0:T(8,128)S(1)}, f32[8,1024]{1,0:T(8,128)S(1)}, u32[]{:S(2)}, u32[]{:S(2)}) collective-permute-start(f32[8,1024]{1,0:T(8,128)S(1)} %add.126), channel_id=1, source_target_pairs={{0,4},{1,5},{2,6},{3,7},{4,0},{5,1},{6,2},{7,3},{8,12},{9,13},{10,... | collective-permute-start | bytes 98312 | tf_op jit(solution)/shard_map/ppermute | solution.py:627
  176.4 8.2 %collective-permute-start.41 = (f32[64,512]{1,0:T(8,128)S(1)}, f32[64,512]{1,0:T(8,128)S(1)}, u32[]{:S(2)}, u32[]{:S(2)}) collective-permute-start(f32[64,512]{1,0:T(8,128)S(1)} %get-tuple-element.207), channel_id=1, source_target_pairs={{0,18},{1,19},{2,16},{3,17},{4,22},{5,23},{6,20},{7,21},{8,26},{9,... | collective-permute-start | bytes 393224 | tf_op jit(solution)/shard_map/ppermute | solution.py:627
  179.4 5.2 %collective-permute-start.42 = (f32[8,1024]{1,0:T(8,128)S(1)}, f32[8,1024]{1,0:T(8,128)S(1)}, u32[]{:S(2)}, u32[]{:S(2)}) collective-permute-start(f32[8,1024]{1,0:T(8,128)S(1)} %add.127), channel_id=1, source_target_pairs={{0,8},{1,9},{2,10},{3,11},{4,12},{5,13},{6,14},{7,15},{8,0},{9,1},... | collective-permute-start | bytes 98312 | tf_op jit(solution)/shard_map/ppermute | solution.py:627
  181.8 9.7 %collective-permute-start.43 = (f32[1,64,1024]{2,1,0:T(8,128)S(1)}, f32[1,64,1024]{2,1,0:T(8,128)S(1)}, u32[]{:S(2)}, u32[]{:S(2)}) collective-permute-start(f32[1,64,1024]{2,1,0:T(8,128)S(1)} %get-tuple-element.205), channel_id=1, source_target_pairs={{0,16},{1,9},{2,18},{3,11},{4,20},{5,13},{6,22},{7,15},{8,24},{9,1... | collective-permute-start | bytes 786440 | tf_op jit(solution)/shard_map/ppermute | solution.py:627
  (28 other events, 219.5 us)

commit v6 on v5

--- a/solution.py
+++ b/solution.py
@@ -849,13 +849,13 @@
     mixed = up.advance(done)
     up_pieces = pieces(mixed)
     done = vec.advance(mixed, up_pieces[1])
+    while small.left > 1:
+        done = small.advance(done)
     down_pieces[0] = after(down_pieces[0], done)
     done = grad_down = place_pieces(member, down_pieces)
     while vec.order:
         done = vec.advance(done)
-    while small.left > 1:
-        done = small.advance(done, up_pieces[2])
-    vec = vec.advance(done, up_pieces[3])
+    vec = vec.advance(done, up_pieces[2], up_pieces[3])
     vec = lax.dynamic_slice_in_dim(vec, links.row * share, share, 1)
     up_pieces[0] = after(up_pieces[0], vec)
     grad_up = place_pieces(member, up_pieces)

time: 193 us -> 196 us (1.016)
  waiting for transfers between devices: 30.3 us -> 34 us
    ppermute x28, waiting for transfers between devices: 22 us -> 25.7 us  [send(): return lax.ppermute(array, ('dp', 'tensor'), pairs)]
  transfers between devices with their start and end apart: 44 -> 44, of which waited for: 14 -> 16; matrix products, arithmetic and copies ran while one was open for 7% -> 6% of each run, Pallas kernels for 51% -> 50%
where the time goes in v6:
time: 196 us; the launch traced here: 195 us
  Pallas kernels  98.2 us (50%)
  starting transfers between devices  41.1 us (21%)
  waiting for transfers between devices  34 us (17%)
  other arithmetic  12.7 us (6%)
  local copies, waits for them, and re-layouts  7.72 us (4%)
    pallas_call x11, Pallas kernels, call(): pl.pallas_call(body, out_shape=shapes, grid_spec=pltpu.PrefetchScalarGrid...  98.2 us
    ppermute x28, starting transfers between devices, send(): return lax.ppermute(array, ('dp', 'tensor'), pairs)  37.8 us
    ppermute x28, waiting for transfers between devices, send(): return lax.ppermute(array, ('dp', 'tensor'), pairs)  25.7 us
    ppermute x16, waiting for transfers between devices, swap(): return lax.ppermute(array, 'tensor', [(0, 1), (1, 0)])  8.31 us
    add x3, other arithmetic, advance(): keep[half:] + self.come[half:]  4.72 us
  transfers between devices with their start and end apart: 44, of which 16 were waited for; matrix products, arithmetic and copies ran while one was open for 6% of the time, Pallas kernels for 50%

profile of v6, /device:TPU:0, one launch (start us, length us, event | category | flops | bytes accessed | tf_op | source)
XLA Modules:
  0.0 194.9 jit_solution(1608706208892636205)
XLA Ops:
  0.6 1.0 dynamic-slice_convert_fusion
  1.7 3.0 %collective-permute-start = (f32[128,1024]{1,0:T(8,128)S(1)}, f32[128,1024]{1,0:T(8,128)S(1)}, u32[]{:S(2)}, u32[]{:S(2)}) collective-permute-start(f32[128,1024]{1,0:T(8,128)S(1)} %dynamic-slice_convert_fusion), channel_id=1, source_target_pairs={{0,2},{1,3},{2,0},{3,1},{4,6},{5,7},{6,4},{7,5},{8,10},{9,11},{10,... | collective-permute-start | bytes 1572872 | tf_op jit(solution)/shard_map/ppermute | solution.py:627
  4.7 2.7 %collective-permute-start.1 = (f32[80,1024]{1,0:T(8,128)S(1)}, f32[80,1024]{1,0:T(8,128)S(1)}, u32[]{:S(2)}, u32[]{:S(2)}) collective-permute-start(f32[80,1024]{1,0:T(8,128)S(1)} %slice.160), channel_id=1, source_target_pairs={{0,16},{1,17},{2,18},{3,19},{4,20},{5,21},{6,22},{7,23},{8,24},{9,... | collective-permute-start | bytes 983048 | tf_op jit(solution)/shard_map/ppermute | solution.py:627
  7.4 14.5 %attend.1 = (bf16[4,640,1024]{2,1,0:T(8,128)(2,1)}, bf16[4,64,256]{2,1,0:T(8,128)(2,1)}, bf16[4,640,256]{2,1,0:T(8,128)(2,1)}, bf16[4,640,256]{2,1,0:T(8,128)(2,...) custom-call(s32[4]{0:T(128)} %buckets_ref.1, ...), custom_call_target="tpu_custom_call" | custom-call | flops 3355443200 | bytes 19171328 | tf_op jit(solution)/shard_map/attend/pallas_call | solution.py:73
  22.7 1.9 maximum_convert_fusion
  25.7 1.6 slice.121
  27.4 4.6 %collective-permute-done.2.far_ref = f32[256,1024]{1,0:T(8,128)S(1)} collective-permute-done((f32[256,1024]{1,0:T(8,128)S(1)}, f32[256,1024]{1,0:T(8,128)S(1)}, u32[]{:S(2)}, u32[]{:S(2)}) %collective-permute-start.2) | collective-permute-done | bytes 1048608 | tf_op jit(solution)/shard_map/ppermute | solution.py:620
  32.0 1.0 copy-done.14
  33.0 3.9 %middle.1 = (f32[256,1024]{1,0:T(8,128)}, bf16[256,1024]{1,0:T(8,128)(2,1)}, f32[128,1024]{1,0:T(8,128)}, f32[48,1024]{1,0:T(8,128)}, f32[80,1024]{1,0:T(8,128)}) custom-call(s32[1]{0:T(128)} %bitcast.core_ref, bf16[256,1024]{1,0:T(8,128)(2,1)} %bitcast.51, f32[256,1024]{1,0:T(8,128)} %bitcast.58, f32[256,1024]{1,0:T(8,128)} %copy-done.14, ...), custom_call_target="tpu_custom_call" | custom-call | bytes 5251072 | tf_op jit(solution)/shard_map/middle/pallas_call | solution.py:73
  36.9 2.9 %collective-permute-done.3.refs_13_ = f32[48,1024]{1,0:T(8,128)} collective-permute-done((f32[48,1024]{1,0:T(8,128)}, f32[48,1024]{1,0:T(8,128)}, u32[]{:S(2)}, u32[]{:S(2)}) %collective-permute-start.3) | collective-permute-done | bytes 196640 | tf_op jit(solution)/shard_map/ppermute | solution.py:627
  39.9 1.6 collective-permute-start.8
  41.9 10.0 %feed.1 = (bf16[256,2048]{1,0:T(8,128)(2,1)}, bf16[256,2048]{1,0:T(8,128)(2,1)}, f32[256,1024]{1,0:T(8,128)}, f32[256,1024]{1,0:T(8,128)}) custom-call(bf16[256,1024]{1,0:T(8,128)(2,1)} %get-tuple-element.118.low_ref.refs_21_, bf16[256,1024]{1,0:T(8,128)(2,1)} %bitcast.55, bf16[1024,2048]{1,0:T(8,128)(2,1)} %refs_20_.1, bf16[2048,1024]{1,0:T(8,128)(2,1)} %down_ref.3), custom_call_target="tpu_custom_call" | custom-call | flops 4294967296 | bytes 13631488 | tf_op jit(solution)/shard_map/feed/pallas_call | solution.py:73
  53.0 2.5 %collective-permute-start.14 = (f32[80,1024]{1,0:T(8,128)}, f32[80,1024]{1,0:T(8,128)S(1)}, u32[]{:S(2)}, u32[]{:S(2)}) collective-permute-start(f32[80,1024]{1,0:T(8,128)} %get-tuple-element.134), channel_id=1, source_target_pairs={{0,16},{1,17},{2,18},{3,19},{4,20},{5,21},{6,22},{7,23},{8,24},{9,... | collective-permute-start | bytes 983048 | tf_op jit(solution)/shard_map/ppermute | solution.py:627
  56.1 1.5 collective-permute-start.15
  57.6 10.5 %back.1 = (f32[256,1024]{1,0:T(8,128)}, bf16[256,1024]{1,0:T(8,128)(2,1)}, bf16[4,640,512]{2,1,0:T(8,128)(2,1)}, f32[4,640,512]{2,1,0:T(8,128)}, bf16[4,64,256]{...) custom-call(f32[256,1024]{1,0:T(8,128)} %get-tuple-element.181.mid_ref, ...), custom_call_target="tpu_custom_call" | custom-call | flops 1677721600 | bytes 19468288 | tf_op jit(solution)/shard_map/back/pallas_call | solution.py:73
  68.2 3.2 %collective-permute-done.15.refs_6_ = f32[48,1024]{1,0:T(8,128)} collective-permute-done((f32[48,1024]{1,0:T(8,128)}, f32[48,1024]{1,0:T(8,128)}, u32[]{:S(2)}, u32[]{:S(2)}) %collective-permute-start.15) | collective-permute-done | bytes 196640 | tf_op jit(solution)/shard_map/ppermute | solution.py:627
  72.0 1.1 collective-permute-start.20
  74.1 9.7 %small_grad.1 = (f32[8,64,1024]{2,1,0:T(8,128)}, f32[8,64,1024]{2,1,0:T(8,128)}) custom-call(s32[16]{0:T(128)} %broadcast_select_fusion.1.place_ref, bf16[2560,1024]{1,0:T(8,128)(2,1)} %bitcast.74, bf16[256,1024]{1,0:T(8,128)(2,1)} %get-tuple-element.137.gb_ref, bf16[2560,512]{1,0:T(8,128)(2,1)} %bitcast.50, bf16[256,256]{1,0:T(8,128)(2,1)} %bitcast.60, ...), custom_call_target="tpu_custom_call" | custom-call | flops 2684354560 | bytes 12845056 | tf_op jit(solution)/shard_map/small_grad/pallas_call | solution.py:73
  83.9 0.9 collective-permute-start.26
  85.9 2.1 %collective-permute-done.23.refs_9_ = f32[80,1024]{1,0:T(8,128)S(1)} collective-permute-done((f32[80,1024]{1,0:T(8,128)S(1)}, f32[80,1024]{1,0:T(8,128)S(1)}, u32[]{:S(2)}, u32[]{:S(2)}) %collective-permute-start.23) | collective-permute-done | bytes 327712 | tf_op jit(solution)/shard_map/ppermute | solution.py:620
  88.7 11.3 %down_side.1 = (f32[8,64,512]{2,1,0:T(8,128)}, f32[8,64,512]{2,1,0:T(8,128)}, bf16[1024,1024]{1,0:T(8,128)(2,1)}, bf16[1024,1024]{1,0:T(8,128)(2,1)}, f32[768,512]{1,0:T(8,128)}) custom-call(s32[1]{0:T(128)} %bitcast.14.member_ref, s32[16]{0:T(128)} %broadcast_select_fusion.place_ref, f32[128,1024]{1,0:T(8,128)} %copy-done.16, f32[128,1024]{1,0:T(8,128)} %copy-done.17, ...), custom_call_target="tpu_custom_call" | custom-call | bytes 20447232 | tf_op jit(solution)/shard_map/down_side/pallas_call | solution.py:73
  100.0 1.6 collective-permute-start.27
  101.6 1.5 collective-permute-done.24.gq_far_ref.refs_3_
  103.8 13.1 %inputs_back.2 = (bf16[4,576,1024]{2,1,0:T(8,128)(2,1)}, bf16[4,64,1024]{2,1,0:T(8,128)(2,1)}, f32[8,1024]{1,0:T(8,128)}) custom-call(bf16[4,640,512]{2,1,0:T(8,128)(2,1)} %get-tuple-element.171.gkv_ref.refs_0_, f32[4,640,512]{2,1,0:T(8,128)} %collective-permute-done.21.gkv_far_ref.refs_1_, bf16[4,64,256]{2,1,0:T(8,128)(2,1)} %get-tuple-element.139.gq_ref.refs_2_, ...), custom_call_target="tpu_custom_call" | custom-call | flops 2415919104 | bytes 24635392 | tf_op jit(solution)/shard_map/inputs_back/pallas_call | solution.py:73
  117.0 3.0 %slice_add_fusion.1 = (f32[4,64,1024]{2,1,0:T(8,128)S(1)}, f32[4,64,1024]{2,1,0:T(8,128)}) fusion(f32[8,64,1024]{2,1,0:T(8,128)} %collective-permute-done.26, f32[8,64,1024]{2,1,0:T(8,128)S(1)} %copy-done.5), kind=kLoop, calls=%fused_computation.2 | loop fusion | flops 524288 | bytes 6291456 | tf_op jit(solution)/shard_map/add | solution.py:660
  120.6 1.4 slice_add_fusion.6
  122.0 0.8 collective-permute-start.28
  122.8 8.4 %up_side.1 = (f32[8,64,512]{2,1,0:T(8,128)}, f32[8,64,512]{2,1,0:T(8,128)}) custom-call(s32[1]{0:T(128)} %bitcast.14.member_ref, s32[16]{0:T(128)} %broadcast_select_fusion.place_ref, bf16[1024,1024]{1,0:T(8,128)(2,1)} %get-tuple-element.164.fl_ref, bf16[1024,1024]{1,0:T(8,128)(2,1)} %get-tuple-element.165.cl_ref, f32[768,512]{1,0:T(8,128)} %get-tuple-element.166.slope_ref, ...), custom_call_target="tpu_custom_call" | custom-call | bytes 13107200 | tf_op jit(solution)/shard_map/up_side/pallas_call | solution.py:73
  131.3 1.6 collective-permute-start.32
  134.2 2.8 %collective-permute-start.31 = (f32[64,512]{1,0:T(8,128)}, f32[64,512]{1,0:T(8,128)S(1)}, u32[]{:S(2)}, u32[]{:S(2)}) collective-permute-start(f32[64,512]{1,0:T(8,128)} %get-tuple-element.211), channel_id=1, source_target_pairs={{0,18},{1,19},{2,16},{3,17},{4,22},{5,23},{6,20},{7,21},{8,26},{9,... | collective-permute-start | bytes 393224 | tf_op jit(solution)/shard_map/ppermute | solution.py:627
  137.1 1.0 collective-permute-start.30
  138.6 13.1 %inputs_back.3 = (bf16[4,576,1024]{2,1,0:T(8,128)(2,1)}, bf16[4,64,1024]{2,1,0:T(8,128)(2,1)}, f32[8,1024]{1,0:T(8,128)}) custom-call(bf16[4,640,512]{2,1,0:T(8,128)(2,1)} %get-tuple-element.171.gkv_ref.refs_0_, f32[4,640,512]{2,1,0:T(8,128)} %collective-permute-done.21.gkv_far_ref.refs_1_, ...), custom_call_target="tpu_custom_call", output_to_operand_aliasing={{0}: (16, {}), {1}: (17, {})} | custom-call | flops 2415919104 | bytes 29845504 | tf_op jit(solution)/shard_map/inputs_back/pallas_call | solution.py:73
  151.8 1.6 slice_add_fusion.2
  153.4 1.3 collective-permute-start.35
  154.7 1.9 collective-permute-start.34
  156.6 3.2 %collective-permute-done.33 = f32[4,64,1024]{2,1,0:T(8,128)S(1)} collective-permute-done((f32[4,64,1024]{2,1,0:T(8,128)}, f32[4,64,1024]{2,1,0:T(8,128)S(1)}, u32[]{:S(2)}, u32[]{:S(2)}) %collective-permute-start.33) | collective-permute-done | bytes 1048608 | tf_op jit(solution)/shard_map/ppermute | solution.py:627
  160.0 1.3 collective-permute-start.38
  161.3 2.3 %add_convert_fusion = bf16[256,1024]{1,0:T(8,128)(2,1)} fusion(f32[256,1024]{1,0:T(8,128)S(1)} %copy-done.4, f32[256,1024]{1,0:T(8,128)S(1)} %copy-done.9, f32[256,1024]{1,0:T(8,128)} %collective-permute-done.25), kind=kLoop, calls=%fused_computation.3 | loop fusion | flops 786432 | bytes 3670016 | tf_op jit(solution)/shard_map/convert_element_type | solution.py:847
  163.6 3.4 %collective-permute-done.34 = f32[8,1024]{1,0:T(8,128)S(1)} collective-permute-done((f32[8,1024]{1,0:T(8,128)S(1)}, f32[8,1024]{1,0:T(8,128)S(1)}, u32[]{:S(2)}, u32[]{:S(2)}) %collective-permute-start.34) | collective-permute-done | bytes 32800 | tf_op jit(solution)/shard_map/ppermute | solution.py:627
  168.5 0.8 collective-permute-start.36
  169.4 1.2 collective-permute-start.37
  170.6 3.5 %collective-permute-start.41 = (f32[64,512]{1,0:T(8,128)S(1)}, f32[64,512]{1,0:T(8,128)S(1)}, u32[]{:S(2)}, u32[]{:S(2)}) collective-permute-start(f32[64,512]{1,0:T(8,128)S(1)} %get-tuple-element.207), channel_id=1, source_target_pairs={{0,18},{1,19},{2,16},{3,17},{4,22},{5,23},{6,20},{7,21},{8,26},{9,... | collective-permute-start | bytes 393224 | tf_op jit(solution)/shard_map/ppermute | solution.py:627
  175.1 1.1 collective-permute-start.39
  176.1 5.5 %collective-permute-done.38 = f32[2,64,1024]{2,1,0:T(8,128)S(1)} collective-permute-done((f32[2,64,1024]{2,1,0:T(8,128)S(1)}, f32[2,64,1024]{2,1,0:T(8,128)S(1)}, u32[]{:S(2)}, u32[]{:S(2)}) %collective-permute-start.38) | collective-permute-done | bytes 524320 | tf_op jit(solution)/shard_map/ppermute | solution.py:627
  181.7 1.9 place_pieces.2
  183.8 3.3 %collective-permute-start.43 = (f32[1,64,1024]{2,1,0:T(8,128)S(1)}, f32[1,64,1024]{2,1,0:T(8,128)S(1)}, u32[]{:S(2)}, u32[]{:S(2)}) collective-permute-start(f32[1,64,1024]{2,1,0:T(8,128)S(1)} %get-tuple-element.205), channel_id=1, source_target_pairs={{0,16},{1,9},{2,18},{3,11},{4,20},{5,13},{6,22},{7,15},{8,24},{9,1... | collective-permute-start | bytes 786440 | tf_op jit(solution)/shard_map/ppermute | solution.py:627
  187.8 1.9 place_pieces.3
  190.2 4.0 %collective-permute-done.43 = f32[1,64,1024]{2,1,0:T(8,128)S(1)} collective-permute-done((f32[1,64,1024]{2,1,0:T(8,128)S(1)}, f32[1,64,1024]{2,1,0:T(8,128)S(1)}, u32[]{:S(2)}, u32[]{:S(2)}) %collective-permute-start.43) | collective-permute-done | bytes 262176 | tf_op jit(solution)/shard_map/ppermute | solution.py:627
  (140 shorter events, 15.7 us)
Async XLA Ops:
  1.7 20.2 %copy-start.6 = (f32[128,1024]{1,0:T(8,128)}, f32[128,1024]{1,0:T(8,128)S(1)}, u32[]{:S(2)}) copy-start(f32[128,1024]{1,0:T(8,128)S(1)} %dynamic-slice_convert_fusion) | copy-start | bytes 1572868
  1.7 20.3 %collective-permute-start = (f32[128,1024]{1,0:T(8,128)S(1)}, f32[128,1024]{1,0:T(8,128)S(1)}, u32[]{:S(2)}, u32[]{:S(2)}) collective-permute-start(f32[128,1024]{1,0:T(8,128)S(1)} %dynamic-slice_convert_fusion), channel_id=1, source_target_pairs={{0,2},{1,3},{2,0},{3,1},{4,6},{5,7},{6,4},{7,5},{8,10},{9,11},{10,... | collective-permute-start | bytes 1572872 | tf_op jit(solution)/shard_map/ppermute | solution.py:627
  4.7 17.2 %collective-permute-start.1 = (f32[80,1024]{1,0:T(8,128)S(1)}, f32[80,1024]{1,0:T(8,128)S(1)}, u32[]{:S(2)}, u32[]{:S(2)}) collective-permute-start(f32[80,1024]{1,0:T(8,128)S(1)} %slice.160), channel_id=1, source_target_pairs={{0,16},{1,17},{2,18},{3,19},{4,20},{5,21},{6,22},{7,23},{8,24},{9,... | collective-permute-start | bytes 983048 | tf_op jit(solution)/shard_map/ppermute | solution.py:627
  21.9 30.0 %copy-start.18 = (f32[80,1024]{1,0:T(8,128)}, f32[80,1024]{1,0:T(8,128)S(1)}, u32[]{:S(2)}) copy-start(f32[80,1024]{1,0:T(8,128)S(1)} %collective-permute-done.1.refs_12_) | copy-start | bytes 983044
  24.6 15.1 %collective-permute-start.6 = (f32[1024,768]{1,0:T(8,128)}, f32[1024,768]{1,0:T(8,128)S(1)}, u32[]{:S(2)}, u32[]{:S(2)}) collective-permute-start(f32[1024,768]{1,0:T(8,128)} %maximum_convert_fusion), channel_id=1, source_target_pairs={{0,1},{1,0},{2,3},{3,2},{4,5},{5,4},{6,7},{7,6},{8,9},{9,8},{10,11... | collective-permute-start | bytes 9437192 | tf_op jit(solution)/shard_map/ppermute | solution.py:620
  24.6 7.4 %collective-permute-start.2 = (f32[256,1024]{1,0:T(8,128)S(1)}, f32[256,1024]{1,0:T(8,128)S(1)}, u32[]{:S(2)}, u32[]{:S(2)}) collective-permute-start(f32[256,1024]{1,0:T(8,128)S(1)} %bitcast.59), channel_id=1, source_target_pairs={{0,1},{1,0},{2,3},{3,2},{4,5},{5,4},{6,7},{7,6},{8,9},{9,8},{10,11... | collective-permute-start | bytes 3145736 | tf_op jit(solution)/shard_map/ppermute | solution.py:620
  25.2 14.6 %collective-permute-start.5 = (f32[128,1024]{1,0:T(8,128)}, f32[128,1024]{1,0:T(8,128)}, u32[]{:S(2)}, u32[]{:S(2)}) collective-permute-start(f32[128,1024]{1,0:T(8,128)} %copy-done.15), channel_id=1, source_target_pairs={{0,1},{1,0},{2,3},{3,2},{4,5},{5,4},{6,7},{7,6},{8,9},{9,8},{10,11... | collective-permute-start | bytes 1572872 | tf_op jit(solution)/shard_map/ppermute | solution.py:620
  25.2 14.6 %collective-permute-start.4 = (f32[80,1024]{1,0:T(8,128)S(1)}, f32[80,1024]{1,0:T(8,128)}, u32[]{:S(2)}, u32[]{:S(2)}) collective-permute-start(f32[80,1024]{1,0:T(8,128)S(1)} %collective-permute-done.1.refs_12_), channel_id=1, source_target_pairs={{0,2},{1,3},{2,0},{3,1},{4,6},{5,7},{6,4},{7,5},{8,10},{9,11},{10,... | collective-permute-start | bytes 983048 | tf_op jit(solution)/shard_map/ppermute | solution.py:627
  27.3 12.5 %collective-permute-start.3 = (f32[48,1024]{1,0:T(8,128)}, f32[48,1024]{1,0:T(8,128)}, u32[]{:S(2)}, u32[]{:S(2)}) collective-permute-start(f32[48,1024]{1,0:T(8,128)} %slice.121), channel_id=1, source_target_pairs={{0,16},{1,17},{2,18},{3,19},{4,20},{5,21},{6,22},{7,23},{8,24},{9,... | collective-permute-start | bytes 589832 | tf_op jit(solution)/shard_map/ppermute | solution.py:627
  39.8 12.6 %collective-permute-start.11 = (f32[48,1024]{1,0:T(8,128)}, f32[48,1024]{1,0:T(8,128)}, u32[]{:S(2)}, u32[]{:S(2)}) collective-permute-start(f32[48,1024]{1,0:T(8,128)} %collective-permute-done.3.refs_13_), channel_id=1, source_target_pairs={{0,1},{1,0},{2,3},{3,2},{4,5},{5,4},{6,7},{7,6},{8,9},{9,8},{10,11... | collective-permute-start | bytes 589832 | tf_op jit(solution)/shard_map/ppermute | solution.py:620
  39.9 12.5 %collective-permute-start.8 = (f32[48,1024]{1,0:T(8,128)}, f32[48,1024]{1,0:T(8,128)}, u32[]{:S(2)}, u32[]{:S(2)}) collective-permute-start(f32[48,1024]{1,0:T(8,128)} %collective-permute-done.3.refs_13_), channel_id=1, source_target_pairs={{0,2},{1,3},{2,0},{3,1},{4,6},{5,7},{6,4},{7,5},{8,10},{9,11},{10,... | collective-permute-start | bytes 589832 | tf_op jit(solution)/shard_map/ppermute | solution.py:627
  41.4 11.0 %collective-permute-start.7 = (f32[48,1024]{1,0:T(8,128)}, f32[48,1024]{1,0:T(8,128)}, u32[]{:S(2)}, u32[]{:S(2)}) collective-permute-start(f32[48,1024]{1,0:T(8,128)} %get-tuple-element.120), channel_id=1, source_target_pairs={{0,16},{1,17},{2,18},{3,19},{4,20},{5,21},{6,22},{7,23},{8,24},{9,... | collective-permute-start | bytes 589832 | tf_op jit(solution)/shard_map/ppermute | solution.py:627
  41.4 11.0 %collective-permute-start.9 = (f32[80,1024]{1,0:T(8,128)S(1)}, f32[80,1024]{1,0:T(8,128)}, u32[]{:S(2)}, u32[]{:S(2)}) collective-permute-start(f32[80,1024]{1,0:T(8,128)S(1)} %collective-permute-done.1.refs_12_), channel_id=1, source_target_pairs={{0,1},{1,0},{2,3},{3,2},{4,5},{5,4},{6,7},{7,6},{8,9},{9,8},{10,11... | collective-permute-start | bytes 983048 | tf_op jit(solution)/shard_map/ppermute | solution.py:620
  41.6 10.8 %collective-permute-start.10 = (f32[80,1024]{1,0:T(8,128)}, f32[80,1024]{1,0:T(8,128)}, u32[]{:S(2)}, u32[]{:S(2)}) collective-permute-start(f32[80,1024]{1,0:T(8,128)} %collective-permute-done.4.refs_16_), channel_id=1, source_target_pairs={{0,1},{1,0},{2,3},{3,2},{4,5},{5,4},{6,7},{7,6},{8,9},{9,8},{10,11... | collective-permute-start | bytes 983048 | tf_op jit(solution)/shard_map/ppermute | solution.py:620
  52.4 3.7 %collective-permute-start.12 = (f32[256,1024]{1,0:T(8,128)}, f32[256,1024]{1,0:T(8,128)S(1)}, u32[]{:S(2)}, u32[]{:S(2)}) collective-permute-start(f32[256,1024]{1,0:T(8,128)} %get-tuple-element.126.own_ref), channel_id=1, source_target_pairs={{0,1},{1,0},{2,3},{3,2},{4,5},{5,4},{6,7},{7,6},{8,9},{9,8},{10,11... | collective-permute-start | bytes 3145736 | tf_op jit(solution)/shard_map/ppermute | solution.py:620
  52.5 18.8 %collective-permute-start.13 = (f32[128,1024]{1,0:T(8,128)}, f32[128,1024]{1,0:T(8,128)S(1)}, u32[]{:S(2)}, u32[]{:S(2)}) collective-permute-start(f32[128,1024]{1,0:T(8,128)} %get-tuple-element.133), channel_id=1, source_target_pairs={{0,2},{1,3},{2,0},{3,1},{4,6},{5,7},{6,4},{7,5},{8,10},{9,11},{10,... | collective-permute-start | bytes 1572872 | tf_op jit(solution)/shard_map/ppermute | solution.py:627
  53.0 18.3 %collective-permute-start.14 = (f32[80,1024]{1,0:T(8,128)}, f32[80,1024]{1,0:T(8,128)S(1)}, u32[]{:S(2)}, u32[]{:S(2)}) collective-permute-start(f32[80,1024]{1,0:T(8,128)} %get-tuple-element.134), channel_id=1, source_target_pairs={{0,16},{1,17},{2,18},{3,19},{4,20},{5,21},{6,22},{7,23},{8,24},{9,... | collective-permute-start | bytes 983048 | tf_op jit(solution)/shard_map/ppermute | solution.py:627
  55.6 12.5 %collective-permute-start.17 = (f32[48,1024]{1,0:T(8,128)}, f32[48,1024]{1,0:T(8,128)S(1)}, u32[]{:S(2)}, u32[]{:S(2)}) collective-permute-start(f32[48,1024]{1,0:T(8,128)} %collective-permute-done.8.refs_17_), channel_id=1, source_target_pairs={{0,1},{1,0},{2,3},{3,2},{4,5},{5,4},{6,7},{7,6},{8,9},{9,8},{10,11... | collective-permute-start | bytes 589832 | tf_op jit(solution)/shard_map/ppermute | solution.py:620
  55.6 12.5 %collective-permute-start.16 = (f32[48,1024]{1,0:T(8,128)}, f32[48,1024]{1,0:T(8,128)S(1)}, u32[]{:S(2)}, u32[]{:S(2)}) collective-permute-start(f32[48,1024]{1,0:T(8,128)} %collective-permute-done.7.refs_2_), channel_id=1, source_target_pairs={{0,1},{1,0},{2,3},{3,2},{4,5},{5,4},{6,7},{7,6},{8,9},{9,8},{10,11... | collective-permute-start | bytes 589832 | tf_op jit(solution)/shard_map/ppermute | solution.py:620
  56.1 15.3 %collective-permute-start.15 = (f32[48,1024]{1,0:T(8,128)}, f32[48,1024]{1,0:T(8,128)}, u32[]{:S(2)}, u32[]{:S(2)}) collective-permute-start(f32[48,1024]{1,0:T(8,128)} %collective-permute-done.7.refs_2_), channel_id=1, source_target_pairs={{0,2},{1,3},{2,0},{3,1},{4,6},{5,7},{6,4},{7,5},{8,10},{9,11},{10,... | collective-permute-start | bytes 589832 | tf_op jit(solution)/shard_map/ppermute | solution.py:627
  68.1 15.7 %copy-start.23 = (f32[48,1024]{1,0:T(8,128)}, f32[48,1024]{1,0:T(8,128)S(1)}, u32[]{:S(2)}) copy-start(f32[48,1024]{1,0:T(8,128)S(1)} %collective-permute-done.17.refs_19_) | copy-start | bytes 589828
  68.1 15.7 %copy-start.24 = (f32[48,1024]{1,0:T(8,128)}, f32[48,1024]{1,0:T(8,128)S(1)}, u32[]{:S(2)}) copy-start(f32[48,1024]{1,0:T(8,128)S(1)} %collective-permute-done.16.refs_4_) | copy-start | bytes 589828
  71.4 12.5 %collective-permute-start.21 = (f32[4,640,512]{2,1,0:T(8,128)}, f32[4,640,512]{2,1,0:T(8,128)}, u32[]{:S(2)}, u32[]{:S(2)}) collective-permute-start(f32[4,640,512]{2,1,0:T(8,128)} %get-tuple-element.148), channel_id=1, source_target_pairs={{0,1},{1,0},{2,3},{3,2},{4,5},{5,4},{6,7},{7,6},{8,9},{9,8},{10,11... | collective-permute-start | bytes 15728648 | tf_op jit(solution)/shard_map/ppermute | solution.py:620
  71.5 12.4 %collective-permute-start.18 = (f32[128,1024]{1,0:T(8,128)S(1)}, f32[128,1024]{1,0:T(8,128)S(1)}, u32[]{:S(2)}, u32[]{:S(2)}) collective-permute-start(f32[128,1024]{1,0:T(8,128)S(1)} %collective-permute-done.13.refs_0_), channel_id=1, source_target_pairs={{0,1},{1,0},{2,3},{3,2},{4,5},{5,4},{6,7},{7,6},{8,9},{9,8},{10,11... | collective-permute-start | bytes 1572872 | tf_op jit(solution)/shard_map/ppermute | solution.py:620
  72.0 11.9 %collective-permute-start.20 = (f32[80,1024]{1,0:T(8,128)S(1)}, f32[80,1024]{1,0:T(8,128)S(1)}, u32[]{:S(2)}, u32[]{:S(2)}) collective-permute-start(f32[80,1024]{1,0:T(8,128)S(1)} %collective-permute-done.14.refs_3_), channel_id=1, source_target_pairs={{0,2},{1,3},{2,0},{3,1},{4,6},{5,7},{6,4},{7,5},{8,10},{9,11},{10,... | collective-permute-start | bytes 983048 | tf_op jit(solution)/shard_map/ppermute | solution.py:627
  73.1 10.8 %collective-permute-start.19 = (f32[80,1024]{1,0:T(8,128)S(1)}, f32[80,1024]{1,0:T(8,128)S(1)}, u32[]{:S(2)}, u32[]{:S(2)}) collective-permute-start(f32[80,1024]{1,0:T(8,128)S(1)} %collective-permute-done.14.refs_3_), channel_id=1, source_target_pairs={{0,1},{1,0},{2,3},{3,2},{4,5},{5,4},{6,7},{7,6},{8,9},{9,8},{10,11... | collective-permute-start | bytes 983048 | tf_op jit(solution)/shard_map/ppermute | solution.py:620
  73.6 10.2 %collective-permute-start.22 = (f32[48,1024]{1,0:T(8,128)}, f32[48,1024]{1,0:T(8,128)}, u32[]{:S(2)}, u32[]{:S(2)}) collective-permute-start(f32[48,1024]{1,0:T(8,128)} %collective-permute-done.15.refs_6_), channel_id=1, source_target_pairs={{0,1},{1,0},{2,3},{3,2},{4,5},{5,4},{6,7},{7,6},{8,9},{9,8},{10,11... | collective-permute-start | bytes 589832 | tf_op jit(solution)/shard_map/ppermute | solution.py:620
  83.9 33.0 %collective-permute-start.26 = (f32[8,64,1024]{2,1,0:T(8,128)}, f32[8,64,1024]{2,1,0:T(8,128)}, u32[]{:S(2)}, u32[]{:S(2)}) collective-permute-start(f32[8,64,1024]{2,1,0:T(8,128)} %get-tuple-element.161), channel_id=1, source_target_pairs={{0,2},{1,5},{2,0},{3,7},{4,6},{5,1},{6,4},{7,3},{8,10},{9,13},{10,... | collective-permute-start | bytes 6291464 | tf_op jit(solution)/shard_map/ppermute | solution.py:627
  84.9 32.1 %collective-permute-start.25 = (f32[256,1024]{1,0:T(8,128)S(1)}, f32[256,1024]{1,0:T(8,128)}, u32[]{:S(2)}, u32[]{:S(2)}) collective-permute-start(f32[256,1024]{1,0:T(8,128)S(1)} %copy-done.8), channel_id=1, source_target_pairs={{0,1},{1,0},{2,3},{3,2},{4,5},{5,4},{6,7},{7,6},{8,9},{9,8},{10,11... | collective-permute-start | bytes 3145736 | tf_op jit(solution)/shard_map/ppermute | solution.py:620
  85.2 2.8 %collective-permute-start.23 = (f32[80,1024]{1,0:T(8,128)S(1)}, f32[80,1024]{1,0:T(8,128)S(1)}, u32[]{:S(2)}, u32[]{:S(2)}) collective-permute-start(f32[80,1024]{1,0:T(8,128)S(1)} %collective-permute-done.20.refs_7_), channel_id=1, source_target_pairs={{0,1},{1,0},{2,3},{3,2},{4,5},{5,4},{6,7},{7,6},{8,9},{9,8},{10,11... | collective-permute-start | bytes 983048 | tf_op jit(solution)/shard_map/ppermute | solution.py:620
  100.0 20.6 %collective-permute-start.27 = (f32[8,64,512]{2,1,0:T(8,128)}, f32[8,64,512]{2,1,0:T(8,128)}, u32[]{:S(2)}, u32[]{:S(2)}) collective-permute-start(f32[8,64,512]{2,1,0:T(8,128)} %get-tuple-element.151), channel_id=1, source_target_pairs={{0,4},{1,9},{2,6},{3,11},{4,0},{5,13},{6,2},{7,15},{8,12},{9,1},{1... | collective-permute-start | bytes 3145736 | tf_op jit(solution)/shard_map/ppermute | solution.py:627
  101.6 1.5 collective-permute-start.24
  122.0 9.2 %collective-permute-start.28 = (f32[4,64,512]{2,1,0:T(8,128)S(1)}, f32[4,64,512]{2,1,0:T(8,128)S(1)}, u32[]{:S(2)}, u32[]{:S(2)}) collective-permute-start(f32[4,64,512]{2,1,0:T(8,128)S(1)} %get-tuple-element.203), channel_id=1, source_target_pairs={{0,8},{1,5},{2,10},{3,7},{4,12},{5,1},{6,14},{7,3},{8,0},{9,13},{1... | collective-permute-start | bytes 1572872 | tf_op jit(solution)/shard_map/ppermute | solution.py:627
  131.3 20.4 %collective-permute-start.32 = (f32[8,64,512]{2,1,0:T(8,128)}, f32[8,64,512]{2,1,0:T(8,128)}, u32[]{:S(2)}, u32[]{:S(2)}) collective-permute-start(f32[8,64,512]{2,1,0:T(8,128)} %get-tuple-element.178), channel_id=1, source_target_pairs={{0,4},{1,9},{2,6},{3,11},{4,0},{5,13},{6,2},{7,15},{8,12},{9,1},{1... | collective-permute-start | bytes 3145736 | tf_op jit(solution)/shard_map/ppermute | solution.py:627
  132.9 26.9 %collective-permute-start.33 = (f32[4,64,1024]{2,1,0:T(8,128)}, f32[4,64,1024]{2,1,0:T(8,128)S(1)}, u32[]{:S(2)}, u32[]{:S(2)}) collective-permute-start(f32[4,64,1024]{2,1,0:T(8,128)} %get-tuple-element.198), channel_id=1, source_target_pairs={{0,4},{1,3},{2,6},{3,1},{4,0},{5,7},{6,2},{7,5},{8,12},{9,11},{10,... | collective-permute-start | bytes 3145736 | tf_op jit(solution)/shard_map/ppermute | solution.py:627
  134.2 17.5 %collective-permute-start.31 = (f32[64,512]{1,0:T(8,128)}, f32[64,512]{1,0:T(8,128)S(1)}, u32[]{:S(2)}, u32[]{:S(2)}) collective-permute-start(f32[64,512]{1,0:T(8,128)} %get-tuple-element.211), channel_id=1, source_target_pairs={{0,18},{1,19},{2,16},{3,17},{4,22},{5,23},{6,20},{7,21},{8,26},{9,... | collective-permute-start | bytes 393224 | tf_op jit(solution)/shard_map/ppermute | solution.py:627
  137.1 14.7 %collective-permute-start.30 = (f32[64,512]{1,0:T(8,128)}, f32[64,512]{1,0:T(8,128)S(1)}, u32[]{:S(2)}, u32[]{:S(2)}) collective-permute-start(f32[64,512]{1,0:T(8,128)} %get-tuple-element.212), channel_id=1, source_target_pairs={{0,16},{1,17},{2,18},{3,19},{4,20},{5,21},{6,22},{7,23},{8,24},{9,... | collective-permute-start | bytes 393224 | tf_op jit(solution)/shard_map/ppermute | solution.py:627
  138.0 13.7 %collective-permute-start.29 = (f32[64,512]{1,0:T(8,128)}, f32[64,512]{1,0:T(8,128)S(1)}, u32[]{:S(2)}, u32[]{:S(2)}) collective-permute-start(f32[64,512]{1,0:T(8,128)} %get-tuple-element.213), channel_id=1, source_target_pairs={{0,2},{1,3},{2,0},{3,1},{4,6},{5,7},{6,4},{7,5},{8,10},{9,11},{10,... | collective-permute-start | bytes 393224 | tf_op jit(solution)/shard_map/ppermute | solution.py:627
  153.4 14.4 %collective-permute-start.35 = (f32[4,64,512]{2,1,0:T(8,128)S(1)}, f32[4,64,512]{2,1,0:T(8,128)S(1)}, u32[]{:S(2)}, u32[]{:S(2)}) collective-permute-start(f32[4,64,512]{2,1,0:T(8,128)S(1)} %get-tuple-element.200), channel_id=1, source_target_pairs={{0,8},{1,5},{2,10},{3,7},{4,12},{5,1},{6,14},{7,3},{8,0},{9,13},{1... | collective-permute-start | bytes 1572872 | tf_op jit(solution)/shard_map/ppermute | solution.py:627
  154.7 12.4 %collective-permute-start.34 = (f32[8,1024]{1,0:T(8,128)S(1)}, f32[8,1024]{1,0:T(8,128)S(1)}, u32[]{:S(2)}, u32[]{:S(2)}) collective-permute-start(f32[8,1024]{1,0:T(8,128)S(1)} %copy-done.31), channel_id=1, source_target_pairs={{0,16},{1,17},{2,18},{3,19},{4,20},{5,21},{6,22},{7,23},{8,24},{9,... | collective-permute-start | bytes 98312 | tf_op jit(solution)/shard_map/ppermute | solution.py:627
  160.0 21.7 %collective-permute-start.38 = (f32[2,64,1024]{2,1,0:T(8,128)S(1)}, f32[2,64,1024]{2,1,0:T(8,128)S(1)}, u32[]{:S(2)}, u32[]{:S(2)}) collective-permute-start(f32[2,64,1024]{2,1,0:T(8,128)S(1)} %get-tuple-element.202), channel_id=1, source_target_pairs={{0,8},{1,17},{2,10},{3,19},{4,12},{5,21},{6,14},{7,23},{8,0},{9,25... | collective-permute-start | bytes 1572872 | tf_op jit(solution)/shard_map/ppermute | solution.py:627
  168.5 6.2 %collective-permute-start.36 = (f32[64,512]{1,0:T(8,128)S(1)}, f32[64,512]{1,0:T(8,128)S(1)}, u32[]{:S(2)}, u32[]{:S(2)}) collective-permute-start(f32[64,512]{1,0:T(8,128)S(1)} %get-tuple-element.210), channel_id=1, source_target_pairs={{0,2},{1,3},{2,0},{3,1},{4,6},{5,7},{6,4},{7,5},{8,10},{9,11},{10,... | collective-permute-start | bytes 393224 | tf_op jit(solution)/shard_map/ppermute | solution.py:627
  169.4 5.7 %collective-permute-start.37 = (f32[8,1024]{1,0:T(8,128)S(1)}, f32[8,1024]{1,0:T(8,128)S(1)}, u32[]{:S(2)}, u32[]{:S(2)}) collective-permute-start(f32[8,1024]{1,0:T(8,128)S(1)} %add.123), channel_id=1, source_target_pairs={{0,2},{1,3},{2,0},{3,1},{4,6},{5,7},{6,4},{7,5},{8,10},{9,11},{10,... | collective-permute-start | bytes 98312 | tf_op jit(solution)/shard_map/ppermute | solution.py:627
  170.6 16.5 %collective-permute-start.41 = (f32[64,512]{1,0:T(8,128)S(1)}, f32[64,512]{1,0:T(8,128)S(1)}, u32[]{:S(2)}, u32[]{:S(2)}) collective-permute-start(f32[64,512]{1,0:T(8,128)S(1)} %get-tuple-element.207), channel_id=1, source_target_pairs={{0,18},{1,19},{2,16},{3,17},{4,22},{5,23},{6,20},{7,21},{8,26},{9,... | collective-permute-start | bytes 393224 | tf_op jit(solution)/shard_map/ppermute | solution.py:627
  174.1 12.9 %collective-permute-start.40 = (f32[64,512]{1,0:T(8,128)S(1)}, f32[64,512]{1,0:T(8,128)S(1)}, u32[]{:S(2)}, u32[]{:S(2)}) collective-permute-start(f32[64,512]{1,0:T(8,128)S(1)} %get-tuple-element.208), channel_id=1, source_target_pairs={{0,16},{1,17},{2,18},{3,19},{4,20},{5,21},{6,22},{7,23},{8,24},{9,... | collective-permute-start | bytes 393224 | tf_op jit(solution)/shard_map/ppermute | solution.py:627
  175.1 8.6 %collective-permute-start.39 = (f32[8,1024]{1,0:T(8,128)S(1)}, f32[8,1024]{1,0:T(8,128)S(1)}, u32[]{:S(2)}, u32[]{:S(2)}) collective-permute-start(f32[8,1024]{1,0:T(8,128)S(1)} %add.126), channel_id=1, source_target_pairs={{0,4},{1,5},{2,6},{3,7},{4,0},{5,1},{6,2},{7,3},{8,12},{9,13},{10,... | collective-permute-start | bytes 98312 | tf_op jit(solution)/shard_map/ppermute | solution.py:627
  183.7 4.0 %collective-permute-start.42 = (f32[8,1024]{1,0:T(8,128)S(1)}, f32[8,1024]{1,0:T(8,128)S(1)}, u32[]{:S(2)}, u32[]{:S(2)}) collective-permute-start(f32[8,1024]{1,0:T(8,128)S(1)} %add.129), channel_id=1, source_target_pairs={{0,8},{1,9},{2,10},{3,11},{4,12},{5,13},{6,14},{7,15},{8,0},{9,1},... | collective-permute-start | bytes 98312 | tf_op jit(solution)/shard_map/ppermute | solution.py:627
  183.8 10.4 %collective-permute-start.43 = (f32[1,64,1024]{2,1,0:T(8,128)S(1)}, f32[1,64,1024]{2,1,0:T(8,128)S(1)}, u32[]{:S(2)}, u32[]{:S(2)}) collective-permute-start(f32[1,64,1024]{2,1,0:T(8,128)S(1)} %get-tuple-element.205), channel_id=1, source_target_pairs={{0,16},{1,9},{2,18},{3,11},{4,20},{5,13},{6,22},{7,15},{8,24},{9,1... | collective-permute-start | bytes 786440 | tf_op jit(solution)/shard_map/ppermute | solution.py:627
  (29 other events, 217.9 us)
